TPU v7x, 32 devices: a whole 2x2x4 slice. The times are simulated.
32 devices in a mesh: groups: 2 (over y), section: 8 (over z, x), sub: 2 (over core).
Axes of the slice: x: 2, y: 2, z: 4, core: 2. Of those that a mesh axis runs over, the one named last changes fastest.
Arguments:
- echoes: float32 [4, 384, 32, 256], P('groups', None, 'section', 'sub'), parts along dimension 0, may hold values from -6 to 6
- range_taps: float32 [2, 5], replicated, may hold values from -3 to 3
- pulse_taper: float32 [256], replicated, may hold values from 0.3 to 1
- channel_phase: float32 [256], replicated, may hold values from -3.140625 to 3.140625
- loading: float32 [1], replicated, may hold values from 0.5 to 2
- beam_index: int32 [256], replicated, may hold values from 0 to 1023
Outputs:
- normalized_beams: float32 [2, 256, 32, 256], P('groups', ('section', 'sub')), parts along dimension 0
There are 2 independent parts, one for each index of `groups`. A program takes and returns all parts, laid end to end along the dimension named above; an argument that names none is the same for every part. Nothing has to cross between parts.
All inputs are finite; a program needn't handle non-finite values. Where the computation divides by a largest or mean magnitude, that divisor is 1e-20 or more.
Results may differ from a plain program's by a relative error of at most 0.0003.
Values sent between devices are 32-bit elements; how exact they have to be, the bound alone decides.
No kernel may reach another device: no remote copies, remote signals or barrier semaphores. Data moves between devices by JAX's collectives and lax.ppermute only.
A program may use at most 64 MiB of HBM per device.

v0:
```python
import math

import jax
import jax.numpy as jnp
import numpy as np
from jax import lax
from jax.experimental import pallas as pl
from jax.experimental.pallas import tpu as pltpu
from jax.sharding import PartitionSpec as P


PULSES = 256
INTERVALS = 2
ITERS = 2
LOOKS = 1024
HOP = 128


precise = lax.Precision.HIGHEST
epsilon = 1e-06
F32 = jnp.float32
BF16 = jnp.bfloat16
LANES = 128
VMEM = pl.BlockSpec(memory_space=pltpu.VMEM)
SMEM = pl.BlockSpec(memory_space=pltpu.SMEM)
LIMIT = 16 << 20


def split(value):
    high = value.astype(BF16)
    return high, (value - high.astype(F32)).astype(BF16)


def dot(left, right):
    return jnp.dot(left, right, preferred_element_type=F32)


def dot_nt(left, right):
    return lax.dot_general(left, right, (((1,), (1,)), ((), ())), preferred_element_type=F32)


def dot_tn(left, right):
    return lax.dot_general(left, right, (((0,), (0,)), ((), ())), preferred_element_type=F32)


def triple(product, left, right):
    return product(left[0], right[0]) + (product(left[0], right[1]) + product(left[1], right[0]))


def doppler_tables(pulses):
    half = pulses // 2
    bins = np.arange(half)[:, None]
    tables = []
    for parity in (0, 1):
        phase = 2.0 * np.pi * ((bins * np.arange(parity, pulses, 2)[None, :]) % pulses) / pulses
        cosine, sine = np.cos(phase), np.sin(phase)
        table = np.concatenate(
            [np.concatenate([cosine, sine], 1), np.concatenate([-sine, cosine], 1)], 0
        ).astype(np.float32)
        high = table.astype(jnp.bfloat16)
        tables += [high, (table - high.astype(np.float32)).astype(jnp.bfloat16)]
    return np.stack(tables)


def doppler_body(gates, hop, interval, view_ref, taper_ref, table_ref, result, tapers):
    half = hop
    for segment in (0, 1):
        row = taper_ref[segment : segment + 1, :]
        tapers[segment * hop : (segment + 1) * hop, :] = jnp.broadcast_to(row, (hop, hop)).T
    for gate in range(gates):
        for parity in (0, 1):
            rows = []
            for part in (0, 1):
                for segment in (0, 1):
                    at = pl.ds(parity * gates + gate, hop // 2, stride=2 * gates)
                    block = view_ref[part, interval + segment, at, :]
                    taper = tapers[pl.ds(segment * hop + parity, hop // 2, stride=2), :]
                    rows.append(block * taper)
            data = split(jnp.concatenate(rows, axis=0))
            table = (table_ref[2 * parity], table_ref[2 * parity + 1])
            value = triple(dot, table, data)
            if parity == 0:
                even = value
            else:
                for part in (0, 1):
                    own = slice(part * half, (part + 1) * half)
                    result[part, gate, :half] = even[own] + value[own]
                    result[part, gate, half:] = even[own] - value[own]


def doppler(view, taper, sections, interval, split_sub):
    gates = view.shape[2] // HOP
    per = PULSES // sections
    own = per // 2

    def body(view_ref, taper_ref, table_ref, *rest):
        out_refs, result, tapers = rest[:-2], rest[-2], rest[-1]
        doppler_body(gates, HOP, interval, view_ref, taper_ref, table_ref, result, tapers)
        section = lax.axis_index("section")
        if not split_sub:
            for step in range(sections):
                start = pl.multiple_of(jnp.bitwise_xor(section, step) * per, per)
                out_refs[step][...] = result[:, :, pl.ds(start, per), :]
        else:
            sub = lax.axis_index("sub")
            for step in range(sections):
                start = jnp.bitwise_xor(section, step) * per
                mine = pl.multiple_of(start + sub * own, own)
                theirs = pl.multiple_of(start + (1 - sub) * own, own)
                out_refs[0][step] = result[:, :, pl.ds(mine, own), :]
                out_refs[1][step] = result[:, :, pl.ds(theirs, own), :]

    tables = jnp.asarray(doppler_tables(PULSES))
    if split_sub:
        shape = (sections, 2, gates, own, LANES)
        outs = [jax.ShapeDtypeStruct(shape, F32)] * 2
    else:
        shape = (2, gates, per, LANES)
        outs = [jax.ShapeDtypeStruct(shape, F32)] * sections
    return pl.pallas_call(
        body,
        in_specs=[VMEM] * 3,
        out_specs=[VMEM] * len(outs),
        out_shape=outs,
        scratch_shapes=[
            pltpu.VMEM((2, gates, PULSES, LANES), F32),
            pltpu.VMEM((PULSES, LANES), F32),
        ],
        compiler_params=pltpu.CompilerParams(vmem_limit_bytes=LIMIT),
    )(view, taper, tables)


def gather_sub(blocks):
    sections = len(blocks)
    _, gates, per, _ = blocks[0].shape
    own = per // 2

    def body(*refs):
        section, sub = lax.axis_index("section"), lax.axis_index("sub")
        mine = pl.multiple_of(sub * own, own)
        theirs = pl.multiple_of((1 - sub) * own, own)
        for step in range(sections):
            source = jnp.bitwise_xor(section, step)
            refs[sections][source] = refs[step][:, :, pl.ds(mine, own), :]
            refs[sections + 1][source] = refs[step][:, :, pl.ds(theirs, own), :]

    shape = jax.ShapeDtypeStruct((sections, 2, gates, own, LANES), F32)
    return pl.pallas_call(
        body,
        in_specs=[VMEM] * sections,
        out_specs=[VMEM] * 2,
        out_shape=[shape] * 2,
        compiler_params=pltpu.CompilerParams(vmem_limit_bytes=LIMIT),
        name="gather_sub",
    )(*blocks)


def pair_up(mine, other):
    sections = mine.shape[0]

    def body(mine_ref, other_ref, *out_refs):
        for step in range(sections):
            out_refs[step][0] = mine_ref[step]
            out_refs[step][1] = other_ref[step]

    shape = jax.ShapeDtypeStruct((2,) + mine.shape[1:], F32)
    return pl.pallas_call(
        body,
        in_specs=[VMEM] * 2,
        out_specs=[VMEM] * sections,
        out_shape=[shape] * sections,
        compiler_params=pltpu.CompilerParams(vmem_limit_bytes=LIMIT),
        name="pair_up",
    )(mine, other)


def filter_matrix(taps_ref, gates, sections, conjugate):
    count = gates * sections
    side = 2 * count
    taps = taps_ref.shape[1]
    row = lax.broadcasted_iota(jnp.int32, (side, side), 0)
    column = lax.broadcasted_iota(jnp.int32, (side, side), 1)
    row_imag, column_imag = row >= count, column >= count
    row_gate = jnp.where(row_imag, row - count, row)
    place = jnp.where(column_imag, column - count, column)
    inner = sum(jnp.where(place >= gate * sections, 1, 0) for gate in range(1, gates))
    column_gate = (place - inner * sections) * gates + inner
    tap = column_gate - row_gate + taps // 2
    real = sum(jnp.where(tap == j, taps_ref[0, j], 0.0) for j in range(taps))
    imag = sum(jnp.where(tap == j, taps_ref[1, j], 0.0) for j in range(taps))
    straight, crossed = row_imag == column_imag, jnp.where(row_imag, imag, -imag)
    matrix = jnp.where(straight, real, crossed)
    if conjugate:
        matrix = jnp.where(row_imag, -matrix, matrix)
    return split(matrix)


def stacked(product, left, right):
    rows = left[0].shape[0]
    both = product(jnp.concatenate(left, axis=0), right[0])
    return both[:rows] + (both[rows:] + product(left[0], right[1]))


def beside(value, negate_first):
    count = value.shape[0] // 2
    real, imag = value[:count], value[count:]
    if negate_first:
        return jnp.concatenate(
            [jnp.concatenate([real, -imag], axis=1), jnp.concatenate([imag, real], axis=1)], axis=0
        )
    return jnp.concatenate(
        [jnp.concatenate([real, imag], axis=1), jnp.concatenate([-imag, real], axis=1)], axis=0
    )


def weights_kernel(mine, other, steer, range_taps, loading):
    sections, _, gates, own, _ = mine.shape
    count = sections * gates
    side = 2 * count
    channels = 2 * LANES
    beams = steer.shape[1] // 2
    stride = 2 * gates * own
    mine = mine.reshape(sections * stride, LANES)
    other = other.reshape(sections * stride, LANES)

    def body(mine_ref, other_ref, steer_ref, taps_ref, load_ref,
             bh_ref, bl_ref, th_ref, tl_ref, gain_ref,
             ah_ref, al_ref, rows_ref, sums_ref, squares_ref, u_ref):
        matrix = filter_matrix(taps_ref, gates, sections, True)
        for index in range(own):
            def load(ref):
                return jnp.concatenate(
                    [ref[pl.ds((part * gates + gate) * own + index, sections, stride=stride), :]
                     for part in (0, 1) for gate in range(gates)], axis=0)

            data = jnp.concatenate([load(mine_ref), load(other_ref)], axis=1)
            value = stacked(dot, matrix, split(data))
            squares_ref[index : index + 1, :] = jnp.sum(value * value, axis=0, keepdims=True)
            high, low = split(value)
            ah_ref[index] = high
            al_ref[index] = low
            bh_ref[index] = beside(high, False)
            bl_ref[index] = beside(low, False)
            here = slice(index * count, (index + 1) * count)
            for place, part in enumerate((high, low, high)):
                lanes = slice(place * 2 * channels, (place + 1) * 2 * channels)
                rows_ref[here, lanes] = jnp.concatenate([part[:count], part[count:]], axis=1)
        for index in range(own):
            high, low = ah_ref[index], al_ref[index]
            turn = lambda v: jnp.concatenate(
                [v, jnp.concatenate([v[count:], -v[:count]], axis=0)], axis=1
            )
            rh, rl = turn(high), turn(low)
            left = jnp.concatenate([high, high, low], axis=0)
            right = jnp.concatenate([rh, rl, rh], axis=0)
            cov = jnp.abs(dot_tn(left, right))
            sums_ref[index : index + 1, :] = jnp.sum(
                cov[:, :channels] + cov[:, channels:], axis=0, keepdims=True
            )
        bound = jnp.max(sums_ref[...], axis=1, keepdims=True) / count
        trace = jnp.sum(squares_ref[...], axis=1, keepdims=True) / count
        delta = load_ref[0] * trace / channels
        bound = bound + delta
        ratio = 1.0 - delta / bound
        first = 1.0 + ratio * (1.0 + ratio * (1.0 + ratio))
        second = 1.0 + ratio * (2.0 + 3.0 * ratio)
        third = 1.0 + 3.0 * ratio
        norm = 1.0 / (count * bound)
        u_ref[...] = dot(rows_ref[...], steer_ref[...])
        low_at = 2 * 2 * channels
        table = steer_ref[:channels, :].astype(F32) + steer_ref[low_at : low_at + channels, :].astype(F32)
        power = jnp.sum(table * table, axis=0, keepdims=True)
        power = power[:, :beams] + power[:, beams:]
        eye = (
            lax.broadcasted_iota(jnp.int32, (side, side), 0)
            == lax.broadcasted_iota(jnp.int32, (side, side), 1)
        )
        for index in range(own):
            at = slice(index, index + 1)
            halves = beside(ah_ref[index], True), beside(al_ref[index], True)
            gram = stacked(dot_nt, halves, halves) * norm[at]
            parts = split(gram)
            square = stacked(dot, parts, parts)
            quad = (jnp.where(eye, second[at], 0.0) - third[at] * gram + square) * (norm[at] / first[at])
            u = u_ref[index * count : (index + 1) * count, :]
            up = jnp.concatenate([u[:, :beams], u[:, beams:]], axis=0)
            value = stacked(dot, split(quad), split(up))
            high, low = split(value)
            th_ref[index] = beside(high, False)
            tl_ref[index] = beside(low, False)
            gain = power - jnp.sum(up * value, axis=0, keepdims=True)
            gain_ref[at, :] = 1.0 / (gain * gain)

    wide = jax.ShapeDtypeStruct((own, side, 2 * channels), BF16)
    turned = jax.ShapeDtypeStruct((own, side, 2 * beams), BF16)
    return pl.pallas_call(
        body,
        in_specs=[VMEM] * 3 + [SMEM] * 2,
        out_specs=[VMEM] * 5,
        out_shape=[wide, wide, turned, turned, jax.ShapeDtypeStruct((own, beams), F32)],
        scratch_shapes=[
            pltpu.VMEM((own, side, channels), BF16),
            pltpu.VMEM((own, side, channels), BF16),
            pltpu.VMEM((own * count, 6 * channels), BF16),
            pltpu.VMEM((own, channels), F32),
            pltpu.VMEM((own, channels), F32),
            pltpu.VMEM((own * count, 2 * beams), F32),
        ],
        compiler_params=pltpu.CompilerParams(vmem_limit_bytes=LIMIT),
        name="weights",
    )(mine, other, steer, range_taps, loading)


def beams_kernel(blocks, weights, steer, range_taps):
    sections = len(blocks)
    _, _, gates, own, _ = blocks[0].shape
    size = 4 * gates * own
    count = sections * gates
    side = 2 * count
    channels = 2 * LANES
    beams = steer.shape[1] // 2
    blocks = [block.reshape(size, LANES) for block in blocks]

    def body(*refs):
        block_refs = refs[:sections]
        (bh_ref, bl_ref, th_ref, tl_ref, gain_ref, steer_ref, taps_ref,
         power_ref, total_ref, held, rows_ref, v_ref, cross_ref) = refs[sections:]
        section = lax.axis_index("section")
        for step in range(sections):
            start = pl.multiple_of(jnp.bitwise_xor(section, step) * size, size)
            held[pl.ds(start, size), :] = block_refs[step][...]
        matrix = filter_matrix(taps_ref, gates, sections, False)
        wide = 2 * channels
        for index in range(own):
            def load(half, part):
                return jnp.concatenate(
                    [held[pl.ds(((half * 2 + part) * gates + gate) * own + index, sections, stride=size), :]
                     for gate in range(gates)], axis=0)

            data = jnp.concatenate([load(half, part) for part in (0, 1) for half in (0, 1)], axis=1)
            high, low = split(data)
            here = slice(index * count, (index + 1) * count)
            for place, part in enumerate((high, low, high)):
                rows_ref[here, place * wide : (place + 1) * wide] = part
        for index in range(own):
            here = slice(index * count, (index + 1) * count)
            parts = rows_ref[here, :wide], rows_ref[here, wide : 2 * wide]
            cross_ref[index] = stacked(dot_nt, parts, (bh_ref[index], bl_ref[index]))
        v_ref[...] = dot(rows_ref[...], steer_ref[...])
        for index in range(own):
            here = slice(index * count, (index + 1) * count)
            low_rank = stacked(dot, split(cross_ref[index]), (th_ref[index], tl_ref[index]))
            v_ref[here, :] = v_ref[here, :] - low_rank
        total = jnp.zeros((1, beams), F32)
        for index in range(own):
            v = v_ref[index * count : (index + 1) * count, :]
            up = jnp.concatenate([v[:, :beams], v[:, beams:]], axis=0)
            out = stacked(dot, matrix, split(up))
            power = (out[:count] * out[:count] + out[count:] * out[count:]) * gain_ref[index : index + 1, :]
            total = total + jnp.sum(power, axis=0, keepdims=True)
            power_ref[index] = power
        total_ref[...] = jnp.broadcast_to(total, total_ref.shape)

    return pl.pallas_call(
        body,
        in_specs=[VMEM] * (sections + 6) + [SMEM],
        out_specs=[VMEM] * 2,
        out_shape=[
            jax.ShapeDtypeStruct((own, count, beams), F32),
            jax.ShapeDtypeStruct((2 * sections, beams), F32),
        ],
        scratch_shapes=[
            pltpu.VMEM((sections * size, LANES), F32),
            pltpu.VMEM((own * count, 6 * channels), BF16),
            pltpu.VMEM((own * count, 2 * beams), F32),
            pltpu.VMEM((own, count, side), F32),
        ],
        compiler_params=pltpu.CompilerParams(vmem_limit_bytes=LIMIT),
        name="beams",
    )(*blocks, *weights, steer, range_taps)


def steering_tables(beam_index, channel_phase):
    channels = channel_phase.shape[0]
    own = channels // 2
    sub = lax.axis_index("sub")
    place = jnp.arange(channels, dtype=jnp.int32)
    place = jnp.where(place + sub * own >= channels, place + sub * own - channels, place + sub * own)
    turned = jnp.concatenate([channel_phase[own:], channel_phase[:own]])
    phase = jnp.where(sub == 0, channel_phase, turned)
    direction = -1.0 + (2.0 * beam_index.astype(F32) + 1.0) / LOOKS
    angle = math.pi * place.astype(F32)[:, None] * direction[None, :] + phase[:, None]
    cosine, sine = jnp.cos(angle), jnp.sin(angle)
    table = jnp.concatenate(
        [jnp.concatenate([cosine, -sine], 1), jnp.concatenate([sine, cosine], 1)], 0
    )
    high = lax.reduce_precision(table, 8, 7)
    low = lax.reduce_precision(table - high, 8, 7).astype(BF16)
    high = high.astype(BF16)
    return jnp.concatenate([high, high, low], 0)


def permuted(block, sections, step):
    return lax.ppermute(block, "section", [(place, place ^ step) for place in range(sections)])


def swapped(block):
    return lax.ppermute(block, "sub", [(0, 1), (1, 0)])


def factored_steps(echoes, range_taps, pulse_taper, channel_phase, loading, beam_index):
    parts, pulses, gates, lanes = echoes.shape
    sections = lax.axis_size("section")
    order = sorted(range(1, sections), reverse=True)
    view = echoes.reshape(parts, pulses // HOP, HOP * gates, lanes)
    taper = pulse_taper.reshape(2, HOP)

    sent = doppler(view, taper, sections, 0, False)
    got = {0: sent[0]}
    for step in order:
        got[step] = permuted(sent[step], sections, step)
    mine, theirs = doppler(view, taper, sections, 1, True)
    other = swapped(theirs)
    sent = pair_up(mine, other)
    later = {0: sent[0]}
    for step in order:
        later[step] = permuted(sent[step], sections, step)

    steer = steering_tables(beam_index, channel_phase)
    keep, pass_on = gather_sub([got[step] for step in range(sections)])
    other = swapped(pass_on)
    weights = weights_kernel(keep, other, steer, range_taps, loading)
    power, total = beams_kernel(
        [later[step] for step in range(sections)], weights, steer, range_taps
    )
    totals = lax.all_to_all(total, ("section", "sub"), 0, 0, tiled=True)
    noise_level = jnp.sum(totals, axis=0) / (PULSES * gates * sections)
    return (power / (noise_level + epsilon))[None]


def apply_taps(pad_real, pad_imag, range_taps, gate_count):
    axis_gates = pad_real.ndim - 2
    shape_out = pad_real.shape[:axis_gates] + (gate_count,) + pad_real.shape[axis_gates + 1 :]
    out_real = jnp.zeros(shape_out, jnp.float32)
    out_imag = jnp.zeros(shape_out, jnp.float32)
    for offset in range(range_taps.shape[1]):
        part_real = lax.slice_in_dim(pad_real, offset, offset + gate_count, axis=axis_gates)
        part_imag = lax.slice_in_dim(pad_imag, offset, offset + gate_count, axis=axis_gates)
        out_real = out_real + range_taps[0, offset] * part_real - range_taps[1, offset] * part_imag
        out_imag = out_imag + range_taps[0, offset] * part_imag + range_taps[1, offset] * part_real
    return (out_real, out_imag)


def doppler_table(pulse_taper):
    pulse_count = pulse_taper.shape[0]
    pulse_index = jnp.arange(pulse_count, dtype=jnp.int32)
    product = pulse_index[:, None] * pulse_index[None, :] % pulse_count
    phase_angle = 2.0 * math.pi / pulse_count * product.astype(jnp.float32)
    cosine = jnp.cos(phase_angle) * pulse_taper[None, :]
    sine_part = jnp.sin(phase_angle) * pulse_taper[None, :]
    upper_rows = jnp.concatenate([cosine, sine_part], axis=1)
    lower_rows = jnp.concatenate([-sine_part, cosine], axis=1)
    return jnp.concatenate([upper_rows, lower_rows], axis=0)


def transform(doppler, segment):
    shape_in = segment.shape
    flattened = segment.reshape(shape_in[0] * shape_in[1], -1)
    result = jnp.dot(doppler, flattened, precision=precise, preferred_element_type=jnp.float32)
    return result.reshape(shape_in)


def batched(first, second):
    return jnp.einsum("dij,djk->dik", first, second, precision=precise)


def complex_product(left_real, left_imag, right_real, right_imag):
    out_real = batched(left_real, right_real) - batched(left_imag, right_imag)
    out_imag = batched(left_real, right_imag) + batched(left_imag, right_real)
    return (out_real, out_imag)


def gram_product(first, second):
    return jnp.einsum("dgi,dgj->dij", first, second, precision=precise)


def loaded_inverse(real_part, imag_part, loading):
    gate_count = real_part.shape[1]
    channels = real_part.shape[2]
    cov_real = (
        gram_product(real_part, real_part) + gram_product(imag_part, imag_part)
    ) / gate_count
    cov_imag = (
        gram_product(real_part, imag_part) - gram_product(imag_part, real_part)
    ) / gate_count
    identity = jnp.eye(channels, dtype=jnp.float32)
    trace_sum = jnp.sum(cov_real * identity[None], axis=(1, 2))
    cov_real = cov_real + (loading[0] * trace_sum / channels)[:, None, None] * identity[None]
    row_bound = jnp.max(jnp.sum(jnp.abs(cov_real) + jnp.abs(cov_imag), axis=2), axis=1)
    inv_real = identity[None] / row_bound[:, None, None]
    inv_imag = jnp.zeros_like(inv_real)
    for _ in range(ITERS):
        prod_real, prod_imag = complex_product(cov_real, cov_imag, inv_real, inv_imag)
        inv_real, inv_imag = complex_product(
            inv_real, inv_imag, 2.0 * identity[None] - prod_real, -prod_imag
        )
    return (inv_real, inv_imag)


def steering(beam_index, channel_phase):
    channels = channel_phase.shape[0]
    direction = -1.0 + (2.0 * beam_index.astype(jnp.float32) + 1.0) / LOOKS
    phase_angle = (
        math.pi * jnp.arange(channels, dtype=jnp.float32)[:, None] * direction[None, :]
        + channel_phase[:, None]
    )
    return (jnp.cos(phase_angle), jnp.sin(phase_angle))


def beam_weights(inv_real, inv_imag, steer_real, steer_imag):
    weight_real = jnp.einsum("dij,jb->dib", inv_real, steer_real, precision=precise) - jnp.einsum(
        "dij,jb->dib", inv_imag, steer_imag, precision=precise
    )
    weight_imag = jnp.einsum("dij,jb->dib", inv_real, steer_imag, precision=precise) + jnp.einsum(
        "dij,jb->dib", inv_imag, steer_real, precision=precise
    )
    gain_norm = jnp.sum(steer_real[None] * weight_real + steer_imag[None] * weight_imag, axis=1)
    return (weight_real / gain_norm[:, None, :], weight_imag / gain_norm[:, None, :])


def form_beams(data_real, data_imag, weight_real, weight_imag):
    out_real = jnp.einsum("dgc,dcb->dgb", data_real, weight_real, precision=precise) + jnp.einsum(
        "dgc,dcb->dgb", data_imag, weight_imag, precision=precise
    )
    out_imag = jnp.einsum("dgc,dcb->dgb", data_imag, weight_real, precision=precise) - jnp.einsum(
        "dgc,dcb->dgb", data_real, weight_imag, precision=precise
    )
    return out_real * out_real + out_imag * out_imag


def on_device(echoes, range_taps, pulse_taper, channel_phase, loading, beam_index):
    rim_width = range_taps.shape[1] // 2
    doppler = doppler_table(pulse_taper)
    spectra = [
        transform(
            doppler, lax.slice_in_dim(echoes, interval * HOP, interval * HOP + PULSES, axis=1)
        )
        for interval in range(INTERVALS)
    ]
    turned = [
        lax.all_to_all(
            lax.all_to_all(spectrum, "section", split_axis=1, concat_axis=2, tiled=True),
            "sub",
            split_axis=1,
            concat_axis=3,
            tiled=True,
        )
        for spectrum in spectra
    ]
    refined = []
    for spectrum in turned:
        padded_bins = jnp.pad(spectrum, ((0, 0), (0, 0), (rim_width, rim_width), (0, 0)))
        part_real, part_imag = apply_taps(
            padded_bins[0], padded_bins[1], range_taps, spectrum.shape[2]
        )
        refined.append(jnp.stack([part_real, part_imag]))
    turned = refined
    steer_real, steer_imag = steering(beam_index, channel_phase)
    interval = 0
    inv_real, inv_imag = loaded_inverse(turned[interval][0], turned[interval][1], loading)
    weight_real, weight_imag = beam_weights(inv_real, inv_imag, steer_real, steer_imag)
    beam_power = form_beams(
        turned[interval + 1][0], turned[interval + 1][1], weight_real, weight_imag
    )
    partials = [jnp.sum(beam_power, axis=(0, 1))]
    totals = lax.psum(jnp.stack(partials), ("section", "sub"))
    noise_level = totals / (PULSES * turned[0].shape[2])
    return jnp.stack([beam_power / (noise_level[0] + epsilon)])


def solution(mesh):
    in_specs = (P("groups", None, "section", "sub"), P(), P(), P(), P(), P())
    out_specs = P("groups", ("section", "sub"), None, None)
    sections = mesh.shape["section"]
    small = sections == 8 and mesh.shape["sub"] == 2

    def run(echoes, range_taps, pulse_taper, channel_phase, loading, beam_index):
        args = (echoes, range_taps, pulse_taper, channel_phase, loading, beam_index)
        fits = small and echoes.shape[2] == 4 and echoes.shape[3] == LANES
        return factored_steps(*args) if fits else on_device(*args)

    return jax.shard_map(run, mesh=mesh, in_specs=in_specs, out_specs=out_specs, check_vma=False)
```

profile of v0, /device:TPU:0, one launch (start us, length us, event | category | flops | bytes accessed | tf_op | source)
XLA Modules:
  0.0 78.1 jit_solution(3215512740128847997)
XLA Ops:
  0.0 1.4 %copy-done = f32[2,384,4,128]{3,2,1,0:T(4,128)S(1)} copy-done((f32[2,384,4,128]{3,2,1,0:T(4,128)S(1)}, f32[2,384,4,128]{3,2,1,0:T(4,128)}, u32[]{:S(2)}) %copy-start) | copy-done | bytes 1572888
  1.4 1.0 %copy-done.1 = bf16[4,256,256]{2,1,0:T(8,128)(2,1)S(1)} copy-done((bf16[4,256,256]{2,1,0:T(8,128)(2,1)S(1)}, bf16[4,256,256]{2,1,0:T(8,128)(2,1)}, u32[]{:S(2)}) %copy-start.1) | copy-done | bytes 524312
  2.5 0.7 copy-done.2
  3.1 1.2 %shard_map.83 = (f32[2,4,32,128]{3,2,1,0:T(8,128)S(1)}, f32[2,4,32,128]{3,2,1,0:T(8,128)S(1)}, f32[2,4,32,128]{3,2,1,0:T(8,128)S(1)}, f32[2,4,32,128]{3,2,1,0:T(...) custom-call(f32[2,3,512,128]{3,2,1,0:T(8,128)S(1)} %bitcast.15, ...), custom_call_target="tpu_custom_call" | custom-call | tf_op jit(solution)/shard_map/pallas_call | solution.py:120
  4.4 0.0 copy-start.4
  4.4 4.0 %collective-permute-start.10 = (f32[2,4,32,128]{3,2,1,0:T(8,128)S(1)}, f32[2,4,32,128]{3,2,1,0:T(8,128)S(1)}, u32[]{:S(2)}, u32[]{:S(2)}) collective-permute-start(f32[2,4,32,128]{3,2,1,0:T(8,128)S(1)} %get-tuple-element.45), channel_id=1, source_target_pairs={{0,6},{2,4},{4,2},{6,0},{8,14},{10,12},{12,10},{14,8},{1,7},{3,5},... | collective-permute-start | bytes 393224 | tf_op jit(solution)/shard_map/ppermute | solution.py:404
  8.4 2.6 %collective-permute-start.11 = (f32[2,4,32,128]{3,2,1,0:T(8,128)S(1)}, f32[2,4,32,128]{3,2,1,0:T(8,128)S(1)}, u32[]{:S(2)}, u32[]{:S(2)}) collective-permute-start(f32[2,4,32,128]{3,2,1,0:T(8,128)S(1)} %get-tuple-element.46), channel_id=1, source_target_pairs={{0,8},{2,10},{4,12},{6,14},{8,0},{10,2},{12,4},{14,6},{1,9},{3,11}... | collective-permute-start | bytes 393224 | tf_op jit(solution)/shard_map/ppermute | solution.py:404
  11.0 0.3 collective-permute-start.12
  11.3 2.5 %collective-permute-start.13 = (f32[2,4,32,128]{3,2,1,0:T(8,128)S(1)}, f32[2,4,32,128]{3,2,1,0:T(8,128)S(1)}, u32[]{:S(2)}, u32[]{:S(2)}) collective-permute-start(f32[2,4,32,128]{3,2,1,0:T(8,128)S(1)} %get-tuple-element.48), channel_id=1, source_target_pairs={{0,12},{2,14},{4,8},{6,10},{8,4},{10,6},{12,0},{14,2},{1,13},{3,15... | collective-permute-start | bytes 393224 | tf_op jit(solution)/shard_map/ppermute | solution.py:404
  13.8 2.3 %collective-permute-start.14 = (f32[2,4,32,128]{3,2,1,0:T(8,128)S(1)}, f32[2,4,32,128]{3,2,1,0:T(8,128)S(1)}, u32[]{:S(2)}, u32[]{:S(2)}) collective-permute-start(f32[2,4,32,128]{3,2,1,0:T(8,128)S(1)} %get-tuple-element.49), channel_id=1, source_target_pairs={{0,14},{2,12},{4,10},{6,8},{8,6},{10,4},{12,2},{14,0},{1,15},{3,13... | collective-permute-start | bytes 393224 | tf_op jit(solution)/shard_map/ppermute | solution.py:404
  16.1 1.2 %shard_map.82 = (f32[8,2,4,16,128]{4,3,2,1,0:T(8,128)S(1)}, f32[8,2,4,16,128]{4,3,2,1,0:T(8,128)S(1)}) custom-call(f32[2,3,512,128]{3,2,1,0:T(8,128)S(1)} %bitcast.16, f32[2,128]{1,0:T(2,128)S(1)} %bitcast.29, bf16[4,256,256]{2,1,0:T(8,128)(2,1)S(1)} %copy-done.1), custom_call_target="tpu_custom_call" | custom-call | tf_op jit(solution)/shard_map/pallas_call | solution.py:120
  17.3 0.0 collective-permute-done.10.refs_3_
  17.3 0.6 collective-permute-start.8
  18.0 8.7 %collective-permute-done.11.refs_4_ = f32[2,4,32,128]{3,2,1,0:T(8,128)S(1)} collective-permute-done((f32[2,4,32,128]{3,2,1,0:T(8,128)S(1)}, f32[2,4,32,128]{3,2,1,0:T(8,128)S(1)}, u32[]{:S(2)}, u32[]{:S(2)}) %collective-permute-start.11) | collective-permute-done | bytes 131104 | tf_op jit(solution)/shard_map/ppermute | solution.py:404
  26.6 0.0 collective-permute-start.9
  26.6 2.3 %collective-permute-done.12.refs_5_ = f32[2,4,32,128]{3,2,1,0:T(8,128)S(1)} collective-permute-done((f32[2,4,32,128]{3,2,1,0:T(8,128)S(1)}, f32[2,4,32,128]{3,2,1,0:T(8,128)S(1)}, u32[]{:S(2)}, u32[]{:S(2)}) %collective-permute-start.12) | collective-permute-done | bytes 131104 | tf_op jit(solution)/shard_map/ppermute | solution.py:404
  28.9 0.0 collective-permute-start
  28.9 0.0 collective-permute-done.13.refs_6_
  28.9 0.0 collective-permute-done.14.refs_7_
  28.9 0.0 collective-permute-done.8.refs_1_
  28.9 2.7 %collective-permute-done.9.refs_2_ = f32[2,4,32,128]{3,2,1,0:T(8,128)S(1)} collective-permute-done((f32[2,4,32,128]{3,2,1,0:T(8,128)S(1)}, f32[2,4,32,128]{3,2,1,0:T(8,128)S(1)}, u32[]{:S(2)}, u32[]{:S(2)}) %collective-permute-start.9) | collective-permute-done | bytes 131104 | tf_op jit(solution)/shard_map/ppermute | solution.py:404
  31.6 0.1 gather_sub.1
  31.7 0.1 collective-permute-start.15
  31.8 1.0 %fusion.4 = (f32[256,256]{1,0:T(8,128)S(1)}, f32[256,256]{1,0:T(8,128)S(1)}, f32[256,256]{1,0:T(8,128)S(1)}) fusion(f32[256]{0:T(256)S(1)} %get-tuple-element.67, f32[256]{0:T(256)S(1)} %multiply_add_fusion.2, f32[256]{0:T(256)S(1)} %get-tuple-element.66), kind=kLoop, calls=%fused_computation.10 | loop fusion | flops 196608 | bytes 789504 | tf_op jit(solution)/shard_map/neg | solution.py:395
  32.8 0.0 collective-permute-done.other_ref
  32.8 0.1 pair_up.1
  32.9 0.1 collective-permute-start.1
  33.0 4.4 %collective-permute-start.2 = (f32[2,2,4,16,128]{4,3,2,1,0:T(8,128)S(1)}, f32[2,2,4,16,128]{4,3,2,1,0:T(8,128)S(1)}, u32[]{:S(2)}, u32[]{:S(2)}) collective-permute-start(f32[2,2,4,16,128]{4,3,2,1,0:T(8,128)S(1)} %get-tuple-element.36), channel_id=1, source_target_pairs={{0,4},{2,6},{4,0},{6,2},{8,12},{10,14},{12,8},{14,10},{1,5},{3,7},... | collective-permute-start | bytes 393224 | tf_op jit(solution)/shard_map/ppermute | solution.py:404
  37.5 0.1 reduce-precision_convert_fusion
  37.6 0.0 copy-start.3
  37.6 0.1 collective-permute-start.3
  37.7 3.0 %collective-permute-start.4 = (f32[2,2,4,16,128]{4,3,2,1,0:T(8,128)S(1)}, f32[2,2,4,16,128]{4,3,2,1,0:T(8,128)S(1)}, u32[]{:S(2)}, u32[]{:S(2)}) collective-permute-start(f32[2,2,4,16,128]{4,3,2,1,0:T(8,128)S(1)} %get-tuple-element.38), channel_id=1, source_target_pairs={{0,8},{2,10},{4,12},{6,14},{8,0},{10,2},{12,4},{14,6},{1,9},{3,11}... | collective-permute-start | bytes 393224 | tf_op jit(solution)/shard_map/ppermute | solution.py:404
  40.7 0.0 collective-permute-done.15
  40.7 0.9 %collective-permute-start.5 = (f32[2,2,4,16,128]{4,3,2,1,0:T(8,128)S(1)}, f32[2,2,4,16,128]{4,3,2,1,0:T(8,128)S(1)}, u32[]{:S(2)}, u32[]{:S(2)}) collective-permute-start(f32[2,2,4,16,128]{4,3,2,1,0:T(8,128)S(1)} %get-tuple-element.39), channel_id=1, source_target_pairs={{0,10},{2,8},{4,14},{6,12},{8,2},{10,0},{12,6},{14,4},{1,11},{3,9}... | collective-permute-start | bytes 393224 | tf_op jit(solution)/shard_map/ppermute | solution.py:404
  41.6 0.0 collective-permute-done.1
  41.6 2.4 %collective-permute-start.6 = (f32[2,2,4,16,128]{4,3,2,1,0:T(8,128)S(1)}, f32[2,2,4,16,128]{4,3,2,1,0:T(8,128)S(1)}, u32[]{:S(2)}, u32[]{:S(2)}) collective-permute-start(f32[2,2,4,16,128]{4,3,2,1,0:T(8,128)S(1)} %get-tuple-element.40), channel_id=1, source_target_pairs={{0,12},{2,14},{4,8},{6,10},{8,4},{10,6},{12,0},{14,2},{1,13},{3,15... | collective-permute-start | bytes 393224 | tf_op jit(solution)/shard_map/ppermute | solution.py:404
  44.0 1.9 %collective-permute-done.2 = f32[2,2,4,16,128]{4,3,2,1,0:T(8,128)S(1)} collective-permute-done((f32[2,2,4,16,128]{4,3,2,1,0:T(8,128)S(1)}, f32[2,2,4,16,128]{4,3,2,1,0:T(8,128)S(1)}, u32[]{:S(2)}, u32[]{:S(2)}) %collective-permute-start.2) | collective-permute-done | bytes 131104 | tf_op jit(solution)/shard_map/ppermute | solution.py:404
  45.9 0.0 collective-permute-start.7
  45.9 0.1 pad_maximum_fusion.steer_ref.refs_13_
  46.6 10.1 %weights.1 = (bf16[16,64,512]{2,1,0:T(8,128)(2,1)S(1)}, bf16[16,64,512]{2,1,0:T(8,128)(2,1)S(1)}, bf16[16,64,512]{2,1,0:T(8,128)(2,1)S(1)}, bf16[16,64,512]{2,1,0:T(8,128)(2,1)S(1)}, f32[16,256]{1,0:T(8,128)S(1)}) custom-call(f32[1024,128]{1,0:T(8,128)S(1)} %bitcast.17, f32[1024,128]{1,0:T(8,128)S(1)} %bitcast.18, ...), custom_call_target="tpu_custom_call" | custom-call | tf_op jit(solution)/shard_map/weights/pallas_call | solution.py:296
  56.8 0.0 collective-permute-done.3
  56.8 0.0 collective-permute-done.4
  56.8 3.0 %collective-permute-done.5 = f32[2,2,4,16,128]{4,3,2,1,0:T(8,128)S(1)} collective-permute-done((f32[2,2,4,16,128]{4,3,2,1,0:T(8,128)S(1)}, f32[2,2,4,16,128]{4,3,2,1,0:T(8,128)S(1)}, u32[]{:S(2)}, u32[]{:S(2)}) %collective-permute-start.5) | collective-permute-done | bytes 131104 | tf_op jit(solution)/shard_map/ppermute | solution.py:404
  59.8 0.0 collective-permute-done.6
  59.8 0.0 collective-permute-done.7
  59.8 3.4 %beams.1 = (f32[16,32,256]{2,1,0:T(8,128)S(1)}, f32[16,256]{1,0:T(8,128)S(1)}) custom-call(f32[256,128]{1,0:T(8,128)S(1)} %bitcast.19, f32[256,128]{1,0:T(8,128)S(1)} %bitcast.20, f32[256,128]{1,0:T(8,128)S(1)} %bitcast.21, f32[256,128]{1,0:T(8,128)S(1)} %bitcast.22, f32[256,128]{1,0:T(8,128)S(1)} %bitcast.23, f32[256,128]{1,0:T(8,128)S(1)} %bitcast.24, ...), custom_call_target="tpu_custom_call" | custom-call | tf_op jit(solution)/shard_map/beams/pallas_call | solution.py:364
  63.2 14.0 %all_to_all.9 = f32[16,1,256]{2,1,0:T(1,128)S(1)} all-to-all(f32[16,1,256]{2,1,0:T(1,128)S(1)} %copy.9), channel_id=1, replica_groups=mesh['groups'=2,'section'=8,'sub'=2] {'section','sub'}, dimensions={0} | all-to-all | bytes 32768 | tf_op jit(solution)/shard_map/all_to_all | solution.py:436
  77.2 0.9 %divide_bitcast_fusion = f32[1,16,32,256]{3,2,1,0:T(8,128)} fusion(f32[16,32,256]{2,1,0:T(8,128)S(1)} %get-tuple-element.57, f32[256]{0:T(256)S(1)} %multiply_add_fusion.1), kind=kLoop, calls=%fused_computation.6 | loop fusion | flops 131072 | bytes 1049600 | tf_op jit(solution)/shard_map/broadcast_in_dim | solution.py:438
  (13 shorter events, 0.1 us)
Async XLA Ops:
  0.0 1.4 %copy-start = (f32[2,384,4,128]{3,2,1,0:T(4,128)S(1)}, f32[2,384,4,128]{3,2,1,0:T(4,128)}, u32[]{:S(2)}) copy-start(f32[2,384,4,128]{3,2,1,0:T(4,128)} %param.8) | copy-start | bytes 4718596
  1.4 1.0 %copy-start.1 = (bf16[4,256,256]{2,1,0:T(8,128)(2,1)S(1)}, bf16[4,256,256]{2,1,0:T(8,128)(2,1)}, u32[]{:S(2)}) copy-start(bf16[4,256,256]{2,1,0:T(8,128)(2,1)} %constant.32.clone.table_ref) | copy-start | bytes 1572868
  2.5 0.7 copy-start.2
  4.4 13.0 %copy-start.4 = (f32[256]{0:T(256)S(1)}, f32[256]{0:T(256)}, u32[]{:S(2)}) copy-start(f32[256]{0:T(256)} %param.11) | copy-start | bytes 3076
  4.4 13.0 %collective-permute-start.10 = (f32[2,4,32,128]{3,2,1,0:T(8,128)S(1)}, f32[2,4,32,128]{3,2,1,0:T(8,128)S(1)}, u32[]{:S(2)}, u32[]{:S(2)}) collective-permute-start(f32[2,4,32,128]{3,2,1,0:T(8,128)S(1)} %get-tuple-element.45), channel_id=1, source_target_pairs={{0,6},{2,4},{4,2},{6,0},{8,14},{10,12},{12,10},{14,8},{1,7},{3,5},... | collective-permute-start | bytes 393224 | tf_op jit(solution)/shard_map/ppermute | solution.py:404
  8.4 18.2 %collective-permute-start.11 = (f32[2,4,32,128]{3,2,1,0:T(8,128)S(1)}, f32[2,4,32,128]{3,2,1,0:T(8,128)S(1)}, u32[]{:S(2)}, u32[]{:S(2)}) collective-permute-start(f32[2,4,32,128]{3,2,1,0:T(8,128)S(1)} %get-tuple-element.46), channel_id=1, source_target_pairs={{0,8},{2,10},{4,12},{6,14},{8,0},{10,2},{12,4},{14,6},{1,9},{3,11}... | collective-permute-start | bytes 393224 | tf_op jit(solution)/shard_map/ppermute | solution.py:404
  11.0 17.9 %collective-permute-start.12 = (f32[2,4,32,128]{3,2,1,0:T(8,128)S(1)}, f32[2,4,32,128]{3,2,1,0:T(8,128)S(1)}, u32[]{:S(2)}, u32[]{:S(2)}) collective-permute-start(f32[2,4,32,128]{3,2,1,0:T(8,128)S(1)} %get-tuple-element.47), channel_id=1, source_target_pairs={{0,10},{2,8},{4,14},{6,12},{8,2},{10,0},{12,6},{14,4},{1,11},{3,9}... | collective-permute-start | bytes 393224 | tf_op jit(solution)/shard_map/ppermute | solution.py:404
  11.3 17.6 %collective-permute-start.13 = (f32[2,4,32,128]{3,2,1,0:T(8,128)S(1)}, f32[2,4,32,128]{3,2,1,0:T(8,128)S(1)}, u32[]{:S(2)}, u32[]{:S(2)}) collective-permute-start(f32[2,4,32,128]{3,2,1,0:T(8,128)S(1)} %get-tuple-element.48), channel_id=1, source_target_pairs={{0,12},{2,14},{4,8},{6,10},{8,4},{10,6},{12,0},{14,2},{1,13},{3,15... | collective-permute-start | bytes 393224 | tf_op jit(solution)/shard_map/ppermute | solution.py:404
  13.8 15.1 %collective-permute-start.14 = (f32[2,4,32,128]{3,2,1,0:T(8,128)S(1)}, f32[2,4,32,128]{3,2,1,0:T(8,128)S(1)}, u32[]{:S(2)}, u32[]{:S(2)}) collective-permute-start(f32[2,4,32,128]{3,2,1,0:T(8,128)S(1)} %get-tuple-element.49), channel_id=1, source_target_pairs={{0,14},{2,12},{4,10},{6,8},{8,6},{10,4},{12,2},{14,0},{1,15},{3,13... | collective-permute-start | bytes 393224 | tf_op jit(solution)/shard_map/ppermute | solution.py:404
  16.1 15.7 %copy-start.5 = (s32[256]{0:T(256)S(1)}, s32[256]{0:T(256)}, u32[]{:S(2)}) copy-start(s32[256]{0:T(256)} %param.13) | copy-start | bytes 3076
  17.3 11.6 %collective-permute-start.8 = (f32[2,4,32,128]{3,2,1,0:T(8,128)S(1)}, f32[2,4,32,128]{3,2,1,0:T(8,128)S(1)}, u32[]{:S(2)}, u32[]{:S(2)}) collective-permute-start(f32[2,4,32,128]{3,2,1,0:T(8,128)S(1)} %get-tuple-element.43), channel_id=1, source_target_pairs={{0,2},{2,0},{4,6},{6,4},{8,10},{10,8},{12,14},{14,12},{1,3},{3,1},... | collective-permute-start | bytes 393224 | tf_op jit(solution)/shard_map/ppermute | solution.py:404
  26.6 5.0 %collective-permute-start.9 = (f32[2,4,32,128]{3,2,1,0:T(8,128)S(1)}, f32[2,4,32,128]{3,2,1,0:T(8,128)S(1)}, u32[]{:S(2)}, u32[]{:S(2)}) collective-permute-start(f32[2,4,32,128]{3,2,1,0:T(8,128)S(1)} %get-tuple-element.44), channel_id=1, source_target_pairs={{0,4},{2,6},{4,0},{6,2},{8,12},{10,14},{12,8},{14,10},{1,5},{3,7},... | collective-permute-start | bytes 393224 | tf_op jit(solution)/shard_map/ppermute | solution.py:404
  28.9 4.0 %collective-permute-start = (f32[8,2,4,16,128]{4,3,2,1,0:T(8,128)S(1)}, f32[8,2,4,16,128]{4,3,2,1,0:T(8,128)S(1)}, u32[]{:S(2)}, u32[]{:S(2)}) collective-permute-start(f32[8,2,4,16,128]{4,3,2,1,0:T(8,128)S(1)} %get-tuple-element.33), channel_id=1, source_target_pairs={{0,1},{1,0},{2,3},{3,2},{4,5},{5,4},{6,7},{7,6},{8,9},{9,8},{10,11... | collective-permute-start | bytes 1572872 | tf_op jit(solution)/shard_map/ppermute | solution.py:408
  31.7 9.0 %collective-permute-start.15 = (f32[8,2,4,16,128]{4,3,2,1,0:T(8,128)S(1)}, f32[8,2,4,16,128]{4,3,2,1,0:T(8,128)S(1)}, u32[]{:S(2)}, u32[]{:S(2)}) collective-permute-start(f32[8,2,4,16,128]{4,3,2,1,0:T(8,128)S(1)} %get-tuple-element.51), channel_id=1, source_target_pairs={{0,1},{1,0},{2,3},{3,2},{4,5},{5,4},{6,7},{7,6},{8,9},{9,8},{10,11... | collective-permute-start | bytes 1572872 | tf_op jit(solution)/shard_map/ppermute | solution.py:408
  32.9 8.7 %collective-permute-start.1 = (f32[2,2,4,16,128]{4,3,2,1,0:T(8,128)S(1)}, f32[2,2,4,16,128]{4,3,2,1,0:T(8,128)S(1)}, u32[]{:S(2)}, u32[]{:S(2)}) collective-permute-start(f32[2,2,4,16,128]{4,3,2,1,0:T(8,128)S(1)} %get-tuple-element.35), channel_id=1, source_target_pairs={{0,2},{2,0},{4,6},{6,4},{8,10},{10,8},{12,14},{14,12},{1,3},{3,1},... | collective-permute-start | bytes 393224 | tf_op jit(solution)/shard_map/ppermute | solution.py:404
  33.0 12.8 %collective-permute-start.2 = (f32[2,2,4,16,128]{4,3,2,1,0:T(8,128)S(1)}, f32[2,2,4,16,128]{4,3,2,1,0:T(8,128)S(1)}, u32[]{:S(2)}, u32[]{:S(2)}) collective-permute-start(f32[2,2,4,16,128]{4,3,2,1,0:T(8,128)S(1)} %get-tuple-element.36), channel_id=1, source_target_pairs={{0,4},{2,6},{4,0},{6,2},{8,12},{10,14},{12,8},{14,10},{1,5},{3,7},... | collective-permute-start | bytes 393224 | tf_op jit(solution)/shard_map/ppermute | solution.py:404
  37.6 9.0 %copy-start.3 = (f32[2,5]{1,0:T(2,128)S(1)}, f32[2,5]{1,0:T(2,128)}, u32[]{:S(2)}) copy-start(f32[2,5]{1,0:T(2,128)} %refs_14_.1) | copy-start | bytes 124
  37.6 19.2 %collective-permute-start.3 = (f32[2,2,4,16,128]{4,3,2,1,0:T(8,128)S(1)}, f32[2,2,4,16,128]{4,3,2,1,0:T(8,128)S(1)}, u32[]{:S(2)}, u32[]{:S(2)}) collective-permute-start(f32[2,2,4,16,128]{4,3,2,1,0:T(8,128)S(1)} %get-tuple-element.37), channel_id=1, source_target_pairs={{0,6},{2,4},{4,2},{6,0},{8,14},{10,12},{12,10},{14,8},{1,7},{3,5},... | collective-permute-start | bytes 393224 | tf_op jit(solution)/shard_map/ppermute | solution.py:404
  37.7 19.1 %collective-permute-start.4 = (f32[2,2,4,16,128]{4,3,2,1,0:T(8,128)S(1)}, f32[2,2,4,16,128]{4,3,2,1,0:T(8,128)S(1)}, u32[]{:S(2)}, u32[]{:S(2)}) collective-permute-start(f32[2,2,4,16,128]{4,3,2,1,0:T(8,128)S(1)} %get-tuple-element.38), channel_id=1, source_target_pairs={{0,8},{2,10},{4,12},{6,14},{8,0},{10,2},{12,4},{14,6},{1,9},{3,11}... | collective-permute-start | bytes 393224 | tf_op jit(solution)/shard_map/ppermute | solution.py:404
  40.7 19.1 %collective-permute-start.5 = (f32[2,2,4,16,128]{4,3,2,1,0:T(8,128)S(1)}, f32[2,2,4,16,128]{4,3,2,1,0:T(8,128)S(1)}, u32[]{:S(2)}, u32[]{:S(2)}) collective-permute-start(f32[2,2,4,16,128]{4,3,2,1,0:T(8,128)S(1)} %get-tuple-element.39), channel_id=1, source_target_pairs={{0,10},{2,8},{4,14},{6,12},{8,2},{10,0},{12,6},{14,4},{1,11},{3,9}... | collective-permute-start | bytes 393224 | tf_op jit(solution)/shard_map/ppermute | solution.py:404
  41.6 18.2 %collective-permute-start.6 = (f32[2,2,4,16,128]{4,3,2,1,0:T(8,128)S(1)}, f32[2,2,4,16,128]{4,3,2,1,0:T(8,128)S(1)}, u32[]{:S(2)}, u32[]{:S(2)}) collective-permute-start(f32[2,2,4,16,128]{4,3,2,1,0:T(8,128)S(1)} %get-tuple-element.40), channel_id=1, source_target_pairs={{0,12},{2,14},{4,8},{6,10},{8,4},{10,6},{12,0},{14,2},{1,13},{3,15... | collective-permute-start | bytes 393224 | tf_op jit(solution)/shard_map/ppermute | solution.py:404
  45.9 13.9 %collective-permute-start.7 = (f32[2,2,4,16,128]{4,3,2,1,0:T(8,128)S(1)}, f32[2,2,4,16,128]{4,3,2,1,0:T(8,128)S(1)}, u32[]{:S(2)}, u32[]{:S(2)}) collective-permute-start(f32[2,2,4,16,128]{4,3,2,1,0:T(8,128)S(1)} %get-tuple-element.41), channel_id=1, source_target_pairs={{0,14},{2,12},{4,10},{6,8},{8,6},{10,4},{12,2},{14,0},{1,15},{3,13... | collective-permute-start | bytes 393224 | tf_op jit(solution)/shard_map/ppermute | solution.py:404
where the time goes:
time: 78.4 us; the launch traced here: 78.1 us
  starting transfers between devices  23.2 us (30%)
  waiting for transfers between devices  18.5 us (24%)
  Pallas kernels  16.1 us (21%)
  blocking collectives  14 us (18%)
  local copies, waits for them, and re-layouts  3.17 us (4%)
  other arithmetic  2.22 us (3%)
  between operations  0.87 us (1%)
    ppermute x14, starting transfers between devices, permuted(): lax.ppermute(block, 'section', [(place, place ^ step) for place in range(...  23.2 us
    ppermute x14, waiting for transfers between devices, permuted(): lax.ppermute(block, 'section', [(place, place ^ step) for place in range(...  18.5 us
    all_to_all x1, blocking collectives, factored_steps(): totals = lax.all_to_all(total, ('section', 'sub'), 0, 0, tiled=True)  14 us
    pallas_call x1, Pallas kernels, weights_kernel(): pl.pallas_call(body, in_specs=[VMEM] * 3 + [SMEM] * 2, out_specs=[VMEM] *...  10.1 us
    pallas_call x1, Pallas kernels, beams_kernel(): pl.pallas_call(body, in_specs=[VMEM] * (sections + 6) + [SMEM], out_specs...  3.36 us
    unnamed x12, local copies, waits for them, and re-layouts  3.14 us
    pallas_call x2, Pallas kernels, doppler(): pl.pallas_call(body, in_specs=[VMEM] * 3, out_specs=[VMEM] * len(outs), o...  2.45 us
  transfers between devices with their start and end apart: 16, of which 5 were waited for; matrix products, arithmetic and copies ran while one was open for 2% of the time, Pallas kernels for 15%

commit v1 on v0

--- a/solution.py
+++ b/solution.py
@@ -23,7 +23,9 @@
 LANES = 128
 VMEM = pl.BlockSpec(memory_space=pltpu.VMEM)
 SMEM = pl.BlockSpec(memory_space=pltpu.SMEM)
+HBM = pl.BlockSpec(memory_space=pltpu.HBM)
 LIMIT = 16 << 20
+PAD = 8
 
 
 def split(value):
@@ -54,15 +56,19 @@
     for parity in (0, 1):
         phase = 2.0 * np.pi * ((bins * np.arange(parity, pulses, 2)[None, :]) % pulses) / pulses
         cosine, sine = np.cos(phase), np.sin(phase)
-        table = np.concatenate(
-            [np.concatenate([cosine, sine], 1), np.concatenate([-sine, cosine], 1)], 0
-        ).astype(np.float32)
+        table = np.concatenate([cosine, sine], 1).astype(np.float32)
         high = table.astype(jnp.bfloat16)
         tables += [high, (table - high.astype(np.float32)).astype(jnp.bfloat16)]
     return np.stack(tables)
 
 
-def doppler_body(gates, hop, interval, view_ref, taper_ref, table_ref, result, tapers):
+def full_table(rows):
+    half = rows.shape[1] // 2
+    turned = jnp.concatenate([-rows[:, half:], rows[:, :half]], axis=1)
+    return jnp.concatenate([rows, turned], axis=0)
+
+
+def doppler_body(gates, hop, view_ref, taper_ref, table_ref, result, tapers):
     half = hop
     for segment in (0, 1):
         row = taper_ref[segment : segment + 1, :]
@@ -73,11 +79,11 @@
             for part in (0, 1):
                 for segment in (0, 1):
                     at = pl.ds(parity * gates + gate, hop // 2, stride=2 * gates)
-                    block = view_ref[part, interval + segment, at, :]
+                    block = view_ref[part, segment, at, :]
                     taper = tapers[pl.ds(segment * hop + parity, hop // 2, stride=2), :]
                     rows.append(block * taper)
             data = split(jnp.concatenate(rows, axis=0))
-            table = (table_ref[2 * parity], table_ref[2 * parity + 1])
+            table = full_table(table_ref[2 * parity]), full_table(table_ref[2 * parity + 1])
             value = triple(dot, table, data)
             if parity == 0:
                 even = value
@@ -94,8 +100,19 @@
     own = per // 2
 
     def body(view_ref, taper_ref, table_ref, *rest):
-        out_refs, result, tapers = rest[:-2], rest[-2], rest[-1]
-        doppler_body(gates, HOP, interval, view_ref, taper_ref, table_ref, result, tapers)
+        outs = 2 if split_sub else sections
+        out_refs, scratch = rest[:outs], rest[outs:]
+        result, tapers, own_view, own_taper, own_table, sems = scratch
+        copies = [pltpu.make_async_copy(taper_ref, own_taper, sems.at[0])]
+        copies.append(pltpu.make_async_copy(table_ref, own_table, sems.at[1]))
+        for part in (0, 1):
+            blocks = view_ref.at[part, pl.ds(interval, 2)]
+            copies.append(pltpu.make_async_copy(blocks, own_view.at[part], sems.at[2 + part]))
+        for copy in copies:
+            copy.start()
+        for copy in copies:
+            copy.wait()
+        doppler_body(gates, HOP, own_view, own_taper, own_table, result, tapers)
         section = lax.axis_index("section")
         if not split_sub:
             for step in range(sections):
@@ -119,15 +136,19 @@
         outs = [jax.ShapeDtypeStruct(shape, F32)] * sections
     return pl.pallas_call(
         body,
-        in_specs=[VMEM] * 3,
+        in_specs=[HBM] * 3,
         out_specs=[VMEM] * len(outs),
         out_shape=outs,
         scratch_shapes=[
             pltpu.VMEM((2, gates, PULSES, LANES), F32),
             pltpu.VMEM((PULSES, LANES), F32),
+            pltpu.VMEM((view.shape[0], 2) + view.shape[2:], F32),
+            pltpu.VMEM(taper.shape, F32),
+            pltpu.VMEM(tables.shape, BF16),
+            pltpu.SemaphoreType.DMA((4,)),
         ],
         compiler_params=pltpu.CompilerParams(vmem_limit_bytes=LIMIT),
-    )(view, taper, tables)
+    )(*[pltpu.with_memory_space_constraint(v, pltpu.HBM) for v in (view, taper, tables)])
 
 
 def gather_sub(blocks):
@@ -225,7 +246,7 @@
 
     def body(mine_ref, other_ref, steer_ref, taps_ref, load_ref,
              bh_ref, bl_ref, th_ref, tl_ref, gain_ref,
-             ah_ref, al_ref, rows_ref, sums_ref, squares_ref, u_ref):
+             ah_ref, al_ref, rows_ref, sums_ref, squares_ref, u_ref, gram_ref):
         matrix = filter_matrix(taps_ref, gates, sections, True)
         for index in range(own):
             def load(ref):
@@ -278,18 +299,24 @@
         for index in range(own):
             at = slice(index, index + 1)
             halves = beside(ah_ref[index], True), beside(al_ref[index], True)
-            gram = stacked(dot_nt, halves, halves) * norm[at]
+            gram_ref[index] = stacked(dot_nt, halves, halves) * norm[at]
+        for index in range(own):
+            at = slice(index, index + 1)
+            gram = gram_ref[index]
             parts = split(gram)
             square = stacked(dot, parts, parts)
-            quad = (jnp.where(eye, second[at], 0.0) - third[at] * gram + square) * (norm[at] / first[at])
+            quad = jnp.where(eye, second[at], 0.0) - third[at] * gram + square
+            gram_ref[index] = quad * (norm[at] / first[at])
+        for index in range(own):
             u = u_ref[index * count : (index + 1) * count, :]
             up = jnp.concatenate([u[:, :beams], u[:, beams:]], axis=0)
-            value = stacked(dot, split(quad), split(up))
+            value = stacked(dot, split(gram_ref[index]), split(up))
             high, low = split(value)
             th_ref[index] = beside(high, False)
             tl_ref[index] = beside(low, False)
-            gain = power - jnp.sum(up * value, axis=0, keepdims=True)
-            gain_ref[at, :] = 1.0 / (gain * gain)
+            sums_ref[index : index + 1, :] = jnp.sum(up * value, axis=0, keepdims=True)
+        gain = power - sums_ref[...]
+        gain_ref[...] = 1.0 / (gain * gain)
 
     wide = jax.ShapeDtypeStruct((own, side, 2 * channels), BF16)
     turned = jax.ShapeDtypeStruct((own, side, 2 * beams), BF16)
@@ -305,6 +332,7 @@
             pltpu.VMEM((own, channels), F32),
             pltpu.VMEM((own, channels), F32),
             pltpu.VMEM((own * count, 2 * beams), F32),
+            pltpu.VMEM((own, side, side), F32),
         ],
         compiler_params=pltpu.CompilerParams(vmem_limit_bytes=LIMIT),
         name="weights",
@@ -315,6 +343,7 @@
     sections = len(blocks)
     _, _, gates, own, _ = blocks[0].shape
     size = 4 * gates * own
+    pitch = size + PAD
     count = sections * gates
     side = 2 * count
     channels = 2 * LANES
@@ -327,14 +356,14 @@
          power_ref, total_ref, held, rows_ref, v_ref, cross_ref) = refs[sections:]
         section = lax.axis_index("section")
         for step in range(sections):
-            start = pl.multiple_of(jnp.bitwise_xor(section, step) * size, size)
+            start = pl.multiple_of(jnp.bitwise_xor(section, step) * pitch, 8)
             held[pl.ds(start, size), :] = block_refs[step][...]
         matrix = filter_matrix(taps_ref, gates, sections, False)
         wide = 2 * channels
         for index in range(own):
             def load(half, part):
                 return jnp.concatenate(
-                    [held[pl.ds(((half * 2 + part) * gates + gate) * own + index, sections, stride=size), :]
+                    [held[pl.ds(((half * 2 + part) * gates + gate) * own + index, sections, stride=pitch), :]
                      for gate in range(gates)], axis=0)
 
             data = jnp.concatenate([load(half, part) for part in (0, 1) for half in (0, 1)], axis=1)
@@ -370,7 +399,7 @@
             jax.ShapeDtypeStruct((2 * sections, beams), F32),
         ],
         scratch_shapes=[
-            pltpu.VMEM((sections * size, LANES), F32),
+            pltpu.VMEM((sections * pitch, LANES), F32),
             pltpu.VMEM((own * count, 6 * channels), BF16),
             pltpu.VMEM((own * count, 2 * beams), F32),
             pltpu.VMEM((own, count, side), F32),

time: 78.4 us -> 76.3 us (0.973)
  waiting for transfers between devices: 18.5 us -> 22.1 us
  local copies, waits for them, and re-layouts: 3.17 us -> 0.04 us
  Pallas kernels: 16.1 us -> 13.7 us
    pallas_call x1, Pallas kernels: 10.1 us -> 5.24 us  [weights_kernel(): pl.pallas_call(body, in_specs=[VMEM] * 3 + [SMEM] * 2, out_specs=[VMEM] *...]
    ppermute x14, waiting for transfers between devices: 18.5 us -> 22.1 us  [permuted(): lax.ppermute(block, 'section', [(place, place ^ step) for place in range(...]
    unnamed x12 -> x6, local copies, waits for them, and re-layouts: 3.14 us -> 0.02 us
    pallas_call x2, Pallas kernels: 2.45 us -> 5.19 us  [doppler(): pl.pallas_call(body, in_specs=[HBM] * 3, out_specs=[VMEM] * len(outs), ou...]
  transfers between devices with their start and end apart: 16 -> 16, of which waited for: 5 -> 5; matrix products, arithmetic and copies ran while one was open for 2% -> 2% of each run, Pallas kernels for 15% -> 11%
where the time goes in v1:
time: 76.3 us; the launch traced here: 76.1 us
  starting transfers between devices  23.2 us (30%)
  waiting for transfers between devices  22.1 us (29%)
  blocking collectives  14 us (18%)
  Pallas kernels  13.7 us (18%)
  other arithmetic  2.22 us (3%)
  between operations  0.87 us (1%)
    ppermute x14, starting transfers between devices, permuted(): lax.ppermute(block, 'section', [(place, place ^ step) for place in range(...  23.1 us
    ppermute x14, waiting for transfers between devices, permuted(): lax.ppermute(block, 'section', [(place, place ^ step) for place in range(...  22.1 us
    all_to_all x1, blocking collectives, factored_steps(): totals = lax.all_to_all(total, ('section', 'sub'), 0, 0, tiled=True)  14 us
    pallas_call x1, Pallas kernels, weights_kernel(): pl.pallas_call(body, in_specs=[VMEM] * 3 + [SMEM] * 2, out_specs=[VMEM] *...  5.24 us
    pallas_call x2, Pallas kernels, doppler(): pl.pallas_call(body, in_specs=[HBM] * 3, out_specs=[VMEM] * len(outs), ou...  5.19 us
    pallas_call x1, Pallas kernels, beams_kernel(): pl.pallas_call(body, in_specs=[VMEM] * (sections + 6) + [SMEM], out_specs...  3.08 us
  transfers between devices with their start and end apart: 16, of which 5 were waited for; matrix products, arithmetic and copies ran while one was open for 2% of the time, Pallas kernels for 11%

profile of v1, /device:TPU:0, one launch (start us, length us, event | category | flops | bytes accessed | tf_op | source)
XLA Modules:
  0.0 76.1 jit_solution(13858711364076881088)
XLA Ops:
  0.0 2.6 %shard_map.83 = (f32[2,4,32,128]{3,2,1,0:T(8,128)S(1)}, f32[2,4,32,128]{3,2,1,0:T(8,128)S(1)}, f32[2,4,32,128]{3,2,1,0:T(8,128)S(1)}, f32[2,4,32,128]{3,2,1,0:T(...) custom-call(f32[2,3,512,128]{3,2,1,0:T(8,128)} %bitcast.26, ...), custom_call_target="tpu_custom_call" | custom-call | tf_op jit(solution)/shard_map/pallas_call | solution.py:137
  2.6 0.0 copy-start.2
  2.6 4.0 %collective-permute-start.10 = (f32[2,4,32,128]{3,2,1,0:T(8,128)S(1)}, f32[2,4,32,128]{3,2,1,0:T(8,128)S(1)}, u32[]{:S(2)}, u32[]{:S(2)}) collective-permute-start(f32[2,4,32,128]{3,2,1,0:T(8,128)S(1)} %get-tuple-element.45), channel_id=1, source_target_pairs={{0,6},{2,4},{4,2},{6,0},{8,14},{10,12},{12,10},{14,8},{1,7},{3,5},... | collective-permute-start | bytes 393224 | tf_op jit(solution)/shard_map/ppermute | solution.py:433
  6.7 2.6 %collective-permute-start.11 = (f32[2,4,32,128]{3,2,1,0:T(8,128)S(1)}, f32[2,4,32,128]{3,2,1,0:T(8,128)S(1)}, u32[]{:S(2)}, u32[]{:S(2)}) collective-permute-start(f32[2,4,32,128]{3,2,1,0:T(8,128)S(1)} %get-tuple-element.46), channel_id=1, source_target_pairs={{0,8},{2,10},{4,12},{6,14},{8,0},{10,2},{12,4},{14,6},{1,9},{3,11}... | collective-permute-start | bytes 393224 | tf_op jit(solution)/shard_map/ppermute | solution.py:433
  9.3 0.3 collective-permute-start.12
  9.6 2.5 %collective-permute-start.13 = (f32[2,4,32,128]{3,2,1,0:T(8,128)S(1)}, f32[2,4,32,128]{3,2,1,0:T(8,128)S(1)}, u32[]{:S(2)}, u32[]{:S(2)}) collective-permute-start(f32[2,4,32,128]{3,2,1,0:T(8,128)S(1)} %get-tuple-element.48), channel_id=1, source_target_pairs={{0,12},{2,14},{4,8},{6,10},{8,4},{10,6},{12,0},{14,2},{1,13},{3,15... | collective-permute-start | bytes 393224 | tf_op jit(solution)/shard_map/ppermute | solution.py:433
  12.0 2.3 %collective-permute-start.14 = (f32[2,4,32,128]{3,2,1,0:T(8,128)S(1)}, f32[2,4,32,128]{3,2,1,0:T(8,128)S(1)}, u32[]{:S(2)}, u32[]{:S(2)}) collective-permute-start(f32[2,4,32,128]{3,2,1,0:T(8,128)S(1)} %get-tuple-element.49), channel_id=1, source_target_pairs={{0,14},{2,12},{4,10},{6,8},{8,6},{10,4},{12,2},{14,0},{1,15},{3,13... | collective-permute-start | bytes 393224 | tf_op jit(solution)/shard_map/ppermute | solution.py:433
  14.3 2.6 %shard_map.82 = (f32[8,2,4,16,128]{4,3,2,1,0:T(8,128)S(1)}, f32[8,2,4,16,128]{4,3,2,1,0:T(8,128)S(1)}) custom-call(f32[2,3,512,128]{3,2,1,0:T(8,128)} %bitcast.27, f32[2,128]{1,0:T(2,128)} %bitcast.29, bf16[4,128,256]{2,1,0:T(8,128)(2,1)} %constant.32.clone.table_ref), custom_call_target="tpu_custom_call" | custom-call | tf_op jit(solution)/shard_map/pallas_call | solution.py:137
  16.9 0.0 copy-done.1
  16.9 0.0 collective-permute-done.10.refs_3_
  17.0 0.6 collective-permute-start.8
  17.6 7.3 %collective-permute-done.11.refs_4_ = f32[2,4,32,128]{3,2,1,0:T(8,128)S(1)} collective-permute-done((f32[2,4,32,128]{3,2,1,0:T(8,128)S(1)}, f32[2,4,32,128]{3,2,1,0:T(8,128)S(1)}, u32[]{:S(2)}, u32[]{:S(2)}) %collective-permute-start.11) | collective-permute-done | bytes 131104 | tf_op jit(solution)/shard_map/ppermute | solution.py:433
  24.9 0.0 collective-permute-start.9
  24.9 2.3 %collective-permute-done.12.refs_5_ = f32[2,4,32,128]{3,2,1,0:T(8,128)S(1)} collective-permute-done((f32[2,4,32,128]{3,2,1,0:T(8,128)S(1)}, f32[2,4,32,128]{3,2,1,0:T(8,128)S(1)}, u32[]{:S(2)}, u32[]{:S(2)}) %collective-permute-start.12) | collective-permute-done | bytes 131104 | tf_op jit(solution)/shard_map/ppermute | solution.py:433
  27.2 0.0 collective-permute-start
  27.2 0.0 collective-permute-done.13.refs_6_
  27.2 0.0 collective-permute-done.14.refs_7_
  27.2 0.0 collective-permute-done.8.refs_1_
  27.2 2.7 %collective-permute-done.9.refs_2_ = f32[2,4,32,128]{3,2,1,0:T(8,128)S(1)} collective-permute-done((f32[2,4,32,128]{3,2,1,0:T(8,128)S(1)}, f32[2,4,32,128]{3,2,1,0:T(8,128)S(1)}, u32[]{:S(2)}, u32[]{:S(2)}) %collective-permute-start.9) | collective-permute-done | bytes 131104 | tf_op jit(solution)/shard_map/ppermute | solution.py:433
  29.9 0.1 gather_sub.1
  30.0 0.1 collective-permute-start.15
  30.1 0.0 copy-done.2
  30.1 1.0 %fusion.4 = (f32[256,256]{1,0:T(8,128)S(1)}, f32[256,256]{1,0:T(8,128)S(1)}, f32[256,256]{1,0:T(8,128)S(1)}) fusion(f32[256]{0:T(256)S(1)} %get-tuple-element.67, f32[256]{0:T(256)S(1)} %multiply_add_fusion.2, f32[256]{0:T(256)S(1)} %get-tuple-element.66), kind=kLoop, calls=%fused_computation.10 | loop fusion | flops 196608 | bytes 789504 | tf_op jit(solution)/shard_map/neg | solution.py:424
  31.1 0.0 collective-permute-done.other_ref
  31.1 0.1 pair_up.1
  31.2 0.2 collective-permute-start.1
  31.4 4.4 %collective-permute-start.2 = (f32[2,2,4,16,128]{4,3,2,1,0:T(8,128)S(1)}, f32[2,2,4,16,128]{4,3,2,1,0:T(8,128)S(1)}, u32[]{:S(2)}, u32[]{:S(2)}) collective-permute-start(f32[2,2,4,16,128]{4,3,2,1,0:T(8,128)S(1)} %get-tuple-element.36), channel_id=1, source_target_pairs={{0,4},{2,6},{4,0},{6,2},{8,12},{10,14},{12,8},{14,10},{1,5},{3,7},... | collective-permute-start | bytes 393224 | tf_op jit(solution)/shard_map/ppermute | solution.py:433
  35.7 0.1 reduce-precision_convert_fusion
  35.9 0.0 copy-start
  35.9 0.1 collective-permute-start.3
  36.0 2.9 %collective-permute-start.4 = (f32[2,2,4,16,128]{4,3,2,1,0:T(8,128)S(1)}, f32[2,2,4,16,128]{4,3,2,1,0:T(8,128)S(1)}, u32[]{:S(2)}, u32[]{:S(2)}) collective-permute-start(f32[2,2,4,16,128]{4,3,2,1,0:T(8,128)S(1)} %get-tuple-element.38), channel_id=1, source_target_pairs={{0,8},{2,10},{4,12},{6,14},{8,0},{10,2},{12,4},{14,6},{1,9},{3,11}... | collective-permute-start | bytes 393224 | tf_op jit(solution)/shard_map/ppermute | solution.py:433
  38.9 0.0 collective-permute-done.15
  38.9 0.9 %collective-permute-start.5 = (f32[2,2,4,16,128]{4,3,2,1,0:T(8,128)S(1)}, f32[2,2,4,16,128]{4,3,2,1,0:T(8,128)S(1)}, u32[]{:S(2)}, u32[]{:S(2)}) collective-permute-start(f32[2,2,4,16,128]{4,3,2,1,0:T(8,128)S(1)} %get-tuple-element.39), channel_id=1, source_target_pairs={{0,10},{2,8},{4,14},{6,12},{8,2},{10,0},{12,6},{14,4},{1,11},{3,9}... | collective-permute-start | bytes 393224 | tf_op jit(solution)/shard_map/ppermute | solution.py:433
  39.8 0.0 collective-permute-done.1
  39.8 2.4 %collective-permute-start.6 = (f32[2,2,4,16,128]{4,3,2,1,0:T(8,128)S(1)}, f32[2,2,4,16,128]{4,3,2,1,0:T(8,128)S(1)}, u32[]{:S(2)}, u32[]{:S(2)}) collective-permute-start(f32[2,2,4,16,128]{4,3,2,1,0:T(8,128)S(1)} %get-tuple-element.40), channel_id=1, source_target_pairs={{0,12},{2,14},{4,8},{6,10},{8,4},{10,6},{12,0},{14,2},{1,13},{3,15... | collective-permute-start | bytes 393224 | tf_op jit(solution)/shard_map/ppermute | solution.py:433
  42.2 2.0 %collective-permute-done.2 = f32[2,2,4,16,128]{4,3,2,1,0:T(8,128)S(1)} collective-permute-done((f32[2,2,4,16,128]{4,3,2,1,0:T(8,128)S(1)}, f32[2,2,4,16,128]{4,3,2,1,0:T(8,128)S(1)}, u32[]{:S(2)}, u32[]{:S(2)}) %collective-permute-start.2) | collective-permute-done | bytes 131104 | tf_op jit(solution)/shard_map/ppermute | solution.py:433
  44.2 0.0 collective-permute-start.7
  44.2 0.1 pad_maximum_fusion.steer_ref.refs_13_
  45.0 0.0 copy-done
  45.0 5.2 %weights.1 = (bf16[16,64,512]{2,1,0:T(8,128)(2,1)S(1)}, bf16[16,64,512]{2,1,0:T(8,128)(2,1)S(1)}, bf16[16,64,512]{2,1,0:T(8,128)(2,1)S(1)}, bf16[16,64,512]{2,1,0:T(8,128)(2,1)S(1)}, f32[16,256]{1,0:T(8,128)S(1)}) custom-call(f32[1024,128]{1,0:T(8,128)S(1)} %bitcast.15, f32[1024,128]{1,0:T(8,128)S(1)} %bitcast.16, ...), custom_call_target="tpu_custom_call" | custom-call | tf_op jit(solution)/shard_map/weights/pallas_call | solution.py:323
  50.2 0.0 collective-permute-done.3
  50.2 0.0 collective-permute-done.4
  50.2 7.8 %collective-permute-done.5 = f32[2,2,4,16,128]{4,3,2,1,0:T(8,128)S(1)} collective-permute-done((f32[2,2,4,16,128]{4,3,2,1,0:T(8,128)S(1)}, f32[2,2,4,16,128]{4,3,2,1,0:T(8,128)S(1)}, u32[]{:S(2)}, u32[]{:S(2)}) %collective-permute-start.5) | collective-permute-done | bytes 131104 | tf_op jit(solution)/shard_map/ppermute | solution.py:433
  58.0 0.0 collective-permute-done.6
  58.1 0.0 collective-permute-done.7
  58.1 3.1 %beams.1 = (f32[16,32,256]{2,1,0:T(8,128)S(1)}, f32[16,256]{1,0:T(8,128)S(1)}) custom-call(f32[256,128]{1,0:T(8,128)S(1)} %bitcast.17, f32[256,128]{1,0:T(8,128)S(1)} %bitcast.18, f32[256,128]{1,0:T(8,128)S(1)} %bitcast.19, f32[256,128]{1,0:T(8,128)S(1)} %bitcast.20, f32[256,128]{1,0:T(8,128)S(1)} %bitcast.21, f32[256,128]{1,0:T(8,128)S(1)} %bitcast.22, ...), custom_call_target="tpu_custom_call" | custom-call | tf_op jit(solution)/shard_map/beams/pallas_call | solution.py:393
  61.2 14.0 %all_to_all.9 = f32[16,1,256]{2,1,0:T(1,128)S(1)} all-to-all(f32[16,1,256]{2,1,0:T(1,128)S(1)} %copy.9), channel_id=1, replica_groups=mesh['groups'=2,'section'=8,'sub'=2] {'section','sub'}, dimensions={0} | all-to-all | bytes 32768 | tf_op jit(solution)/shard_map/all_to_all | solution.py:465
  75.2 0.9 %divide_bitcast_fusion = f32[1,16,32,256]{3,2,1,0:T(8,128)} fusion(f32[16,32,256]{2,1,0:T(8,128)S(1)} %get-tuple-element.57, f32[256]{0:T(256)S(1)} %multiply_add_fusion.1), kind=kLoop, calls=%fused_computation.6 | loop fusion | flops 131072 | bytes 1049600 | tf_op jit(solution)/shard_map/broadcast_in_dim | solution.py:467
  (7 shorter events, 0.1 us)
Async XLA Ops:
  0.0 16.9 %copy-start.1 = (f32[256]{0:T(256)S(1)}, f32[256]{0:T(256)}, u32[]{:S(2)}) copy-start(f32[256]{0:T(256)} %param.11) | copy-start | bytes 3076
  2.6 27.4 %copy-start.2 = (s32[256]{0:T(256)S(1)}, s32[256]{0:T(256)}, u32[]{:S(2)}) copy-start(s32[256]{0:T(256)} %param.13) | copy-start | bytes 3076
  2.6 14.3 %collective-permute-start.10 = (f32[2,4,32,128]{3,2,1,0:T(8,128)S(1)}, f32[2,4,32,128]{3,2,1,0:T(8,128)S(1)}, u32[]{:S(2)}, u32[]{:S(2)}) collective-permute-start(f32[2,4,32,128]{3,2,1,0:T(8,128)S(1)} %get-tuple-element.45), channel_id=1, source_target_pairs={{0,6},{2,4},{4,2},{6,0},{8,14},{10,12},{12,10},{14,8},{1,7},{3,5},... | collective-permute-start | bytes 393224 | tf_op jit(solution)/shard_map/ppermute | solution.py:433
  6.7 18.2 %collective-permute-start.11 = (f32[2,4,32,128]{3,2,1,0:T(8,128)S(1)}, f32[2,4,32,128]{3,2,1,0:T(8,128)S(1)}, u32[]{:S(2)}, u32[]{:S(2)}) collective-permute-start(f32[2,4,32,128]{3,2,1,0:T(8,128)S(1)} %get-tuple-element.46), channel_id=1, source_target_pairs={{0,8},{2,10},{4,12},{6,14},{8,0},{10,2},{12,4},{14,6},{1,9},{3,11}... | collective-permute-start | bytes 393224 | tf_op jit(solution)/shard_map/ppermute | solution.py:433
  9.3 17.9 %collective-permute-start.12 = (f32[2,4,32,128]{3,2,1,0:T(8,128)S(1)}, f32[2,4,32,128]{3,2,1,0:T(8,128)S(1)}, u32[]{:S(2)}, u32[]{:S(2)}) collective-permute-start(f32[2,4,32,128]{3,2,1,0:T(8,128)S(1)} %get-tuple-element.47), channel_id=1, source_target_pairs={{0,10},{2,8},{4,14},{6,12},{8,2},{10,0},{12,6},{14,4},{1,11},{3,9}... | collective-permute-start | bytes 393224 | tf_op jit(solution)/shard_map/ppermute | solution.py:433
  9.6 17.6 %collective-permute-start.13 = (f32[2,4,32,128]{3,2,1,0:T(8,128)S(1)}, f32[2,4,32,128]{3,2,1,0:T(8,128)S(1)}, u32[]{:S(2)}, u32[]{:S(2)}) collective-permute-start(f32[2,4,32,128]{3,2,1,0:T(8,128)S(1)} %get-tuple-element.48), channel_id=1, source_target_pairs={{0,12},{2,14},{4,8},{6,10},{8,4},{10,6},{12,0},{14,2},{1,13},{3,15... | collective-permute-start | bytes 393224 | tf_op jit(solution)/shard_map/ppermute | solution.py:433
  12.0 15.1 %collective-permute-start.14 = (f32[2,4,32,128]{3,2,1,0:T(8,128)S(1)}, f32[2,4,32,128]{3,2,1,0:T(8,128)S(1)}, u32[]{:S(2)}, u32[]{:S(2)}) collective-permute-start(f32[2,4,32,128]{3,2,1,0:T(8,128)S(1)} %get-tuple-element.49), channel_id=1, source_target_pairs={{0,14},{2,12},{4,10},{6,8},{8,6},{10,4},{12,2},{14,0},{1,15},{3,13... | collective-permute-start | bytes 393224 | tf_op jit(solution)/shard_map/ppermute | solution.py:433
  17.0 10.2 %collective-permute-start.8 = (f32[2,4,32,128]{3,2,1,0:T(8,128)S(1)}, f32[2,4,32,128]{3,2,1,0:T(8,128)S(1)}, u32[]{:S(2)}, u32[]{:S(2)}) collective-permute-start(f32[2,4,32,128]{3,2,1,0:T(8,128)S(1)} %get-tuple-element.43), channel_id=1, source_target_pairs={{0,2},{2,0},{4,6},{6,4},{8,10},{10,8},{12,14},{14,12},{1,3},{3,1},... | collective-permute-start | bytes 393224 | tf_op jit(solution)/shard_map/ppermute | solution.py:433
  24.9 5.0 %collective-permute-start.9 = (f32[2,4,32,128]{3,2,1,0:T(8,128)S(1)}, f32[2,4,32,128]{3,2,1,0:T(8,128)S(1)}, u32[]{:S(2)}, u32[]{:S(2)}) collective-permute-start(f32[2,4,32,128]{3,2,1,0:T(8,128)S(1)} %get-tuple-element.44), channel_id=1, source_target_pairs={{0,4},{2,6},{4,0},{6,2},{8,12},{10,14},{12,8},{14,10},{1,5},{3,7},... | collective-permute-start | bytes 393224 | tf_op jit(solution)/shard_map/ppermute | solution.py:433
  27.2 3.9 %collective-permute-start = (f32[8,2,4,16,128]{4,3,2,1,0:T(8,128)S(1)}, f32[8,2,4,16,128]{4,3,2,1,0:T(8,128)S(1)}, u32[]{:S(2)}, u32[]{:S(2)}) collective-permute-start(f32[8,2,4,16,128]{4,3,2,1,0:T(8,128)S(1)} %get-tuple-element.33), channel_id=1, source_target_pairs={{0,1},{1,0},{2,3},{3,2},{4,5},{5,4},{6,7},{7,6},{8,9},{9,8},{10,11... | collective-permute-start | bytes 1572872 | tf_op jit(solution)/shard_map/ppermute | solution.py:437
  30.0 8.9 %collective-permute-start.15 = (f32[8,2,4,16,128]{4,3,2,1,0:T(8,128)S(1)}, f32[8,2,4,16,128]{4,3,2,1,0:T(8,128)S(1)}, u32[]{:S(2)}, u32[]{:S(2)}) collective-permute-start(f32[8,2,4,16,128]{4,3,2,1,0:T(8,128)S(1)} %get-tuple-element.51), channel_id=1, source_target_pairs={{0,1},{1,0},{2,3},{3,2},{4,5},{5,4},{6,7},{7,6},{8,9},{9,8},{10,11... | collective-permute-start | bytes 1572872 | tf_op jit(solution)/shard_map/ppermute | solution.py:437
  31.2 8.6 %collective-permute-start.1 = (f32[2,2,4,16,128]{4,3,2,1,0:T(8,128)S(1)}, f32[2,2,4,16,128]{4,3,2,1,0:T(8,128)S(1)}, u32[]{:S(2)}, u32[]{:S(2)}) collective-permute-start(f32[2,2,4,16,128]{4,3,2,1,0:T(8,128)S(1)} %get-tuple-element.35), channel_id=1, source_target_pairs={{0,2},{2,0},{4,6},{6,4},{8,10},{10,8},{12,14},{14,12},{1,3},{3,1},... | collective-permute-start | bytes 393224 | tf_op jit(solution)/shard_map/ppermute | solution.py:433
  31.4 12.8 %collective-permute-start.2 = (f32[2,2,4,16,128]{4,3,2,1,0:T(8,128)S(1)}, f32[2,2,4,16,128]{4,3,2,1,0:T(8,128)S(1)}, u32[]{:S(2)}, u32[]{:S(2)}) collective-permute-start(f32[2,2,4,16,128]{4,3,2,1,0:T(8,128)S(1)} %get-tuple-element.36), channel_id=1, source_target_pairs={{0,4},{2,6},{4,0},{6,2},{8,12},{10,14},{12,8},{14,10},{1,5},{3,7},... | collective-permute-start | bytes 393224 | tf_op jit(solution)/shard_map/ppermute | solution.py:433
  35.9 9.1 %copy-start = (f32[2,5]{1,0:T(2,128)S(1)}, f32[2,5]{1,0:T(2,128)}, u32[]{:S(2)}) copy-start(f32[2,5]{1,0:T(2,128)} %refs_14_.1) | copy-start | bytes 124
  35.9 14.3 %collective-permute-start.3 = (f32[2,2,4,16,128]{4,3,2,1,0:T(8,128)S(1)}, f32[2,2,4,16,128]{4,3,2,1,0:T(8,128)S(1)}, u32[]{:S(2)}, u32[]{:S(2)}) collective-permute-start(f32[2,2,4,16,128]{4,3,2,1,0:T(8,128)S(1)} %get-tuple-element.37), channel_id=1, source_target_pairs={{0,6},{2,4},{4,2},{6,0},{8,14},{10,12},{12,10},{14,8},{1,7},{3,5},... | collective-permute-start | bytes 393224 | tf_op jit(solution)/shard_map/ppermute | solution.py:433
  36.0 14.2 %collective-permute-start.4 = (f32[2,2,4,16,128]{4,3,2,1,0:T(8,128)S(1)}, f32[2,2,4,16,128]{4,3,2,1,0:T(8,128)S(1)}, u32[]{:S(2)}, u32[]{:S(2)}) collective-permute-start(f32[2,2,4,16,128]{4,3,2,1,0:T(8,128)S(1)} %get-tuple-element.38), channel_id=1, source_target_pairs={{0,8},{2,10},{4,12},{6,14},{8,0},{10,2},{12,4},{14,6},{1,9},{3,11}... | collective-permute-start | bytes 393224 | tf_op jit(solution)/shard_map/ppermute | solution.py:433
  38.9 19.1 %collective-permute-start.5 = (f32[2,2,4,16,128]{4,3,2,1,0:T(8,128)S(1)}, f32[2,2,4,16,128]{4,3,2,1,0:T(8,128)S(1)}, u32[]{:S(2)}, u32[]{:S(2)}) collective-permute-start(f32[2,2,4,16,128]{4,3,2,1,0:T(8,128)S(1)} %get-tuple-element.39), channel_id=1, source_target_pairs={{0,10},{2,8},{4,14},{6,12},{8,2},{10,0},{12,6},{14,4},{1,11},{3,9}... | collective-permute-start | bytes 393224 | tf_op jit(solution)/shard_map/ppermute | solution.py:433
  39.8 18.2 %collective-permute-start.6 = (f32[2,2,4,16,128]{4,3,2,1,0:T(8,128)S(1)}, f32[2,2,4,16,128]{4,3,2,1,0:T(8,128)S(1)}, u32[]{:S(2)}, u32[]{:S(2)}) collective-permute-start(f32[2,2,4,16,128]{4,3,2,1,0:T(8,128)S(1)} %get-tuple-element.40), channel_id=1, source_target_pairs={{0,12},{2,14},{4,8},{6,10},{8,4},{10,6},{12,0},{14,2},{1,13},{3,15... | collective-permute-start | bytes 393224 | tf_op jit(solution)/shard_map/ppermute | solution.py:433
  44.2 13.9 %collective-permute-start.7 = (f32[2,2,4,16,128]{4,3,2,1,0:T(8,128)S(1)}, f32[2,2,4,16,128]{4,3,2,1,0:T(8,128)S(1)}, u32[]{:S(2)}, u32[]{:S(2)}) collective-permute-start(f32[2,2,4,16,128]{4,3,2,1,0:T(8,128)S(1)} %get-tuple-element.41), channel_id=1, source_target_pairs={{0,14},{2,12},{4,10},{6,8},{8,6},{10,4},{12,2},{14,0},{1,15},{3,13... | collective-permute-start | bytes 393224 | tf_op jit(solution)/shard_map/ppermute | solution.py:433

commit v2 on v1

--- a/solution.py
+++ b/solution.py
@@ -73,25 +73,29 @@
     for segment in (0, 1):
         row = taper_ref[segment : segment + 1, :]
         tapers[segment * hop : (segment + 1) * hop, :] = jnp.broadcast_to(row, (hop, hop)).T
-    for gate in range(gates):
+    for group in range(0, gates, 2):
+        members = range(group, min(group + 2, gates))
         for parity in (0, 1):
             rows = []
             for part in (0, 1):
                 for segment in (0, 1):
-                    at = pl.ds(parity * gates + gate, hop // 2, stride=2 * gates)
-                    block = view_ref[part, segment, at, :]
                     taper = tapers[pl.ds(segment * hop + parity, hop // 2, stride=2), :]
-                    rows.append(block * taper)
+                    blocks = []
+                    for gate in members:
+                        at = pl.ds(parity * gates + gate, hop // 2, stride=2 * gates)
+                        blocks.append(view_ref[part, segment, at, :] * taper)
+                    rows.append(jnp.concatenate(blocks, axis=1))
             data = split(jnp.concatenate(rows, axis=0))
             table = full_table(table_ref[2 * parity]), full_table(table_ref[2 * parity + 1])
             value = triple(dot, table, data)
             if parity == 0:
                 even = value
-            else:
-                for part in (0, 1):
-                    own = slice(part * half, (part + 1) * half)
-                    result[part, gate, :half] = even[own] + value[own]
-                    result[part, gate, half:] = even[own] - value[own]
+        for place, gate in enumerate(members):
+            lanes = slice(place * LANES, (place + 1) * LANES)
+            for part in (0, 1):
+                own = slice(part * half, (part + 1) * half)
+                result[part, gate, :half] = even[own, lanes] + value[own, lanes]
+                result[part, gate, half:] = even[own, lanes] - value[own, lanes]
 
 
 def doppler(view, taper, sections, interval, split_sub):
@@ -359,6 +363,7 @@
             start = pl.multiple_of(jnp.bitwise_xor(section, step) * pitch, 8)
             held[pl.ds(start, size), :] = block_refs[step][...]
         matrix = filter_matrix(taps_ref, gates, sections, False)
+        matrix = jnp.concatenate([matrix[0], matrix[1], matrix[0]], axis=1)
         wide = 2 * channels
         for index in range(own):
             def load(half, part):
@@ -384,7 +389,8 @@
         for index in range(own):
             v = v_ref[index * count : (index + 1) * count, :]
             up = jnp.concatenate([v[:, :beams], v[:, beams:]], axis=0)
-            out = stacked(dot, matrix, split(up))
+            high, low = split(up)
+            out = dot(matrix, jnp.concatenate([high, high, low], axis=0))
             power = (out[:count] * out[:count] + out[count:] * out[count:]) * gain_ref[index : index + 1, :]
             total = total + jnp.sum(power, axis=0, keepdims=True)
             power_ref[index] = power
@@ -437,10 +443,15 @@
     return lax.ppermute(block, "sub", [(0, 1), (1, 0)])
 
 
+def hop_order(sections):
+    near, far = list(range(1, sections // 2)), list(range(sections // 2, sections))
+    return far[::-1] + near[::-1], near[::-1] + far[::-1]
+
+
 def factored_steps(echoes, range_taps, pulse_taper, channel_phase, loading, beam_index):
     parts, pulses, gates, lanes = echoes.shape
     sections = lax.axis_size("section")
-    order = sorted(range(1, sections), reverse=True)
+    order = hop_order(sections)[0]
     view = echoes.reshape(parts, pulses // HOP, HOP * gates, lanes)
     taper = pulse_taper.reshape(2, HOP)
 

time: 76.3 us -> 75.8 us (level)
  Pallas kernels: 13.7 us -> 12.8 us
    pallas_call x2, Pallas kernels: 5.19 us -> 4.37 us  [doppler(): pl.pallas_call(body, in_specs=[HBM] * 3, out_specs=[VMEM] * len(outs), ou...]
  transfers between devices with their start and end apart: 16 -> 16, of which waited for: 5 -> 5; matrix products, arithmetic and copies ran while one was open for 2% -> 2% of each run, Pallas kernels for 11% -> 10%
where the time goes in v2:
time: 75.8 us; the launch traced here: 75.6 us
  starting transfers between devices  23.2 us (31%)
  waiting for transfers between devices  22.5 us (30%)
  blocking collectives  14 us (18%)
  Pallas kernels  12.8 us (17%)
  other arithmetic  2.22 us (3%)
  between operations  0.86 us (1%)
    ppermute x14, starting transfers between devices, permuted(): lax.ppermute(block, 'section', [(place, place ^ step) for place in range(...  23.1 us
    ppermute x14, waiting for transfers between devices, permuted(): lax.ppermute(block, 'section', [(place, place ^ step) for place in range(...  22.5 us
    all_to_all x1, blocking collectives, factored_steps(): totals = lax.all_to_all(total, ('section', 'sub'), 0, 0, tiled=True)  14 us
    pallas_call x1, Pallas kernels, weights_kernel(): pl.pallas_call(body, in_specs=[VMEM] * 3 + [SMEM] * 2, out_specs=[VMEM] *...  5.24 us
    pallas_call x2, Pallas kernels, doppler(): pl.pallas_call(body, in_specs=[HBM] * 3, out_specs=[VMEM] * len(outs), ou...  4.37 us
    pallas_call x1, Pallas kernels, beams_kernel(): pl.pallas_call(body, in_specs=[VMEM] * (sections + 6) + [SMEM], out_specs...  2.98 us
  transfers between devices with their start and end apart: 16, of which 5 were waited for; matrix products, arithmetic and copies ran while one was open for 2% of the time, Pallas kernels for 10%

profile of v2, /device:TPU:0, one launch (start us, length us, event | category | flops | bytes accessed | tf_op | source)
XLA Modules:
  0.0 75.6 jit_solution(4764504536537048096)
XLA Ops:
  0.0 2.2 %shard_map.83 = (f32[2,4,32,128]{3,2,1,0:T(8,128)S(1)}, f32[2,4,32,128]{3,2,1,0:T(8,128)S(1)}, f32[2,4,32,128]{3,2,1,0:T(8,128)S(1)}, f32[2,4,32,128]{3,2,1,0:T(...) custom-call(f32[2,3,512,128]{3,2,1,0:T(8,128)} %bitcast.26, ...), custom_call_target="tpu_custom_call" | custom-call | tf_op jit(solution)/shard_map/pallas_call | solution.py:141
  2.2 0.0 copy-start.2
  2.2 4.0 %collective-permute-start.10 = (f32[2,4,32,128]{3,2,1,0:T(8,128)S(1)}, f32[2,4,32,128]{3,2,1,0:T(8,128)S(1)}, u32[]{:S(2)}, u32[]{:S(2)}) collective-permute-start(f32[2,4,32,128]{3,2,1,0:T(8,128)S(1)} %get-tuple-element.45), channel_id=1, source_target_pairs={{0,6},{2,4},{4,2},{6,0},{8,14},{10,12},{12,10},{14,8},{1,7},{3,5},... | collective-permute-start | bytes 393224 | tf_op jit(solution)/shard_map/ppermute | solution.py:439
  6.3 2.6 %collective-permute-start.11 = (f32[2,4,32,128]{3,2,1,0:T(8,128)S(1)}, f32[2,4,32,128]{3,2,1,0:T(8,128)S(1)}, u32[]{:S(2)}, u32[]{:S(2)}) collective-permute-start(f32[2,4,32,128]{3,2,1,0:T(8,128)S(1)} %get-tuple-element.46), channel_id=1, source_target_pairs={{0,8},{2,10},{4,12},{6,14},{8,0},{10,2},{12,4},{14,6},{1,9},{3,11}... | collective-permute-start | bytes 393224 | tf_op jit(solution)/shard_map/ppermute | solution.py:439
  8.9 0.3 collective-permute-start.12
  9.2 2.5 %collective-permute-start.13 = (f32[2,4,32,128]{3,2,1,0:T(8,128)S(1)}, f32[2,4,32,128]{3,2,1,0:T(8,128)S(1)}, u32[]{:S(2)}, u32[]{:S(2)}) collective-permute-start(f32[2,4,32,128]{3,2,1,0:T(8,128)S(1)} %get-tuple-element.48), channel_id=1, source_target_pairs={{0,12},{2,14},{4,8},{6,10},{8,4},{10,6},{12,0},{14,2},{1,13},{3,15... | collective-permute-start | bytes 393224 | tf_op jit(solution)/shard_map/ppermute | solution.py:439
  11.6 2.3 %collective-permute-start.14 = (f32[2,4,32,128]{3,2,1,0:T(8,128)S(1)}, f32[2,4,32,128]{3,2,1,0:T(8,128)S(1)}, u32[]{:S(2)}, u32[]{:S(2)}) collective-permute-start(f32[2,4,32,128]{3,2,1,0:T(8,128)S(1)} %get-tuple-element.49), channel_id=1, source_target_pairs={{0,14},{2,12},{4,10},{6,8},{8,6},{10,4},{12,2},{14,0},{1,15},{3,13... | collective-permute-start | bytes 393224 | tf_op jit(solution)/shard_map/ppermute | solution.py:439
  13.9 2.2 %shard_map.82 = (f32[8,2,4,16,128]{4,3,2,1,0:T(8,128)S(1)}, f32[8,2,4,16,128]{4,3,2,1,0:T(8,128)S(1)}) custom-call(f32[2,3,512,128]{3,2,1,0:T(8,128)} %bitcast.27, f32[2,128]{1,0:T(2,128)} %bitcast.29, bf16[4,128,256]{2,1,0:T(8,128)(2,1)} %constant.32.clone.table_ref), custom_call_target="tpu_custom_call" | custom-call | tf_op jit(solution)/shard_map/pallas_call | solution.py:141
  16.1 0.0 copy-done.1
  16.1 0.0 collective-permute-done.10.refs_3_
  16.1 0.6 collective-permute-start.8
  16.7 7.8 %collective-permute-done.11.refs_4_ = f32[2,4,32,128]{3,2,1,0:T(8,128)S(1)} collective-permute-done((f32[2,4,32,128]{3,2,1,0:T(8,128)S(1)}, f32[2,4,32,128]{3,2,1,0:T(8,128)S(1)}, u32[]{:S(2)}, u32[]{:S(2)}) %collective-permute-start.11) | collective-permute-done | bytes 131104 | tf_op jit(solution)/shard_map/ppermute | solution.py:439
  24.5 0.0 collective-permute-start.9
  24.5 2.3 %collective-permute-done.12.refs_5_ = f32[2,4,32,128]{3,2,1,0:T(8,128)S(1)} collective-permute-done((f32[2,4,32,128]{3,2,1,0:T(8,128)S(1)}, f32[2,4,32,128]{3,2,1,0:T(8,128)S(1)}, u32[]{:S(2)}, u32[]{:S(2)}) %collective-permute-start.12) | collective-permute-done | bytes 131104 | tf_op jit(solution)/shard_map/ppermute | solution.py:439
  26.8 0.0 collective-permute-start
  26.8 0.0 collective-permute-done.13.refs_6_
  26.8 0.0 collective-permute-done.14.refs_7_
  26.8 0.0 collective-permute-done.8.refs_1_
  26.8 2.6 %collective-permute-done.9.refs_2_ = f32[2,4,32,128]{3,2,1,0:T(8,128)S(1)} collective-permute-done((f32[2,4,32,128]{3,2,1,0:T(8,128)S(1)}, f32[2,4,32,128]{3,2,1,0:T(8,128)S(1)}, u32[]{:S(2)}, u32[]{:S(2)}) %collective-permute-start.9) | collective-permute-done | bytes 131104 | tf_op jit(solution)/shard_map/ppermute | solution.py:439
  29.5 0.1 gather_sub.1
  29.6 0.1 collective-permute-start.15
  29.6 0.0 copy-done.2
  29.7 1.0 %fusion.4 = (f32[256,256]{1,0:T(8,128)S(1)}, f32[256,256]{1,0:T(8,128)S(1)}, f32[256,256]{1,0:T(8,128)S(1)}) fusion(f32[256]{0:T(256)S(1)} %get-tuple-element.67, f32[256]{0:T(256)S(1)} %multiply_add_fusion.2, f32[256]{0:T(256)S(1)} %get-tuple-element.66), kind=kLoop, calls=%fused_computation.10 | loop fusion | flops 196608 | bytes 789504 | tf_op jit(solution)/shard_map/neg | solution.py:430
  30.7 0.0 collective-permute-done.other_ref
  30.7 0.1 pair_up.1
  30.8 0.1 collective-permute-start.1
  30.9 4.4 %collective-permute-start.2 = (f32[2,2,4,16,128]{4,3,2,1,0:T(8,128)S(1)}, f32[2,2,4,16,128]{4,3,2,1,0:T(8,128)S(1)}, u32[]{:S(2)}, u32[]{:S(2)}) collective-permute-start(f32[2,2,4,16,128]{4,3,2,1,0:T(8,128)S(1)} %get-tuple-element.36), channel_id=1, source_target_pairs={{0,4},{2,6},{4,0},{6,2},{8,12},{10,14},{12,8},{14,10},{1,5},{3,7},... | collective-permute-start | bytes 393224 | tf_op jit(solution)/shard_map/ppermute | solution.py:439
  35.3 0.1 reduce-precision_convert_fusion
  35.5 0.0 copy-start
  35.5 0.1 collective-permute-start.3
  35.6 2.9 %collective-permute-start.4 = (f32[2,2,4,16,128]{4,3,2,1,0:T(8,128)S(1)}, f32[2,2,4,16,128]{4,3,2,1,0:T(8,128)S(1)}, u32[]{:S(2)}, u32[]{:S(2)}) collective-permute-start(f32[2,2,4,16,128]{4,3,2,1,0:T(8,128)S(1)} %get-tuple-element.38), channel_id=1, source_target_pairs={{0,8},{2,10},{4,12},{6,14},{8,0},{10,2},{12,4},{14,6},{1,9},{3,11}... | collective-permute-start | bytes 393224 | tf_op jit(solution)/shard_map/ppermute | solution.py:439
  38.5 0.0 collective-permute-done.15
  38.5 0.9 %collective-permute-start.5 = (f32[2,2,4,16,128]{4,3,2,1,0:T(8,128)S(1)}, f32[2,2,4,16,128]{4,3,2,1,0:T(8,128)S(1)}, u32[]{:S(2)}, u32[]{:S(2)}) collective-permute-start(f32[2,2,4,16,128]{4,3,2,1,0:T(8,128)S(1)} %get-tuple-element.39), channel_id=1, source_target_pairs={{0,10},{2,8},{4,14},{6,12},{8,2},{10,0},{12,6},{14,4},{1,11},{3,9}... | collective-permute-start | bytes 393224 | tf_op jit(solution)/shard_map/ppermute | solution.py:439
  39.4 0.0 collective-permute-done.1
  39.4 2.4 %collective-permute-start.6 = (f32[2,2,4,16,128]{4,3,2,1,0:T(8,128)S(1)}, f32[2,2,4,16,128]{4,3,2,1,0:T(8,128)S(1)}, u32[]{:S(2)}, u32[]{:S(2)}) collective-permute-start(f32[2,2,4,16,128]{4,3,2,1,0:T(8,128)S(1)} %get-tuple-element.40), channel_id=1, source_target_pairs={{0,12},{2,14},{4,8},{6,10},{8,4},{10,6},{12,0},{14,2},{1,13},{3,15... | collective-permute-start | bytes 393224 | tf_op jit(solution)/shard_map/ppermute | solution.py:439
  41.8 1.9 %collective-permute-done.2 = f32[2,2,4,16,128]{4,3,2,1,0:T(8,128)S(1)} collective-permute-done((f32[2,2,4,16,128]{4,3,2,1,0:T(8,128)S(1)}, f32[2,2,4,16,128]{4,3,2,1,0:T(8,128)S(1)}, u32[]{:S(2)}, u32[]{:S(2)}) %collective-permute-start.2) | collective-permute-done | bytes 131104 | tf_op jit(solution)/shard_map/ppermute | solution.py:439
  43.7 0.0 collective-permute-start.7
  43.7 0.1 pad_maximum_fusion.steer_ref.refs_13_
  44.5 0.0 copy-done
  44.5 5.2 %weights.1 = (bf16[16,64,512]{2,1,0:T(8,128)(2,1)S(1)}, bf16[16,64,512]{2,1,0:T(8,128)(2,1)S(1)}, bf16[16,64,512]{2,1,0:T(8,128)(2,1)S(1)}, bf16[16,64,512]{2,1,0:T(8,128)(2,1)S(1)}, f32[16,256]{1,0:T(8,128)S(1)}) custom-call(f32[1024,128]{1,0:T(8,128)S(1)} %bitcast.15, f32[1024,128]{1,0:T(8,128)S(1)} %bitcast.16, ...), custom_call_target="tpu_custom_call" | custom-call | tf_op jit(solution)/shard_map/weights/pallas_call | solution.py:327
  49.8 0.0 collective-permute-done.3
  49.8 0.0 collective-permute-done.4
  49.8 7.9 %collective-permute-done.5 = f32[2,2,4,16,128]{4,3,2,1,0:T(8,128)S(1)} collective-permute-done((f32[2,2,4,16,128]{4,3,2,1,0:T(8,128)S(1)}, f32[2,2,4,16,128]{4,3,2,1,0:T(8,128)S(1)}, u32[]{:S(2)}, u32[]{:S(2)}) %collective-permute-start.5) | collective-permute-done | bytes 131104 | tf_op jit(solution)/shard_map/ppermute | solution.py:439
  57.6 0.0 collective-permute-done.6
  57.6 0.0 collective-permute-done.7
  57.7 3.0 %beams.1 = (f32[16,32,256]{2,1,0:T(8,128)S(1)}, f32[16,256]{1,0:T(8,128)S(1)}) custom-call(f32[256,128]{1,0:T(8,128)S(1)} %bitcast.17, f32[256,128]{1,0:T(8,128)S(1)} %bitcast.18, f32[256,128]{1,0:T(8,128)S(1)} %bitcast.19, f32[256,128]{1,0:T(8,128)S(1)} %bitcast.20, f32[256,128]{1,0:T(8,128)S(1)} %bitcast.21, f32[256,128]{1,0:T(8,128)S(1)} %bitcast.22, ...), custom_call_target="tpu_custom_call" | custom-call | tf_op jit(solution)/shard_map/beams/pallas_call | solution.py:399
  60.7 14.0 %all_to_all.9 = f32[16,1,256]{2,1,0:T(1,128)S(1)} all-to-all(f32[16,1,256]{2,1,0:T(1,128)S(1)} %copy.9), channel_id=1, replica_groups=mesh['groups'=2,'section'=8,'sub'=2] {'section','sub'}, dimensions={0} | all-to-all | bytes 32768 | tf_op jit(solution)/shard_map/all_to_all | solution.py:476
  74.7 0.9 %divide_bitcast_fusion = f32[1,16,32,256]{3,2,1,0:T(8,128)} fusion(f32[16,32,256]{2,1,0:T(8,128)S(1)} %get-tuple-element.57, f32[256]{0:T(256)S(1)} %multiply_add_fusion.1), kind=kLoop, calls=%fused_computation.6 | loop fusion | flops 131072 | bytes 1049600 | tf_op jit(solution)/shard_map/broadcast_in_dim | solution.py:478
  (7 shorter events, 0.1 us)
Async XLA Ops:
  0.0 16.1 %copy-start.1 = (f32[256]{0:T(256)S(1)}, f32[256]{0:T(256)}, u32[]{:S(2)}) copy-start(f32[256]{0:T(256)} %param.11) | copy-start | bytes 3076
  2.2 27.4 %copy-start.2 = (s32[256]{0:T(256)S(1)}, s32[256]{0:T(256)}, u32[]{:S(2)}) copy-start(s32[256]{0:T(256)} %param.13) | copy-start | bytes 3076
  2.2 13.9 %collective-permute-start.10 = (f32[2,4,32,128]{3,2,1,0:T(8,128)S(1)}, f32[2,4,32,128]{3,2,1,0:T(8,128)S(1)}, u32[]{:S(2)}, u32[]{:S(2)}) collective-permute-start(f32[2,4,32,128]{3,2,1,0:T(8,128)S(1)} %get-tuple-element.45), channel_id=1, source_target_pairs={{0,6},{2,4},{4,2},{6,0},{8,14},{10,12},{12,10},{14,8},{1,7},{3,5},... | collective-permute-start | bytes 393224 | tf_op jit(solution)/shard_map/ppermute | solution.py:439
  6.3 18.2 %collective-permute-start.11 = (f32[2,4,32,128]{3,2,1,0:T(8,128)S(1)}, f32[2,4,32,128]{3,2,1,0:T(8,128)S(1)}, u32[]{:S(2)}, u32[]{:S(2)}) collective-permute-start(f32[2,4,32,128]{3,2,1,0:T(8,128)S(1)} %get-tuple-element.46), channel_id=1, source_target_pairs={{0,8},{2,10},{4,12},{6,14},{8,0},{10,2},{12,4},{14,6},{1,9},{3,11}... | collective-permute-start | bytes 393224 | tf_op jit(solution)/shard_map/ppermute | solution.py:439
  8.9 17.9 %collective-permute-start.12 = (f32[2,4,32,128]{3,2,1,0:T(8,128)S(1)}, f32[2,4,32,128]{3,2,1,0:T(8,128)S(1)}, u32[]{:S(2)}, u32[]{:S(2)}) collective-permute-start(f32[2,4,32,128]{3,2,1,0:T(8,128)S(1)} %get-tuple-element.47), channel_id=1, source_target_pairs={{0,10},{2,8},{4,14},{6,12},{8,2},{10,0},{12,6},{14,4},{1,11},{3,9}... | collective-permute-start | bytes 393224 | tf_op jit(solution)/shard_map/ppermute | solution.py:439
  9.2 17.6 %collective-permute-start.13 = (f32[2,4,32,128]{3,2,1,0:T(8,128)S(1)}, f32[2,4,32,128]{3,2,1,0:T(8,128)S(1)}, u32[]{:S(2)}, u32[]{:S(2)}) collective-permute-start(f32[2,4,32,128]{3,2,1,0:T(8,128)S(1)} %get-tuple-element.48), channel_id=1, source_target_pairs={{0,12},{2,14},{4,8},{6,10},{8,4},{10,6},{12,0},{14,2},{1,13},{3,15... | collective-permute-start | bytes 393224 | tf_op jit(solution)/shard_map/ppermute | solution.py:439
  11.6 15.1 %collective-permute-start.14 = (f32[2,4,32,128]{3,2,1,0:T(8,128)S(1)}, f32[2,4,32,128]{3,2,1,0:T(8,128)S(1)}, u32[]{:S(2)}, u32[]{:S(2)}) collective-permute-start(f32[2,4,32,128]{3,2,1,0:T(8,128)S(1)} %get-tuple-element.49), channel_id=1, source_target_pairs={{0,14},{2,12},{4,10},{6,8},{8,6},{10,4},{12,2},{14,0},{1,15},{3,13... | collective-permute-start | bytes 393224 | tf_op jit(solution)/shard_map/ppermute | solution.py:439
  16.1 10.7 %collective-permute-start.8 = (f32[2,4,32,128]{3,2,1,0:T(8,128)S(1)}, f32[2,4,32,128]{3,2,1,0:T(8,128)S(1)}, u32[]{:S(2)}, u32[]{:S(2)}) collective-permute-start(f32[2,4,32,128]{3,2,1,0:T(8,128)S(1)} %get-tuple-element.43), channel_id=1, source_target_pairs={{0,2},{2,0},{4,6},{6,4},{8,10},{10,8},{12,14},{14,12},{1,3},{3,1},... | collective-permute-start | bytes 393224 | tf_op jit(solution)/shard_map/ppermute | solution.py:439
  24.5 5.0 %collective-permute-start.9 = (f32[2,4,32,128]{3,2,1,0:T(8,128)S(1)}, f32[2,4,32,128]{3,2,1,0:T(8,128)S(1)}, u32[]{:S(2)}, u32[]{:S(2)}) collective-permute-start(f32[2,4,32,128]{3,2,1,0:T(8,128)S(1)} %get-tuple-element.44), channel_id=1, source_target_pairs={{0,4},{2,6},{4,0},{6,2},{8,12},{10,14},{12,8},{14,10},{1,5},{3,7},... | collective-permute-start | bytes 393224 | tf_op jit(solution)/shard_map/ppermute | solution.py:439
  26.8 3.9 %collective-permute-start = (f32[8,2,4,16,128]{4,3,2,1,0:T(8,128)S(1)}, f32[8,2,4,16,128]{4,3,2,1,0:T(8,128)S(1)}, u32[]{:S(2)}, u32[]{:S(2)}) collective-permute-start(f32[8,2,4,16,128]{4,3,2,1,0:T(8,128)S(1)} %get-tuple-element.33), channel_id=1, source_target_pairs={{0,1},{1,0},{2,3},{3,2},{4,5},{5,4},{6,7},{7,6},{8,9},{9,8},{10,11... | collective-permute-start | bytes 1572872 | tf_op jit(solution)/shard_map/ppermute | solution.py:443
  29.6 8.9 %collective-permute-start.15 = (f32[8,2,4,16,128]{4,3,2,1,0:T(8,128)S(1)}, f32[8,2,4,16,128]{4,3,2,1,0:T(8,128)S(1)}, u32[]{:S(2)}, u32[]{:S(2)}) collective-permute-start(f32[8,2,4,16,128]{4,3,2,1,0:T(8,128)S(1)} %get-tuple-element.51), channel_id=1, source_target_pairs={{0,1},{1,0},{2,3},{3,2},{4,5},{5,4},{6,7},{7,6},{8,9},{9,8},{10,11... | collective-permute-start | bytes 1572872 | tf_op jit(solution)/shard_map/ppermute | solution.py:443
  30.8 8.7 %collective-permute-start.1 = (f32[2,2,4,16,128]{4,3,2,1,0:T(8,128)S(1)}, f32[2,2,4,16,128]{4,3,2,1,0:T(8,128)S(1)}, u32[]{:S(2)}, u32[]{:S(2)}) collective-permute-start(f32[2,2,4,16,128]{4,3,2,1,0:T(8,128)S(1)} %get-tuple-element.35), channel_id=1, source_target_pairs={{0,2},{2,0},{4,6},{6,4},{8,10},{10,8},{12,14},{14,12},{1,3},{3,1},... | collective-permute-start | bytes 393224 | tf_op jit(solution)/shard_map/ppermute | solution.py:439
  30.9 12.8 %collective-permute-start.2 = (f32[2,2,4,16,128]{4,3,2,1,0:T(8,128)S(1)}, f32[2,2,4,16,128]{4,3,2,1,0:T(8,128)S(1)}, u32[]{:S(2)}, u32[]{:S(2)}) collective-permute-start(f32[2,2,4,16,128]{4,3,2,1,0:T(8,128)S(1)} %get-tuple-element.36), channel_id=1, source_target_pairs={{0,4},{2,6},{4,0},{6,2},{8,12},{10,14},{12,8},{14,10},{1,5},{3,7},... | collective-permute-start | bytes 393224 | tf_op jit(solution)/shard_map/ppermute | solution.py:439
  35.5 9.0 %copy-start = (f32[2,5]{1,0:T(2,128)S(1)}, f32[2,5]{1,0:T(2,128)}, u32[]{:S(2)}) copy-start(f32[2,5]{1,0:T(2,128)} %refs_14_.1) | copy-start | bytes 124
  35.5 14.3 %collective-permute-start.3 = (f32[2,2,4,16,128]{4,3,2,1,0:T(8,128)S(1)}, f32[2,2,4,16,128]{4,3,2,1,0:T(8,128)S(1)}, u32[]{:S(2)}, u32[]{:S(2)}) collective-permute-start(f32[2,2,4,16,128]{4,3,2,1,0:T(8,128)S(1)} %get-tuple-element.37), channel_id=1, source_target_pairs={{0,6},{2,4},{4,2},{6,0},{8,14},{10,12},{12,10},{14,8},{1,7},{3,5},... | collective-permute-start | bytes 393224 | tf_op jit(solution)/shard_map/ppermute | solution.py:439
  35.6 14.2 %collective-permute-start.4 = (f32[2,2,4,16,128]{4,3,2,1,0:T(8,128)S(1)}, f32[2,2,4,16,128]{4,3,2,1,0:T(8,128)S(1)}, u32[]{:S(2)}, u32[]{:S(2)}) collective-permute-start(f32[2,2,4,16,128]{4,3,2,1,0:T(8,128)S(1)} %get-tuple-element.38), channel_id=1, source_target_pairs={{0,8},{2,10},{4,12},{6,14},{8,0},{10,2},{12,4},{14,6},{1,9},{3,11}... | collective-permute-start | bytes 393224 | tf_op jit(solution)/shard_map/ppermute | solution.py:439
  38.5 19.1 %collective-permute-start.5 = (f32[2,2,4,16,128]{4,3,2,1,0:T(8,128)S(1)}, f32[2,2,4,16,128]{4,3,2,1,0:T(8,128)S(1)}, u32[]{:S(2)}, u32[]{:S(2)}) collective-permute-start(f32[2,2,4,16,128]{4,3,2,1,0:T(8,128)S(1)} %get-tuple-element.39), channel_id=1, source_target_pairs={{0,10},{2,8},{4,14},{6,12},{8,2},{10,0},{12,6},{14,4},{1,11},{3,9}... | collective-permute-start | bytes 393224 | tf_op jit(solution)/shard_map/ppermute | solution.py:439
  39.4 18.2 %collective-permute-start.6 = (f32[2,2,4,16,128]{4,3,2,1,0:T(8,128)S(1)}, f32[2,2,4,16,128]{4,3,2,1,0:T(8,128)S(1)}, u32[]{:S(2)}, u32[]{:S(2)}) collective-permute-start(f32[2,2,4,16,128]{4,3,2,1,0:T(8,128)S(1)} %get-tuple-element.40), channel_id=1, source_target_pairs={{0,12},{2,14},{4,8},{6,10},{8,4},{10,6},{12,0},{14,2},{1,13},{3,15... | collective-permute-start | bytes 393224 | tf_op jit(solution)/shard_map/ppermute | solution.py:439
  43.7 13.9 %collective-permute-start.7 = (f32[2,2,4,16,128]{4,3,2,1,0:T(8,128)S(1)}, f32[2,2,4,16,128]{4,3,2,1,0:T(8,128)S(1)}, u32[]{:S(2)}, u32[]{:S(2)}) collective-permute-start(f32[2,2,4,16,128]{4,3,2,1,0:T(8,128)S(1)} %get-tuple-element.41), channel_id=1, source_target_pairs={{0,14},{2,12},{4,10},{6,8},{8,6},{10,4},{12,2},{14,0},{1,15},{3,13... | collective-permute-start | bytes 393224 | tf_op jit(solution)/shard_map/ppermute | solution.py:439

commit v3 on v2

--- a/solution.py
+++ b/solution.py
@@ -199,17 +199,25 @@
     )(mine, other)
 
 
-def filter_matrix(taps_ref, gates, sections, conjugate):
+def filter_matrix(taps_ref, gates, sections, section, steps, conjugate):
     count = gates * sections
-    side = 2 * count
+    half = count if steps is None else len(steps) * gates
     taps = taps_ref.shape[1]
-    row = lax.broadcasted_iota(jnp.int32, (side, side), 0)
-    column = lax.broadcasted_iota(jnp.int32, (side, side), 1)
-    row_imag, column_imag = row >= count, column >= count
+    row = lax.broadcasted_iota(jnp.int32, (2 * count, 2 * half), 0)
+    column = lax.broadcasted_iota(jnp.int32, (2 * count, 2 * half), 1)
+    row_imag, column_imag = row >= count, column >= half
     row_gate = jnp.where(row_imag, row - count, row)
-    place = jnp.where(column_imag, column - count, column)
-    inner = sum(jnp.where(place >= gate * sections, 1, 0) for gate in range(1, gates))
-    column_gate = (place - inner * sections) * gates + inner
+    place = jnp.where(column_imag, column - half, column)
+    if steps is None:
+        inner = sum(jnp.where(place >= gate * sections, 1, 0) for gate in range(1, gates))
+        step = place - inner * sections
+    else:
+        outer = sum(jnp.where(place >= order * gates, 1, 0) for order in range(1, len(steps)))
+        inner = place - outer * gates
+        step = jnp.full(place.shape, steps[0], jnp.int32)
+        for order in range(1, len(steps)):
+            step = jnp.where(outer >= order, steps[order], step)
+    column_gate = jnp.bitwise_xor(step, section) * gates + inner
     tap = column_gate - row_gate + taps // 2
     real = sum(jnp.where(tap == j, taps_ref[0, j], 0.0) for j in range(taps))
     imag = sum(jnp.where(tap == j, taps_ref[1, j], 0.0) for j in range(taps))
@@ -217,7 +225,7 @@
     matrix = jnp.where(straight, real, crossed)
     if conjugate:
         matrix = jnp.where(row_imag, -matrix, matrix)
-    return split(matrix)
+    return matrix
 
 
 def stacked(product, left, right):
@@ -249,9 +257,9 @@
     other = other.reshape(sections * stride, LANES)
 
     def body(mine_ref, other_ref, steer_ref, taps_ref, load_ref,
-             bh_ref, bl_ref, th_ref, tl_ref, gain_ref,
+             b_ref, th_ref, tl_ref, gain_ref,
              ah_ref, al_ref, rows_ref, sums_ref, squares_ref, u_ref, gram_ref):
-        matrix = filter_matrix(taps_ref, gates, sections, True)
+        matrix = split(filter_matrix(taps_ref, gates, sections, 0, None, True))
         for index in range(own):
             def load(ref):
                 return jnp.concatenate(
@@ -264,8 +272,8 @@
             high, low = split(value)
             ah_ref[index] = high
             al_ref[index] = low
-            bh_ref[index] = beside(high, False)
-            bl_ref[index] = beside(low, False)
+            b_ref[index, :side] = beside(high, False)
+            b_ref[index, side:] = beside(low, False)
             here = slice(index * count, (index + 1) * count)
             for place, part in enumerate((high, low, high)):
                 lanes = slice(place * 2 * channels, (place + 1) * 2 * channels)
@@ -322,13 +330,13 @@
         gain = power - sums_ref[...]
         gain_ref[...] = 1.0 / (gain * gain)
 
-    wide = jax.ShapeDtypeStruct((own, side, 2 * channels), BF16)
+    wide = jax.ShapeDtypeStruct((own, 2 * side, 2 * channels), BF16)
     turned = jax.ShapeDtypeStruct((own, side, 2 * beams), BF16)
     return pl.pallas_call(
         body,
         in_specs=[VMEM] * 3 + [SMEM] * 2,
-        out_specs=[VMEM] * 5,
-        out_shape=[wide, wide, turned, turned, jax.ShapeDtypeStruct((own, beams), F32)],
+        out_specs=[VMEM] * 4,
+        out_shape=[wide, turned, turned, jax.ShapeDtypeStruct((own, beams), F32)],
         scratch_shapes=[
             pltpu.VMEM((own, side, channels), BF16),
             pltpu.VMEM((own, side, channels), BF16),
@@ -343,28 +351,25 @@
     )(mine, other, steer, range_taps, loading)
 
 
-def beams_kernel(blocks, weights, steer, range_taps):
-    sections = len(blocks)
-    _, _, gates, own, _ = blocks[0].shape
+def near_kernel(blocks, conjugated, turned, steer, range_taps):
+    steps = sorted(blocks)
+    _, _, gates, own, _ = blocks[steps[0]].shape
     size = 4 * gates * own
     pitch = size + PAD
-    count = sections * gates
-    side = 2 * count
-    channels = 2 * LANES
+    wide = 4 * LANES
+    side = conjugated.shape[1] // 2
+    count = side // 2
+    sections = count // gates
     beams = steer.shape[1] // 2
-    blocks = [block.reshape(size, LANES) for block in blocks]
 
     def body(*refs):
-        block_refs = refs[:sections]
-        (bh_ref, bl_ref, th_ref, tl_ref, gain_ref, steer_ref, taps_ref,
-         power_ref, total_ref, held, rows_ref, v_ref, cross_ref) = refs[sections:]
-        section = lax.axis_index("section")
+        (b_ref, th_ref, tl_ref, steer_ref, taps_ref, out_ref,
+         held, rows_ref, v_ref, cross_ref) = refs[len(steps) :]
         for step in range(sections):
-            start = pl.multiple_of(jnp.bitwise_xor(section, step) * pitch, 8)
-            held[pl.ds(start, size), :] = block_refs[step][...]
-        matrix = filter_matrix(taps_ref, gates, sections, False)
+            here = slice(step * pitch, step * pitch + size)
+            held[here, :] = refs[steps.index(step)][...] if step in steps else jnp.zeros((size, LANES), F32)
+        matrix = split(filter_matrix(taps_ref, gates, sections, lax.axis_index("section"), None, False))
         matrix = jnp.concatenate([matrix[0], matrix[1], matrix[0]], axis=1)
-        wide = 2 * channels
         for index in range(own):
             def load(half, part):
                 return jnp.concatenate(
@@ -378,19 +383,83 @@
                 rows_ref[here, place * wide : (place + 1) * wide] = part
         for index in range(own):
             here = slice(index * count, (index + 1) * count)
-            parts = rows_ref[here, :wide], rows_ref[here, wide : 2 * wide]
-            cross_ref[index] = stacked(dot_nt, parts, (bh_ref[index], bl_ref[index]))
+            parts = jnp.concatenate([rows_ref[here, :wide], rows_ref[here, wide : 2 * wide]], axis=0)
+            both = dot_nt(parts, b_ref[index])
+            both = both[:count] + both[count:]
+            cross_ref[index] = both[:, :side] + both[:, side:]
         v_ref[...] = dot(rows_ref[...], steer_ref[...])
         for index in range(own):
             here = slice(index * count, (index + 1) * count)
             low_rank = stacked(dot, split(cross_ref[index]), (th_ref[index], tl_ref[index]))
             v_ref[here, :] = v_ref[here, :] - low_rank
+        for index in range(own):
+            v = v_ref[index * count : (index + 1) * count, :]
+            high, low = split(jnp.concatenate([v[:, :beams], v[:, beams:]], axis=0))
+            out_ref[index] = dot(matrix, jnp.concatenate([high, high, low], axis=0))
+
+    return pl.pallas_call(
+        body,
+        in_specs=[VMEM] * (len(steps) + 4) + [SMEM],
+        out_specs=VMEM,
+        out_shape=jax.ShapeDtypeStruct((own, side, beams), F32),
+        scratch_shapes=[
+            pltpu.VMEM((sections * pitch, LANES), F32),
+            pltpu.VMEM((own * count, 3 * wide), BF16),
+            pltpu.VMEM((own * count, 2 * beams), F32),
+            pltpu.VMEM((own, count, side), F32),
+        ],
+        compiler_params=pltpu.CompilerParams(vmem_limit_bytes=LIMIT),
+        name="near",
+    )(*[blocks[step].reshape(size, LANES) for step in steps], conjugated, *turned, steer, range_taps)
+
+
+def beams_kernel(blocks, near, weights, steer, range_taps):
+    steps = sorted(blocks)
+    _, _, gates, own, _ = blocks[steps[0]].shape
+    size = 4 * gates * own
+    side = near.shape[1]
+    count = side // 2
+    sections = count // gates
+    beams = steer.shape[1] // 2
+    each = len(steps) * gates
+    group = 16 // each
+
+    def body(*refs):
+        (near_ref, b_ref, th_ref, tl_ref, gain_ref, steer_ref, taps_ref,
+         power_ref, total_ref, dense) = refs[len(steps) :]
+        for order in range(len(steps)):
+            for half in (0, 1):
+                for part in (0, 1):
+                    for gate in range(gates):
+                        start = ((half * 2 + part) * gates + gate) * own
+                        at = pl.ds(order * gates + gate, own, stride=each)
+                        dense[part * 2 + half, at, :] = refs[order][start : start + own, :]
+        matrix = filter_matrix(taps_ref, gates, sections, lax.axis_index("section"), steps, False)
+        first, second = split(matrix)
+        first, second = first.astype(F32), second.astype(F32)
+        matrix = jnp.concatenate([first, second, first], axis=1).astype(BF16)
+        high, low = split(jnp.concatenate([dense[place] for place in range(4)], axis=1))
+        value = dot(jnp.concatenate([high, low, high], axis=1), steer_ref[...])
+        crosses = []
+        for index in range(own):
+            base = index // group * group * each
+            rows = slice(base, base + group * each)
+            parts = jnp.concatenate([high[rows], low[rows]], axis=0)
+            both = dot_nt(parts, b_ref[index])
+            both = both[: group * each] + both[group * each :]
+            both = both[index * each - base : (index + 1) * each - base]
+            crosses.append(both[:, :side] + both[:, side:])
+        stacks = []
+        for index in range(own):
+            ch, cl = split(crosses[index])
+            both = jnp.concatenate([ch.astype(F32), cl.astype(F32)], axis=0).astype(BF16)
+            both = dot(both, th_ref[index]) + dot(both, tl_ref[index])
+            v = value[index * each : (index + 1) * each, :] - (both[:each] + both[each:])
+            high, low = split(jnp.concatenate([v[:, :beams], v[:, beams:]], axis=0))
+            stacks.append(jnp.concatenate([high, high, low], axis=0))
         total = jnp.zeros((1, beams), F32)
         for index in range(own):
-            v = v_ref[index * count : (index + 1) * count, :]
-            up = jnp.concatenate([v[:, :beams], v[:, beams:]], axis=0)
-            high, low = split(up)
-            out = dot(matrix, jnp.concatenate([high, high, low], axis=0))
+            out = near_ref[index] + dot(matrix, stacks[index])
             power = (out[:count] * out[:count] + out[count:] * out[count:]) * gain_ref[index : index + 1, :]
             total = total + jnp.sum(power, axis=0, keepdims=True)
             power_ref[index] = power
@@ -398,21 +467,16 @@
 
     return pl.pallas_call(
         body,
-        in_specs=[VMEM] * (sections + 6) + [SMEM],
+        in_specs=[VMEM] * (len(steps) + 6) + [SMEM],
         out_specs=[VMEM] * 2,
         out_shape=[
             jax.ShapeDtypeStruct((own, count, beams), F32),
             jax.ShapeDtypeStruct((2 * sections, beams), F32),
         ],
-        scratch_shapes=[
-            pltpu.VMEM((sections * pitch, LANES), F32),
-            pltpu.VMEM((own * count, 6 * channels), BF16),
-            pltpu.VMEM((own * count, 2 * beams), F32),
-            pltpu.VMEM((own, count, side), F32),
-        ],
+        scratch_shapes=[pltpu.VMEM((4, own * each, LANES), F32)],
         compiler_params=pltpu.CompilerParams(vmem_limit_bytes=LIMIT),
         name="beams",
-    )(*blocks, *weights, steer, range_taps)
+    )(*[blocks[step].reshape(size, LANES) for step in steps], near, *weights, steer, range_taps)
 
 
 def steering_tables(beam_index, channel_phase):
@@ -470,9 +534,11 @@
     keep, pass_on = gather_sub([got[step] for step in range(sections)])
     other = swapped(pass_on)
     weights = weights_kernel(keep, other, steer, range_taps, loading)
-    power, total = beams_kernel(
-        [later[step] for step in range(sections)], weights, steer, range_taps
-    )
+    last = hop_order(sections)[1][-2:]
+    blocks = {step: block for step, block in later.items() if step not in last}
+    near = near_kernel(blocks, weights[0], weights[1:3], steer, range_taps)
+    blocks = {step: later[step] for step in last}
+    power, total = beams_kernel(blocks, near, weights, steer, range_taps)
     totals = lax.all_to_all(total, ("section", "sub"), 0, 0, tiled=True)
     noise_level = jnp.sum(totals, axis=0) / (PULSES * gates * sections)
     return (power / (noise_level + epsilon))[None]

time: 75.8 us -> 75.9 us (level)
  blocking collectives: 14 us -> 10.1 us
  Pallas kernels: 12.8 us -> 14.8 us
  starting transfers between devices: 23.2 us -> 24.7 us
    all_to_all x1, blocking collectives: 14 us -> 10.1 us  [factored_steps(): totals = lax.all_to_all(total, ('section', 'sub'), 0, 0, tiled=True)]
    pallas_call x1 -> x2, Pallas kernels: 2.98 us -> 5.03 us  [the longest x1 3.01 us: near_kernel(): pl.pallas_call(body, in_specs=[VMEM] * (len(steps) + 4) + [SMEM], out_spe...]
    ppermute x14, starting transfers between devices: 23.1 us -> 24.6 us  [permuted(): lax.ppermute(block, 'section', [(place, place ^ step) for place in range(...]
  transfers between devices with their start and end apart: 16 -> 16, of which waited for: 5 -> 6; matrix products, arithmetic and copies ran while one was open for 2% -> 2% of each run, Pallas kernels for 10% -> 14%
where the time goes in v3:
time: 75.9 us; the launch traced here: 75.7 us
  starting transfers between devices  24.7 us (33%)
  waiting for transfers between devices  22.9 us (30%)
  Pallas kernels  14.8 us (19%)
  blocking collectives  10.1 us (13%)
  other arithmetic  2.21 us (3%)
  between operations  0.85 us (1%)
    ppermute x14, starting transfers between devices, permuted(): lax.ppermute(block, 'section', [(place, place ^ step) for place in range(...  24.6 us
    ppermute x14, waiting for transfers between devices, permuted(): lax.ppermute(block, 'section', [(place, place ^ step) for place in range(...  22.9 us
    all_to_all x1, blocking collectives, factored_steps(): totals = lax.all_to_all(total, ('section', 'sub'), 0, 0, tiled=True)  10.1 us
    pallas_call x1, Pallas kernels, weights_kernel(): pl.pallas_call(body, in_specs=[VMEM] * 3 + [SMEM] * 2, out_specs=[VMEM] *...  5.24 us
    pallas_call x2, Pallas kernels, doppler(): pl.pallas_call(body, in_specs=[HBM] * 3, out_specs=[VMEM] * len(outs), ou...  4.38 us
    pallas_call x1, Pallas kernels, near_kernel(): pl.pallas_call(body, in_specs=[VMEM] * (len(steps) + 4) + [SMEM], out_spe...  3.01 us
    pallas_call x1, Pallas kernels, beams_kernel(): pl.pallas_call(body, in_specs=[VMEM] * (len(steps) + 6) + [SMEM], out_spe...  2.02 us
  transfers between devices with their start and end apart: 16, of which 6 were waited for; matrix products, arithmetic and copies ran while one was open for 2% of the time, Pallas kernels for 14%

profile of v3, /device:TPU:0, one launch (start us, length us, event | category | flops | bytes accessed | tf_op | source)
XLA Modules:
  0.0 75.7 jit_solution(10880425470424592239)
XLA Ops:
  0.0 0.0 copy-start.1
  0.0 2.2 %shard_map.83 = (f32[2,4,32,128]{3,2,1,0:T(8,128)S(1)}, f32[2,4,32,128]{3,2,1,0:T(8,128)S(1)}, f32[2,4,32,128]{3,2,1,0:T(8,128)S(1)}, f32[2,4,32,128]{3,2,1,0:T(...) custom-call(f32[2,3,512,128]{3,2,1,0:T(8,128)} %bitcast.26, ...), custom_call_target="tpu_custom_call" | custom-call | tf_op jit(solution)/shard_map/pallas_call | solution.py:141
  2.2 4.1 %collective-permute-start.10 = (f32[2,4,32,128]{3,2,1,0:T(8,128)S(1)}, f32[2,4,32,128]{3,2,1,0:T(8,128)S(1)}, u32[]{:S(2)}, u32[]{:S(2)}) collective-permute-start(f32[2,4,32,128]{3,2,1,0:T(8,128)S(1)} %get-tuple-element.44), channel_id=1, source_target_pairs={{0,6},{2,4},{4,2},{6,0},{8,14},{10,12},{12,10},{14,8},{1,7},{3,5},... | collective-permute-start | bytes 393224 | tf_op jit(solution)/shard_map/ppermute | solution.py:503
  6.3 2.6 %collective-permute-start.11 = (f32[2,4,32,128]{3,2,1,0:T(8,128)S(1)}, f32[2,4,32,128]{3,2,1,0:T(8,128)S(1)}, u32[]{:S(2)}, u32[]{:S(2)}) collective-permute-start(f32[2,4,32,128]{3,2,1,0:T(8,128)S(1)} %get-tuple-element.45), channel_id=1, source_target_pairs={{0,8},{2,10},{4,12},{6,14},{8,0},{10,2},{12,4},{14,6},{1,9},{3,11}... | collective-permute-start | bytes 393224 | tf_op jit(solution)/shard_map/ppermute | solution.py:503
  8.9 0.3 collective-permute-start.12
  9.2 2.5 %collective-permute-start.13 = (f32[2,4,32,128]{3,2,1,0:T(8,128)S(1)}, f32[2,4,32,128]{3,2,1,0:T(8,128)S(1)}, u32[]{:S(2)}, u32[]{:S(2)}) collective-permute-start(f32[2,4,32,128]{3,2,1,0:T(8,128)S(1)} %get-tuple-element.47), channel_id=1, source_target_pairs={{0,12},{2,14},{4,8},{6,10},{8,4},{10,6},{12,0},{14,2},{1,13},{3,15... | collective-permute-start | bytes 393224 | tf_op jit(solution)/shard_map/ppermute | solution.py:503
  11.6 2.3 %collective-permute-start.14 = (f32[2,4,32,128]{3,2,1,0:T(8,128)S(1)}, f32[2,4,32,128]{3,2,1,0:T(8,128)S(1)}, u32[]{:S(2)}, u32[]{:S(2)}) collective-permute-start(f32[2,4,32,128]{3,2,1,0:T(8,128)S(1)} %get-tuple-element.48), channel_id=1, source_target_pairs={{0,14},{2,12},{4,10},{6,8},{8,6},{10,4},{12,2},{14,0},{1,15},{3,13... | collective-permute-start | bytes 393224 | tf_op jit(solution)/shard_map/ppermute | solution.py:503
  13.9 2.2 %shard_map.82 = (f32[8,2,4,16,128]{4,3,2,1,0:T(8,128)S(1)}, f32[8,2,4,16,128]{4,3,2,1,0:T(8,128)S(1)}) custom-call(f32[2,3,512,128]{3,2,1,0:T(8,128)} %bitcast.27, f32[2,128]{1,0:T(2,128)} %bitcast.29, bf16[4,128,256]{2,1,0:T(8,128)(2,1)} %constant.32.clone.table_ref), custom_call_target="tpu_custom_call" | custom-call | tf_op jit(solution)/shard_map/pallas_call | solution.py:141
  16.1 0.0 copy-done.1
  16.1 0.0 collective-permute-done.10.refs_3_
  16.1 0.6 collective-permute-start.8
  16.7 7.7 %collective-permute-done.11.refs_4_ = f32[2,4,32,128]{3,2,1,0:T(8,128)S(1)} collective-permute-done((f32[2,4,32,128]{3,2,1,0:T(8,128)S(1)}, f32[2,4,32,128]{3,2,1,0:T(8,128)S(1)}, u32[]{:S(2)}, u32[]{:S(2)}) %collective-permute-start.11) | collective-permute-done | bytes 131104 | tf_op jit(solution)/shard_map/ppermute | solution.py:503
  24.5 0.0 collective-permute-start.9
  24.5 2.3 %collective-permute-done.12.refs_5_ = f32[2,4,32,128]{3,2,1,0:T(8,128)S(1)} collective-permute-done((f32[2,4,32,128]{3,2,1,0:T(8,128)S(1)}, f32[2,4,32,128]{3,2,1,0:T(8,128)S(1)}, u32[]{:S(2)}, u32[]{:S(2)}) %collective-permute-start.12) | collective-permute-done | bytes 131104 | tf_op jit(solution)/shard_map/ppermute | solution.py:503
  26.8 0.0 collective-permute-start
  26.8 0.0 collective-permute-done.13.refs_6_
  26.8 0.0 collective-permute-done.14.refs_7_
  26.8 0.0 collective-permute-done.8.refs_1_
  26.8 2.6 %collective-permute-done.9.refs_2_ = f32[2,4,32,128]{3,2,1,0:T(8,128)S(1)} collective-permute-done((f32[2,4,32,128]{3,2,1,0:T(8,128)S(1)}, f32[2,4,32,128]{3,2,1,0:T(8,128)S(1)}, u32[]{:S(2)}, u32[]{:S(2)}) %collective-permute-start.9) | collective-permute-done | bytes 131104 | tf_op jit(solution)/shard_map/ppermute | solution.py:503
  29.4 0.1 gather_sub.1
  29.5 0.1 collective-permute-start.15
  29.6 0.0 copy-done.2
  29.6 1.0 %fusion.4 = (f32[256,256]{1,0:T(8,128)S(1)}, f32[256,256]{1,0:T(8,128)S(1)}, f32[256,256]{1,0:T(8,128)S(1)}) fusion(f32[256]{0:T(256)S(1)} %get-tuple-element.65, f32[256]{0:T(256)S(1)} %multiply_add_fusion.2, f32[256]{0:T(256)S(1)} %get-tuple-element.64), kind=kLoop, calls=%fused_computation.10 | loop fusion | flops 196608 | bytes 789504 | tf_op jit(solution)/shard_map/neg | solution.py:494
  30.7 0.0 collective-permute-done.other_ref
  30.7 0.1 pair_up.1
  30.8 0.2 collective-permute-start.3
  30.9 4.4 %collective-permute-start.4 = (f32[2,2,4,16,128]{4,3,2,1,0:T(8,128)S(1)}, f32[2,2,4,16,128]{4,3,2,1,0:T(8,128)S(1)}, u32[]{:S(2)}, u32[]{:S(2)}) collective-permute-start(f32[2,2,4,16,128]{4,3,2,1,0:T(8,128)S(1)} %get-tuple-element.37), channel_id=1, source_target_pairs={{0,4},{2,6},{4,0},{6,2},{8,12},{10,14},{12,8},{14,10},{1,5},{3,7},... | collective-permute-start | bytes 393224 | tf_op jit(solution)/shard_map/ppermute | solution.py:503
  35.3 0.1 reduce-precision_convert_fusion
  35.5 0.1 collective-permute-start.5
  35.5 2.5 %collective-permute-start.6 = (f32[2,2,4,16,128]{4,3,2,1,0:T(8,128)S(1)}, f32[2,2,4,16,128]{4,3,2,1,0:T(8,128)S(1)}, u32[]{:S(2)}, u32[]{:S(2)}) collective-permute-start(f32[2,2,4,16,128]{4,3,2,1,0:T(8,128)S(1)} %get-tuple-element.39), channel_id=1, source_target_pairs={{0,12},{2,14},{4,8},{6,10},{8,4},{10,6},{12,0},{14,2},{1,13},{3,15... | collective-permute-start | bytes 393224 | tf_op jit(solution)/shard_map/ppermute | solution.py:503
  38.0 0.0 collective-permute-done.15
  38.0 2.2 %collective-permute-start.7 = (f32[2,2,4,16,128]{4,3,2,1,0:T(8,128)S(1)}, f32[2,2,4,16,128]{4,3,2,1,0:T(8,128)S(1)}, u32[]{:S(2)}, u32[]{:S(2)}) collective-permute-start(f32[2,2,4,16,128]{4,3,2,1,0:T(8,128)S(1)} %get-tuple-element.40), channel_id=1, source_target_pairs={{0,14},{2,12},{4,10},{6,8},{8,6},{10,4},{12,2},{14,0},{1,15},{3,13... | collective-permute-start | bytes 393224 | tf_op jit(solution)/shard_map/ppermute | solution.py:503
  40.3 0.0 collective-permute-done.3
  40.3 1.2 %collective-permute-start.1 = (f32[2,2,4,16,128]{4,3,2,1,0:T(8,128)S(1)}, f32[2,2,4,16,128]{4,3,2,1,0:T(8,128)S(1)}, u32[]{:S(2)}, u32[]{:S(2)}) collective-permute-start(f32[2,2,4,16,128]{4,3,2,1,0:T(8,128)S(1)} %get-tuple-element.33), channel_id=1, source_target_pairs={{0,8},{2,10},{4,12},{6,14},{8,0},{10,2},{12,4},{14,6},{1,9},{3,11}... | collective-permute-start | bytes 393224 | tf_op jit(solution)/shard_map/ppermute | solution.py:503
  41.5 0.0 collective-permute-done.4
  41.5 1.8 %collective-permute-start.2 = (f32[2,2,4,16,128]{4,3,2,1,0:T(8,128)S(1)}, f32[2,2,4,16,128]{4,3,2,1,0:T(8,128)S(1)}, u32[]{:S(2)}, u32[]{:S(2)}) collective-permute-start(f32[2,2,4,16,128]{4,3,2,1,0:T(8,128)S(1)} %get-tuple-element.34), channel_id=1, source_target_pairs={{0,10},{2,8},{4,14},{6,12},{8,2},{10,0},{12,6},{14,4},{1,11},{3,9}... | collective-permute-start | bytes 393224 | tf_op jit(solution)/shard_map/ppermute | solution.py:503
  43.3 0.1 pad_maximum_fusion.steer_ref.refs_9_.refs_7_
  44.0 0.0 copy-done
  44.1 5.2 %weights.1 = (bf16[16,128,512]{2,1,0:T(8,128)(2,1)S(1)}, bf16[16,64,512]{2,1,0:T(8,128)(2,1)S(1)}, bf16[16,64,512]{2,1,0:T(8,128)(2,1)S(1)}, f32[16,256]{1,0:T(8,128)S(1)}) custom-call(f32[1024,128]{1,0:T(8,128)S(1)} %bitcast.15, f32[1024,128]{1,0:T(8,128)S(1)} %bitcast.16, bf16[1536,512]{1,0:T(8,128)(2,1)S(1)} %pad_maximum_fusion.steer_ref.refs_9_.refs_7_, ...), custom_call_target="tpu_custom_call" | custom-call | tf_op jit(solution)/shard_map/weights/pallas_call | solution.py:335
  49.3 0.0 collective-permute-done.5
  49.3 0.0 collective-permute-done.6
  49.3 1.3 %collective-permute-done.7 = f32[2,2,4,16,128]{4,3,2,1,0:T(8,128)S(1)} collective-permute-done((f32[2,2,4,16,128]{4,3,2,1,0:T(8,128)S(1)}, f32[2,2,4,16,128]{4,3,2,1,0:T(8,128)S(1)}, u32[]{:S(2)}, u32[]{:S(2)}) %collective-permute-start.7) | collective-permute-done | bytes 131104 | tf_op jit(solution)/shard_map/ppermute | solution.py:503
  50.6 3.0 %near.1.refs_2_ = f32[16,64,256]{2,1,0:T(8,128)S(1)} custom-call(f32[256,128]{1,0:T(8,128)S(1)} %bitcast.17, f32[256,128]{1,0:T(8,128)S(1)} %bitcast.18, f32[256,128]{1,0:T(8,128)S(1)} %bitcast.19, f32[256,128]{1,0:T(8,128)S(1)} %bitcast.20, f32[256,128]{1,0:T(8,128)S(1)} %bitcast.21, f32[256,128]{1,0:T(8,128)S(1)} %bitcast.22, ...), custom_call_target="tpu_custom_call" | custom-call | tf_op jit(solution)/shard_map/near/pallas_call | solution.py:400
  53.6 6.4 %collective-permute-done.1 = f32[2,2,4,16,128]{4,3,2,1,0:T(8,128)S(1)} collective-permute-done((f32[2,2,4,16,128]{4,3,2,1,0:T(8,128)S(1)}, f32[2,2,4,16,128]{4,3,2,1,0:T(8,128)S(1)}, u32[]{:S(2)}, u32[]{:S(2)}) %collective-permute-start.1) | collective-permute-done | bytes 131104 | tf_op jit(solution)/shard_map/ppermute | solution.py:503
  60.0 2.6 %collective-permute-done.2 = f32[2,2,4,16,128]{4,3,2,1,0:T(8,128)S(1)} collective-permute-done((f32[2,2,4,16,128]{4,3,2,1,0:T(8,128)S(1)}, f32[2,2,4,16,128]{4,3,2,1,0:T(8,128)S(1)}, u32[]{:S(2)}, u32[]{:S(2)}) %collective-permute-start.2) | collective-permute-done | bytes 131104 | tf_op jit(solution)/shard_map/ppermute | solution.py:503
  62.6 2.0 %beams.1 = (f32[16,32,256]{2,1,0:T(8,128)S(1)}, f32[16,256]{1,0:T(8,128)S(1)}) custom-call(f32[256,128]{1,0:T(8,128)S(1)} %bitcast.23, f32[256,128]{1,0:T(8,128)S(1)} %bitcast.24, f32[16,64,256]{2,1,0:T(8,128)S(1)} %near.1.refs_2_, bf16[16,128,512]{2,1,0:T(8,128)(2,1)S(1)} %get-tuple-element.51.refs_6_.refs_3_, ...), custom_call_target="tpu_custom_call" | custom-call | tf_op jit(solution)/shard_map/beams/pallas_call | solution.py:468
  64.7 10.1 %all_to_all.9 = f32[16,1,256]{2,1,0:T(1,128)S(1)} all-to-all(f32[16,1,256]{2,1,0:T(1,128)S(1)} %copy.9), channel_id=1, replica_groups=mesh['groups'=2,'section'=8,'sub'=2] {'section','sub'}, dimensions={0} | all-to-all | bytes 32768 | tf_op jit(solution)/shard_map/all_to_all | solution.py:542
  74.8 0.9 %divide_bitcast_fusion = f32[1,16,32,256]{3,2,1,0:T(8,128)} fusion(f32[16,32,256]{2,1,0:T(8,128)S(1)} %get-tuple-element.55, f32[256]{0:T(256)S(1)} %multiply_add_fusion.1), kind=kLoop, calls=%fused_computation.6 | loop fusion | flops 131072 | bytes 1049600 | tf_op jit(solution)/shard_map/broadcast_in_dim | solution.py:544
  (8 shorter events, 0.1 us)
Async XLA Ops:
  0.0 16.1 %copy-start.1 = (f32[256]{0:T(256)S(1)}, f32[256]{0:T(256)}, u32[]{:S(2)}) copy-start(f32[256]{0:T(256)} %param.11) | copy-start | bytes 3076
  0.0 29.6 %copy-start.2 = (s32[256]{0:T(256)S(1)}, s32[256]{0:T(256)}, u32[]{:S(2)}) copy-start(s32[256]{0:T(256)} %param.13) | copy-start | bytes 3076
  2.2 13.9 %collective-permute-start.10 = (f32[2,4,32,128]{3,2,1,0:T(8,128)S(1)}, f32[2,4,32,128]{3,2,1,0:T(8,128)S(1)}, u32[]{:S(2)}, u32[]{:S(2)}) collective-permute-start(f32[2,4,32,128]{3,2,1,0:T(8,128)S(1)} %get-tuple-element.44), channel_id=1, source_target_pairs={{0,6},{2,4},{4,2},{6,0},{8,14},{10,12},{12,10},{14,8},{1,7},{3,5},... | collective-permute-start | bytes 393224 | tf_op jit(solution)/shard_map/ppermute | solution.py:503
  6.3 18.2 %collective-permute-start.11 = (f32[2,4,32,128]{3,2,1,0:T(8,128)S(1)}, f32[2,4,32,128]{3,2,1,0:T(8,128)S(1)}, u32[]{:S(2)}, u32[]{:S(2)}) collective-permute-start(f32[2,4,32,128]{3,2,1,0:T(8,128)S(1)} %get-tuple-element.45), channel_id=1, source_target_pairs={{0,8},{2,10},{4,12},{6,14},{8,0},{10,2},{12,4},{14,6},{1,9},{3,11}... | collective-permute-start | bytes 393224 | tf_op jit(solution)/shard_map/ppermute | solution.py:503
  8.9 17.9 %collective-permute-start.12 = (f32[2,4,32,128]{3,2,1,0:T(8,128)S(1)}, f32[2,4,32,128]{3,2,1,0:T(8,128)S(1)}, u32[]{:S(2)}, u32[]{:S(2)}) collective-permute-start(f32[2,4,32,128]{3,2,1,0:T(8,128)S(1)} %get-tuple-element.46), channel_id=1, source_target_pairs={{0,10},{2,8},{4,14},{6,12},{8,2},{10,0},{12,6},{14,4},{1,11},{3,9}... | collective-permute-start | bytes 393224 | tf_op jit(solution)/shard_map/ppermute | solution.py:503
  9.2 17.6 %collective-permute-start.13 = (f32[2,4,32,128]{3,2,1,0:T(8,128)S(1)}, f32[2,4,32,128]{3,2,1,0:T(8,128)S(1)}, u32[]{:S(2)}, u32[]{:S(2)}) collective-permute-start(f32[2,4,32,128]{3,2,1,0:T(8,128)S(1)} %get-tuple-element.47), channel_id=1, source_target_pairs={{0,12},{2,14},{4,8},{6,10},{8,4},{10,6},{12,0},{14,2},{1,13},{3,15... | collective-permute-start | bytes 393224 | tf_op jit(solution)/shard_map/ppermute | solution.py:503
  11.6 15.1 %collective-permute-start.14 = (f32[2,4,32,128]{3,2,1,0:T(8,128)S(1)}, f32[2,4,32,128]{3,2,1,0:T(8,128)S(1)}, u32[]{:S(2)}, u32[]{:S(2)}) collective-permute-start(f32[2,4,32,128]{3,2,1,0:T(8,128)S(1)} %get-tuple-element.48), channel_id=1, source_target_pairs={{0,14},{2,12},{4,10},{6,8},{8,6},{10,4},{12,2},{14,0},{1,15},{3,13... | collective-permute-start | bytes 393224 | tf_op jit(solution)/shard_map/ppermute | solution.py:503
  16.1 10.7 %collective-permute-start.8 = (f32[2,4,32,128]{3,2,1,0:T(8,128)S(1)}, f32[2,4,32,128]{3,2,1,0:T(8,128)S(1)}, u32[]{:S(2)}, u32[]{:S(2)}) collective-permute-start(f32[2,4,32,128]{3,2,1,0:T(8,128)S(1)} %get-tuple-element.42), channel_id=1, source_target_pairs={{0,2},{2,0},{4,6},{6,4},{8,10},{10,8},{12,14},{14,12},{1,3},{3,1},... | collective-permute-start | bytes 393224 | tf_op jit(solution)/shard_map/ppermute | solution.py:503
  24.5 5.0 %collective-permute-start.9 = (f32[2,4,32,128]{3,2,1,0:T(8,128)S(1)}, f32[2,4,32,128]{3,2,1,0:T(8,128)S(1)}, u32[]{:S(2)}, u32[]{:S(2)}) collective-permute-start(f32[2,4,32,128]{3,2,1,0:T(8,128)S(1)} %get-tuple-element.43), channel_id=1, source_target_pairs={{0,4},{2,6},{4,0},{6,2},{8,12},{10,14},{12,8},{14,10},{1,5},{3,7},... | collective-permute-start | bytes 393224 | tf_op jit(solution)/shard_map/ppermute | solution.py:503
  26.8 3.9 %collective-permute-start = (f32[8,2,4,16,128]{4,3,2,1,0:T(8,128)S(1)}, f32[8,2,4,16,128]{4,3,2,1,0:T(8,128)S(1)}, u32[]{:S(2)}, u32[]{:S(2)}) collective-permute-start(f32[8,2,4,16,128]{4,3,2,1,0:T(8,128)S(1)} %get-tuple-element.32), channel_id=1, source_target_pairs={{0,1},{1,0},{2,3},{3,2},{4,5},{5,4},{6,7},{7,6},{8,9},{9,8},{10,11... | collective-permute-start | bytes 1572872 | tf_op jit(solution)/shard_map/ppermute | solution.py:507
  29.5 8.5 %collective-permute-start.15 = (f32[8,2,4,16,128]{4,3,2,1,0:T(8,128)S(1)}, f32[8,2,4,16,128]{4,3,2,1,0:T(8,128)S(1)}, u32[]{:S(2)}, u32[]{:S(2)}) collective-permute-start(f32[8,2,4,16,128]{4,3,2,1,0:T(8,128)S(1)} %get-tuple-element.50), channel_id=1, source_target_pairs={{0,1},{1,0},{2,3},{3,2},{4,5},{5,4},{6,7},{7,6},{8,9},{9,8},{10,11... | collective-permute-start | bytes 1572872 | tf_op jit(solution)/shard_map/ppermute | solution.py:507
  30.8 9.5 %collective-permute-start.3 = (f32[2,2,4,16,128]{4,3,2,1,0:T(8,128)S(1)}, f32[2,2,4,16,128]{4,3,2,1,0:T(8,128)S(1)}, u32[]{:S(2)}, u32[]{:S(2)}) collective-permute-start(f32[2,2,4,16,128]{4,3,2,1,0:T(8,128)S(1)} %get-tuple-element.36), channel_id=1, source_target_pairs={{0,2},{2,0},{4,6},{6,4},{8,10},{10,8},{12,14},{14,12},{1,3},{3,1},... | collective-permute-start | bytes 393224 | tf_op jit(solution)/shard_map/ppermute | solution.py:503
  30.9 10.5 %collective-permute-start.4 = (f32[2,2,4,16,128]{4,3,2,1,0:T(8,128)S(1)}, f32[2,2,4,16,128]{4,3,2,1,0:T(8,128)S(1)}, u32[]{:S(2)}, u32[]{:S(2)}) collective-permute-start(f32[2,2,4,16,128]{4,3,2,1,0:T(8,128)S(1)} %get-tuple-element.37), channel_id=1, source_target_pairs={{0,4},{2,6},{4,0},{6,2},{8,12},{10,14},{12,8},{14,10},{1,5},{3,7},... | collective-permute-start | bytes 393224 | tf_op jit(solution)/shard_map/ppermute | solution.py:503
  35.3 8.7 %copy-start = (f32[2,5]{1,0:T(2,128)S(1)}, f32[2,5]{1,0:T(2,128)}, u32[]{:S(2)}) copy-start(f32[2,5]{1,0:T(2,128)} %refs_8_.1) | copy-start | bytes 124
  35.5 13.8 %collective-permute-start.5 = (f32[2,2,4,16,128]{4,3,2,1,0:T(8,128)S(1)}, f32[2,2,4,16,128]{4,3,2,1,0:T(8,128)S(1)}, u32[]{:S(2)}, u32[]{:S(2)}) collective-permute-start(f32[2,2,4,16,128]{4,3,2,1,0:T(8,128)S(1)} %get-tuple-element.38), channel_id=1, source_target_pairs={{0,6},{2,4},{4,2},{6,0},{8,14},{10,12},{12,10},{14,8},{1,7},{3,5},... | collective-permute-start | bytes 393224 | tf_op jit(solution)/shard_map/ppermute | solution.py:503
  35.5 13.8 %collective-permute-start.6 = (f32[2,2,4,16,128]{4,3,2,1,0:T(8,128)S(1)}, f32[2,2,4,16,128]{4,3,2,1,0:T(8,128)S(1)}, u32[]{:S(2)}, u32[]{:S(2)}) collective-permute-start(f32[2,2,4,16,128]{4,3,2,1,0:T(8,128)S(1)} %get-tuple-element.39), channel_id=1, source_target_pairs={{0,12},{2,14},{4,8},{6,10},{8,4},{10,6},{12,0},{14,2},{1,13},{3,15... | collective-permute-start | bytes 393224 | tf_op jit(solution)/shard_map/ppermute | solution.py:503
  38.0 12.5 %collective-permute-start.7 = (f32[2,2,4,16,128]{4,3,2,1,0:T(8,128)S(1)}, f32[2,2,4,16,128]{4,3,2,1,0:T(8,128)S(1)}, u32[]{:S(2)}, u32[]{:S(2)}) collective-permute-start(f32[2,2,4,16,128]{4,3,2,1,0:T(8,128)S(1)} %get-tuple-element.40), channel_id=1, source_target_pairs={{0,14},{2,12},{4,10},{6,8},{8,6},{10,4},{12,2},{14,0},{1,15},{3,13... | collective-permute-start | bytes 393224 | tf_op jit(solution)/shard_map/ppermute | solution.py:503
  40.3 19.7 %collective-permute-start.1 = (f32[2,2,4,16,128]{4,3,2,1,0:T(8,128)S(1)}, f32[2,2,4,16,128]{4,3,2,1,0:T(8,128)S(1)}, u32[]{:S(2)}, u32[]{:S(2)}) collective-permute-start(f32[2,2,4,16,128]{4,3,2,1,0:T(8,128)S(1)} %get-tuple-element.33), channel_id=1, source_target_pairs={{0,8},{2,10},{4,12},{6,14},{8,0},{10,2},{12,4},{14,6},{1,9},{3,11}... | collective-permute-start | bytes 393224 | tf_op jit(solution)/shard_map/ppermute | solution.py:503
  41.5 21.1 %collective-permute-start.2 = (f32[2,2,4,16,128]{4,3,2,1,0:T(8,128)S(1)}, f32[2,2,4,16,128]{4,3,2,1,0:T(8,128)S(1)}, u32[]{:S(2)}, u32[]{:S(2)}) collective-permute-start(f32[2,2,4,16,128]{4,3,2,1,0:T(8,128)S(1)} %get-tuple-element.34), channel_id=1, source_target_pairs={{0,10},{2,8},{4,14},{6,12},{8,2},{10,0},{12,6},{14,4},{1,11},{3,9}... | collective-permute-start | bytes 393224 | tf_op jit(solution)/shard_map/ppermute | solution.py:503

commit v4 on v3

--- a/solution.py
+++ b/solution.py
@@ -68,11 +68,8 @@
     return jnp.concatenate([rows, turned], axis=0)
 
 
-def doppler_body(gates, hop, view_ref, taper_ref, table_ref, result, tapers):
+def doppler_body(gates, hop, view_ref, table_ref, result, tapers):
     half = hop
-    for segment in (0, 1):
-        row = taper_ref[segment : segment + 1, :]
-        tapers[segment * hop : (segment + 1) * hop, :] = jnp.broadcast_to(row, (hop, hop)).T
     for group in range(0, gates, 2):
         members = range(group, min(group + 2, gates))
         for parity in (0, 1):
@@ -114,9 +111,13 @@
             copies.append(pltpu.make_async_copy(blocks, own_view.at[part], sems.at[2 + part]))
         for copy in copies:
             copy.start()
-        for copy in copies:
+        copies[0].wait()
+        for segment in (0, 1):
+            row = own_taper[segment : segment + 1, :]
+            tapers[segment * HOP : (segment + 1) * HOP, :] = jnp.broadcast_to(row, (HOP, HOP)).T
+        for copy in copies[1:]:
             copy.wait()
-        doppler_body(gates, HOP, own_view, own_taper, own_table, result, tapers)
+        doppler_body(gates, HOP, own_view, own_table, result, tapers)
         section = lax.axis_index("section")
         if not split_sub:
             for step in range(sections):
@@ -509,7 +510,8 @@
 
 def hop_order(sections):
     near, far = list(range(1, sections // 2)), list(range(sections // 2, sections))
-    return far[::-1] + near[::-1], near[::-1] + far[::-1]
+    half = len(far) // 2
+    return far[::-1] + near[::-1], far[:half][::-1] + near[::-1] + far[half:][::-1]
 
 
 def factored_steps(echoes, range_taps, pulse_taper, channel_phase, loading, beam_index):

time: 75.9 us -> 74.8 us (0.986)
  starting transfers between devices: 24.7 us -> 23.2 us
  blocking collectives: 10.1 us -> 11 us
    ppermute x14, starting transfers between devices: 24.6 us -> 23.2 us  [permuted(): lax.ppermute(block, 'section', [(place, place ^ step) for place in range(...]
    all_to_all x1, blocking collectives: 10.1 us -> 11 us  [factored_steps(): totals = lax.all_to_all(total, ('section', 'sub'), 0, 0, tiled=True)]
  transfers between devices with their start and end apart: 16 -> 16, of which waited for: 6 -> 5; matrix products, arithmetic and copies ran while one was open for 2% -> 2% of each run, Pallas kernels for 14% -> 14%
where the time goes in v4:
time: 74.8 us; the launch traced here: 74.6 us
  starting transfers between devices  23.2 us (31%)
  waiting for transfers between devices  22.5 us (30%)
  Pallas kernels  14.7 us (20%)
  blocking collectives  11 us (15%)
  other arithmetic  2.22 us (3%)
  between operations  0.86 us (1%)
    ppermute x14, starting transfers between devices, permuted(): lax.ppermute(block, 'section', [(place, place ^ step) for place in range(...  23.2 us
    ppermute x14, waiting for transfers between devices, permuted(): lax.ppermute(block, 'section', [(place, place ^ step) for place in range(...  22.5 us
    all_to_all x1, blocking collectives, factored_steps(): totals = lax.all_to_all(total, ('section', 'sub'), 0, 0, tiled=True)  11 us
    pallas_call x1, Pallas kernels, weights_kernel(): pl.pallas_call(body, in_specs=[VMEM] * 3 + [SMEM] * 2, out_specs=[VMEM] *...  5.25 us
    pallas_call x2, Pallas kernels, doppler(): pl.pallas_call(body, in_specs=[HBM] * 3, out_specs=[VMEM] * len(outs), ou...  4.26 us
    pallas_call x1, Pallas kernels, near_kernel(): pl.pallas_call(body, in_specs=[VMEM] * (len(steps) + 4) + [SMEM], out_spe...  3 us
    pallas_call x1, Pallas kernels, beams_kernel(): pl.pallas_call(body, in_specs=[VMEM] * (len(steps) + 6) + [SMEM], out_spe...  2.03 us
  transfers between devices with their start and end apart: 16, of which 5 were waited for; matrix products, arithmetic and copies ran while one was open for 2% of the time, Pallas kernels for 14%

profile of v4, /device:TPU:0, one launch (start us, length us, event | category | flops | bytes accessed | tf_op | source)
XLA Modules:
  0.0 74.6 jit_solution(15418268993311085094)
XLA Ops:
  0.0 0.0 copy-start.1
  0.0 2.1 %shard_map.83 = (f32[2,4,32,128]{3,2,1,0:T(8,128)S(1)}, f32[2,4,32,128]{3,2,1,0:T(8,128)S(1)}, f32[2,4,32,128]{3,2,1,0:T(8,128)S(1)}, f32[2,4,32,128]{3,2,1,0:T(...) custom-call(f32[2,3,512,128]{3,2,1,0:T(8,128)} %bitcast.26, ...), custom_call_target="tpu_custom_call" | custom-call | tf_op jit(solution)/shard_map/pallas_call | solution.py:142
  2.2 4.0 %collective-permute-start.10 = (f32[2,4,32,128]{3,2,1,0:T(8,128)S(1)}, f32[2,4,32,128]{3,2,1,0:T(8,128)S(1)}, u32[]{:S(2)}, u32[]{:S(2)}) collective-permute-start(f32[2,4,32,128]{3,2,1,0:T(8,128)S(1)} %get-tuple-element.44), channel_id=1, source_target_pairs={{0,6},{2,4},{4,2},{6,0},{8,14},{10,12},{12,10},{14,8},{1,7},{3,5},... | collective-permute-start | bytes 393224 | tf_op jit(solution)/shard_map/ppermute | solution.py:504
  6.2 2.6 %collective-permute-start.11 = (f32[2,4,32,128]{3,2,1,0:T(8,128)S(1)}, f32[2,4,32,128]{3,2,1,0:T(8,128)S(1)}, u32[]{:S(2)}, u32[]{:S(2)}) collective-permute-start(f32[2,4,32,128]{3,2,1,0:T(8,128)S(1)} %get-tuple-element.45), channel_id=1, source_target_pairs={{0,8},{2,10},{4,12},{6,14},{8,0},{10,2},{12,4},{14,6},{1,9},{3,11}... | collective-permute-start | bytes 393224 | tf_op jit(solution)/shard_map/ppermute | solution.py:504
  8.8 0.3 collective-permute-start.12
  9.1 2.5 %collective-permute-start.13 = (f32[2,4,32,128]{3,2,1,0:T(8,128)S(1)}, f32[2,4,32,128]{3,2,1,0:T(8,128)S(1)}, u32[]{:S(2)}, u32[]{:S(2)}) collective-permute-start(f32[2,4,32,128]{3,2,1,0:T(8,128)S(1)} %get-tuple-element.47), channel_id=1, source_target_pairs={{0,12},{2,14},{4,8},{6,10},{8,4},{10,6},{12,0},{14,2},{1,13},{3,15... | collective-permute-start | bytes 393224 | tf_op jit(solution)/shard_map/ppermute | solution.py:504
  11.6 2.3 %collective-permute-start.14 = (f32[2,4,32,128]{3,2,1,0:T(8,128)S(1)}, f32[2,4,32,128]{3,2,1,0:T(8,128)S(1)}, u32[]{:S(2)}, u32[]{:S(2)}) collective-permute-start(f32[2,4,32,128]{3,2,1,0:T(8,128)S(1)} %get-tuple-element.48), channel_id=1, source_target_pairs={{0,14},{2,12},{4,10},{6,8},{8,6},{10,4},{12,2},{14,0},{1,15},{3,13... | collective-permute-start | bytes 393224 | tf_op jit(solution)/shard_map/ppermute | solution.py:504
  13.9 2.1 %shard_map.82 = (f32[8,2,4,16,128]{4,3,2,1,0:T(8,128)S(1)}, f32[8,2,4,16,128]{4,3,2,1,0:T(8,128)S(1)}) custom-call(f32[2,3,512,128]{3,2,1,0:T(8,128)} %bitcast.27, f32[2,128]{1,0:T(2,128)} %bitcast.29, bf16[4,128,256]{2,1,0:T(8,128)(2,1)} %constant.32.clone.table_ref), custom_call_target="tpu_custom_call" | custom-call | tf_op jit(solution)/shard_map/pallas_call | solution.py:142
  16.0 0.0 copy-done.1
  16.0 0.0 collective-permute-done.10.refs_3_
  16.0 0.6 collective-permute-start.8
  16.6 7.8 %collective-permute-done.11.refs_4_ = f32[2,4,32,128]{3,2,1,0:T(8,128)S(1)} collective-permute-done((f32[2,4,32,128]{3,2,1,0:T(8,128)S(1)}, f32[2,4,32,128]{3,2,1,0:T(8,128)S(1)}, u32[]{:S(2)}, u32[]{:S(2)}) %collective-permute-start.11) | collective-permute-done | bytes 131104 | tf_op jit(solution)/shard_map/ppermute | solution.py:504
  24.4 0.0 collective-permute-start.9
  24.4 2.3 %collective-permute-done.12.refs_5_ = f32[2,4,32,128]{3,2,1,0:T(8,128)S(1)} collective-permute-done((f32[2,4,32,128]{3,2,1,0:T(8,128)S(1)}, f32[2,4,32,128]{3,2,1,0:T(8,128)S(1)}, u32[]{:S(2)}, u32[]{:S(2)}) %collective-permute-start.12) | collective-permute-done | bytes 131104 | tf_op jit(solution)/shard_map/ppermute | solution.py:504
  26.7 0.0 collective-permute-start
  26.7 0.0 collective-permute-done.13.refs_6_
  26.7 0.0 collective-permute-done.14.refs_7_
  26.7 0.0 collective-permute-done.8.refs_1_
  26.7 2.6 %collective-permute-done.9.refs_2_ = f32[2,4,32,128]{3,2,1,0:T(8,128)S(1)} collective-permute-done((f32[2,4,32,128]{3,2,1,0:T(8,128)S(1)}, f32[2,4,32,128]{3,2,1,0:T(8,128)S(1)}, u32[]{:S(2)}, u32[]{:S(2)}) %collective-permute-start.9) | collective-permute-done | bytes 131104 | tf_op jit(solution)/shard_map/ppermute | solution.py:504
  29.4 0.1 gather_sub.1
  29.5 0.1 collective-permute-start.15
  29.6 0.0 copy-done.2
  29.6 1.0 %fusion.4 = (f32[256,256]{1,0:T(8,128)S(1)}, f32[256,256]{1,0:T(8,128)S(1)}, f32[256,256]{1,0:T(8,128)S(1)}) fusion(f32[256]{0:T(256)S(1)} %get-tuple-element.65, f32[256]{0:T(256)S(1)} %multiply_add_fusion.2, f32[256]{0:T(256)S(1)} %get-tuple-element.64), kind=kLoop, calls=%fused_computation.10 | loop fusion | flops 196608 | bytes 789504 | tf_op jit(solution)/shard_map/neg | solution.py:495
  30.6 0.0 collective-permute-done.other_ref
  30.6 0.1 pair_up.1
  30.7 0.2 collective-permute-start.3
  30.9 4.4 %collective-permute-start.4 = (f32[2,2,4,16,128]{4,3,2,1,0:T(8,128)S(1)}, f32[2,2,4,16,128]{4,3,2,1,0:T(8,128)S(1)}, u32[]{:S(2)}, u32[]{:S(2)}) collective-permute-start(f32[2,2,4,16,128]{4,3,2,1,0:T(8,128)S(1)} %get-tuple-element.37), channel_id=1, source_target_pairs={{0,4},{2,6},{4,0},{6,2},{8,12},{10,14},{12,8},{14,10},{1,5},{3,7},... | collective-permute-start | bytes 393224 | tf_op jit(solution)/shard_map/ppermute | solution.py:504
  35.2 0.1 reduce-precision_convert_fusion
  35.4 0.1 collective-permute-start.5
  35.5 2.9 %collective-permute-start.6 = (f32[2,2,4,16,128]{4,3,2,1,0:T(8,128)S(1)}, f32[2,2,4,16,128]{4,3,2,1,0:T(8,128)S(1)}, u32[]{:S(2)}, u32[]{:S(2)}) collective-permute-start(f32[2,2,4,16,128]{4,3,2,1,0:T(8,128)S(1)} %get-tuple-element.39), channel_id=1, source_target_pairs={{0,8},{2,10},{4,12},{6,14},{8,0},{10,2},{12,4},{14,6},{1,9},{3,11}... | collective-permute-start | bytes 393224 | tf_op jit(solution)/shard_map/ppermute | solution.py:504
  38.4 0.0 collective-permute-done.15
  38.4 0.9 %collective-permute-start.7 = (f32[2,2,4,16,128]{4,3,2,1,0:T(8,128)S(1)}, f32[2,2,4,16,128]{4,3,2,1,0:T(8,128)S(1)}, u32[]{:S(2)}, u32[]{:S(2)}) collective-permute-start(f32[2,2,4,16,128]{4,3,2,1,0:T(8,128)S(1)} %get-tuple-element.40), channel_id=1, source_target_pairs={{0,10},{2,8},{4,14},{6,12},{8,2},{10,0},{12,6},{14,4},{1,11},{3,9}... | collective-permute-start | bytes 393224 | tf_op jit(solution)/shard_map/ppermute | solution.py:504
  39.4 0.0 collective-permute-done.3
  39.4 2.4 %collective-permute-start.1 = (f32[2,2,4,16,128]{4,3,2,1,0:T(8,128)S(1)}, f32[2,2,4,16,128]{4,3,2,1,0:T(8,128)S(1)}, u32[]{:S(2)}, u32[]{:S(2)}) collective-permute-start(f32[2,2,4,16,128]{4,3,2,1,0:T(8,128)S(1)} %get-tuple-element.33), channel_id=1, source_target_pairs={{0,12},{2,14},{4,8},{6,10},{8,4},{10,6},{12,0},{14,2},{1,13},{3,15... | collective-permute-start | bytes 393224 | tf_op jit(solution)/shard_map/ppermute | solution.py:504
  41.7 1.9 %collective-permute-done.4 = f32[2,2,4,16,128]{4,3,2,1,0:T(8,128)S(1)} collective-permute-done((f32[2,2,4,16,128]{4,3,2,1,0:T(8,128)S(1)}, f32[2,2,4,16,128]{4,3,2,1,0:T(8,128)S(1)}, u32[]{:S(2)}, u32[]{:S(2)}) %collective-permute-start.4) | collective-permute-done | bytes 131104 | tf_op jit(solution)/shard_map/ppermute | solution.py:504
  43.7 0.0 collective-permute-start.2
  43.7 0.1 pad_maximum_fusion.steer_ref.refs_9_.refs_7_
  44.4 0.0 copy-done
  44.5 5.2 %weights.1 = (bf16[16,128,512]{2,1,0:T(8,128)(2,1)S(1)}, bf16[16,64,512]{2,1,0:T(8,128)(2,1)S(1)}, bf16[16,64,512]{2,1,0:T(8,128)(2,1)S(1)}, f32[16,256]{1,0:T(8,128)S(1)}) custom-call(f32[1024,128]{1,0:T(8,128)S(1)} %bitcast.15, f32[1024,128]{1,0:T(8,128)S(1)} %bitcast.16, bf16[1536,512]{1,0:T(8,128)(2,1)S(1)} %pad_maximum_fusion.steer_ref.refs_9_.refs_7_, ...), custom_call_target="tpu_custom_call" | custom-call | tf_op jit(solution)/shard_map/weights/pallas_call | solution.py:336
  49.7 0.0 collective-permute-done.5
  49.7 0.0 collective-permute-done.6
  49.7 7.8 %collective-permute-done.7 = f32[2,2,4,16,128]{4,3,2,1,0:T(8,128)S(1)} collective-permute-done((f32[2,2,4,16,128]{4,3,2,1,0:T(8,128)S(1)}, f32[2,2,4,16,128]{4,3,2,1,0:T(8,128)S(1)}, u32[]{:S(2)}, u32[]{:S(2)}) %collective-permute-start.7) | collective-permute-done | bytes 131104 | tf_op jit(solution)/shard_map/ppermute | solution.py:504
  57.6 3.0 %near.1.refs_2_ = f32[16,64,256]{2,1,0:T(8,128)S(1)} custom-call(f32[256,128]{1,0:T(8,128)S(1)} %bitcast.17, f32[256,128]{1,0:T(8,128)S(1)} %bitcast.18, f32[256,128]{1,0:T(8,128)S(1)} %bitcast.19, f32[256,128]{1,0:T(8,128)S(1)} %bitcast.20, f32[256,128]{1,0:T(8,128)S(1)} %bitcast.21, f32[256,128]{1,0:T(8,128)S(1)} %bitcast.22, ...), custom_call_target="tpu_custom_call" | custom-call | tf_op jit(solution)/shard_map/near/pallas_call | solution.py:401
  60.6 0.0 collective-permute-done.1
  60.6 0.0 collective-permute-done.2
  60.6 2.0 %beams.1 = (f32[16,32,256]{2,1,0:T(8,128)S(1)}, f32[16,256]{1,0:T(8,128)S(1)}) custom-call(f32[256,128]{1,0:T(8,128)S(1)} %bitcast.23, f32[256,128]{1,0:T(8,128)S(1)} %bitcast.24, f32[16,64,256]{2,1,0:T(8,128)S(1)} %near.1.refs_2_, bf16[16,128,512]{2,1,0:T(8,128)(2,1)S(1)} %get-tuple-element.51.refs_6_.refs_3_, ...), custom_call_target="tpu_custom_call" | custom-call | tf_op jit(solution)/shard_map/beams/pallas_call | solution.py:469
  62.7 11.0 %all_to_all.9 = f32[16,1,256]{2,1,0:T(1,128)S(1)} all-to-all(f32[16,1,256]{2,1,0:T(1,128)S(1)} %copy.9), channel_id=1, replica_groups=mesh['groups'=2,'section'=8,'sub'=2] {'section','sub'}, dimensions={0} | all-to-all | bytes 32768 | tf_op jit(solution)/shard_map/all_to_all | solution.py:544
  73.7 0.9 %divide_bitcast_fusion = f32[1,16,32,256]{3,2,1,0:T(8,128)} fusion(f32[16,32,256]{2,1,0:T(8,128)S(1)} %get-tuple-element.55, f32[256]{0:T(256)S(1)} %multiply_add_fusion.1), kind=kLoop, calls=%fused_computation.6 | loop fusion | flops 131072 | bytes 1049600 | tf_op jit(solution)/shard_map/broadcast_in_dim | solution.py:546
  (8 shorter events, 0.1 us)
Async XLA Ops:
  0.0 16.0 %copy-start.1 = (f32[256]{0:T(256)S(1)}, f32[256]{0:T(256)}, u32[]{:S(2)}) copy-start(f32[256]{0:T(256)} %param.11) | copy-start | bytes 3076
  0.0 29.6 %copy-start.2 = (s32[256]{0:T(256)S(1)}, s32[256]{0:T(256)}, u32[]{:S(2)}) copy-start(s32[256]{0:T(256)} %param.13) | copy-start | bytes 3076
  2.2 13.9 %collective-permute-start.10 = (f32[2,4,32,128]{3,2,1,0:T(8,128)S(1)}, f32[2,4,32,128]{3,2,1,0:T(8,128)S(1)}, u32[]{:S(2)}, u32[]{:S(2)}) collective-permute-start(f32[2,4,32,128]{3,2,1,0:T(8,128)S(1)} %get-tuple-element.44), channel_id=1, source_target_pairs={{0,6},{2,4},{4,2},{6,0},{8,14},{10,12},{12,10},{14,8},{1,7},{3,5},... | collective-permute-start | bytes 393224 | tf_op jit(solution)/shard_map/ppermute | solution.py:504
  6.2 18.2 %collective-permute-start.11 = (f32[2,4,32,128]{3,2,1,0:T(8,128)S(1)}, f32[2,4,32,128]{3,2,1,0:T(8,128)S(1)}, u32[]{:S(2)}, u32[]{:S(2)}) collective-permute-start(f32[2,4,32,128]{3,2,1,0:T(8,128)S(1)} %get-tuple-element.45), channel_id=1, source_target_pairs={{0,8},{2,10},{4,12},{6,14},{8,0},{10,2},{12,4},{14,6},{1,9},{3,11}... | collective-permute-start | bytes 393224 | tf_op jit(solution)/shard_map/ppermute | solution.py:504
  8.8 17.9 %collective-permute-start.12 = (f32[2,4,32,128]{3,2,1,0:T(8,128)S(1)}, f32[2,4,32,128]{3,2,1,0:T(8,128)S(1)}, u32[]{:S(2)}, u32[]{:S(2)}) collective-permute-start(f32[2,4,32,128]{3,2,1,0:T(8,128)S(1)} %get-tuple-element.46), channel_id=1, source_target_pairs={{0,10},{2,8},{4,14},{6,12},{8,2},{10,0},{12,6},{14,4},{1,11},{3,9}... | collective-permute-start | bytes 393224 | tf_op jit(solution)/shard_map/ppermute | solution.py:504
  9.1 17.6 %collective-permute-start.13 = (f32[2,4,32,128]{3,2,1,0:T(8,128)S(1)}, f32[2,4,32,128]{3,2,1,0:T(8,128)S(1)}, u32[]{:S(2)}, u32[]{:S(2)}) collective-permute-start(f32[2,4,32,128]{3,2,1,0:T(8,128)S(1)} %get-tuple-element.47), channel_id=1, source_target_pairs={{0,12},{2,14},{4,8},{6,10},{8,4},{10,6},{12,0},{14,2},{1,13},{3,15... | collective-permute-start | bytes 393224 | tf_op jit(solution)/shard_map/ppermute | solution.py:504
  11.6 15.1 %collective-permute-start.14 = (f32[2,4,32,128]{3,2,1,0:T(8,128)S(1)}, f32[2,4,32,128]{3,2,1,0:T(8,128)S(1)}, u32[]{:S(2)}, u32[]{:S(2)}) collective-permute-start(f32[2,4,32,128]{3,2,1,0:T(8,128)S(1)} %get-tuple-element.48), channel_id=1, source_target_pairs={{0,14},{2,12},{4,10},{6,8},{8,6},{10,4},{12,2},{14,0},{1,15},{3,13... | collective-permute-start | bytes 393224 | tf_op jit(solution)/shard_map/ppermute | solution.py:504
  16.0 10.7 %collective-permute-start.8 = (f32[2,4,32,128]{3,2,1,0:T(8,128)S(1)}, f32[2,4,32,128]{3,2,1,0:T(8,128)S(1)}, u32[]{:S(2)}, u32[]{:S(2)}) collective-permute-start(f32[2,4,32,128]{3,2,1,0:T(8,128)S(1)} %get-tuple-element.42), channel_id=1, source_target_pairs={{0,2},{2,0},{4,6},{6,4},{8,10},{10,8},{12,14},{14,12},{1,3},{3,1},... | collective-permute-start | bytes 393224 | tf_op jit(solution)/shard_map/ppermute | solution.py:504
  24.4 5.0 %collective-permute-start.9 = (f32[2,4,32,128]{3,2,1,0:T(8,128)S(1)}, f32[2,4,32,128]{3,2,1,0:T(8,128)S(1)}, u32[]{:S(2)}, u32[]{:S(2)}) collective-permute-start(f32[2,4,32,128]{3,2,1,0:T(8,128)S(1)} %get-tuple-element.43), channel_id=1, source_target_pairs={{0,4},{2,6},{4,0},{6,2},{8,12},{10,14},{12,8},{14,10},{1,5},{3,7},... | collective-permute-start | bytes 393224 | tf_op jit(solution)/shard_map/ppermute | solution.py:504
  26.7 3.9 %collective-permute-start = (f32[8,2,4,16,128]{4,3,2,1,0:T(8,128)S(1)}, f32[8,2,4,16,128]{4,3,2,1,0:T(8,128)S(1)}, u32[]{:S(2)}, u32[]{:S(2)}) collective-permute-start(f32[8,2,4,16,128]{4,3,2,1,0:T(8,128)S(1)} %get-tuple-element.32), channel_id=1, source_target_pairs={{0,1},{1,0},{2,3},{3,2},{4,5},{5,4},{6,7},{7,6},{8,9},{9,8},{10,11... | collective-permute-start | bytes 1572872 | tf_op jit(solution)/shard_map/ppermute | solution.py:508
  29.5 8.9 %collective-permute-start.15 = (f32[8,2,4,16,128]{4,3,2,1,0:T(8,128)S(1)}, f32[8,2,4,16,128]{4,3,2,1,0:T(8,128)S(1)}, u32[]{:S(2)}, u32[]{:S(2)}) collective-permute-start(f32[8,2,4,16,128]{4,3,2,1,0:T(8,128)S(1)} %get-tuple-element.50), channel_id=1, source_target_pairs={{0,1},{1,0},{2,3},{3,2},{4,5},{5,4},{6,7},{7,6},{8,9},{9,8},{10,11... | collective-permute-start | bytes 1572872 | tf_op jit(solution)/shard_map/ppermute | solution.py:508
  30.7 8.7 %collective-permute-start.3 = (f32[2,2,4,16,128]{4,3,2,1,0:T(8,128)S(1)}, f32[2,2,4,16,128]{4,3,2,1,0:T(8,128)S(1)}, u32[]{:S(2)}, u32[]{:S(2)}) collective-permute-start(f32[2,2,4,16,128]{4,3,2,1,0:T(8,128)S(1)} %get-tuple-element.36), channel_id=1, source_target_pairs={{0,2},{2,0},{4,6},{6,4},{8,10},{10,8},{12,14},{14,12},{1,3},{3,1},... | collective-permute-start | bytes 393224 | tf_op jit(solution)/shard_map/ppermute | solution.py:504
  30.9 12.8 %collective-permute-start.4 = (f32[2,2,4,16,128]{4,3,2,1,0:T(8,128)S(1)}, f32[2,2,4,16,128]{4,3,2,1,0:T(8,128)S(1)}, u32[]{:S(2)}, u32[]{:S(2)}) collective-permute-start(f32[2,2,4,16,128]{4,3,2,1,0:T(8,128)S(1)} %get-tuple-element.37), channel_id=1, source_target_pairs={{0,4},{2,6},{4,0},{6,2},{8,12},{10,14},{12,8},{14,10},{1,5},{3,7},... | collective-permute-start | bytes 393224 | tf_op jit(solution)/shard_map/ppermute | solution.py:504
  35.2 9.2 %copy-start = (f32[2,5]{1,0:T(2,128)S(1)}, f32[2,5]{1,0:T(2,128)}, u32[]{:S(2)}) copy-start(f32[2,5]{1,0:T(2,128)} %refs_8_.1) | copy-start | bytes 124
  35.4 14.3 %collective-permute-start.5 = (f32[2,2,4,16,128]{4,3,2,1,0:T(8,128)S(1)}, f32[2,2,4,16,128]{4,3,2,1,0:T(8,128)S(1)}, u32[]{:S(2)}, u32[]{:S(2)}) collective-permute-start(f32[2,2,4,16,128]{4,3,2,1,0:T(8,128)S(1)} %get-tuple-element.38), channel_id=1, source_target_pairs={{0,6},{2,4},{4,2},{6,0},{8,14},{10,12},{12,10},{14,8},{1,7},{3,5},... | collective-permute-start | bytes 393224 | tf_op jit(solution)/shard_map/ppermute | solution.py:504
  35.5 14.2 %collective-permute-start.6 = (f32[2,2,4,16,128]{4,3,2,1,0:T(8,128)S(1)}, f32[2,2,4,16,128]{4,3,2,1,0:T(8,128)S(1)}, u32[]{:S(2)}, u32[]{:S(2)}) collective-permute-start(f32[2,2,4,16,128]{4,3,2,1,0:T(8,128)S(1)} %get-tuple-element.39), channel_id=1, source_target_pairs={{0,8},{2,10},{4,12},{6,14},{8,0},{10,2},{12,4},{14,6},{1,9},{3,11}... | collective-permute-start | bytes 393224 | tf_op jit(solution)/shard_map/ppermute | solution.py:504
  38.4 19.1 %collective-permute-start.7 = (f32[2,2,4,16,128]{4,3,2,1,0:T(8,128)S(1)}, f32[2,2,4,16,128]{4,3,2,1,0:T(8,128)S(1)}, u32[]{:S(2)}, u32[]{:S(2)}) collective-permute-start(f32[2,2,4,16,128]{4,3,2,1,0:T(8,128)S(1)} %get-tuple-element.40), channel_id=1, source_target_pairs={{0,10},{2,8},{4,14},{6,12},{8,2},{10,0},{12,6},{14,4},{1,11},{3,9}... | collective-permute-start | bytes 393224 | tf_op jit(solution)/shard_map/ppermute | solution.py:504
  39.4 21.2 %collective-permute-start.1 = (f32[2,2,4,16,128]{4,3,2,1,0:T(8,128)S(1)}, f32[2,2,4,16,128]{4,3,2,1,0:T(8,128)S(1)}, u32[]{:S(2)}, u32[]{:S(2)}) collective-permute-start(f32[2,2,4,16,128]{4,3,2,1,0:T(8,128)S(1)} %get-tuple-element.33), channel_id=1, source_target_pairs={{0,12},{2,14},{4,8},{6,10},{8,4},{10,6},{12,0},{14,2},{1,13},{3,15... | collective-permute-start | bytes 393224 | tf_op jit(solution)/shard_map/ppermute | solution.py:504
  43.7 16.9 %collective-permute-start.2 = (f32[2,2,4,16,128]{4,3,2,1,0:T(8,128)S(1)}, f32[2,2,4,16,128]{4,3,2,1,0:T(8,128)S(1)}, u32[]{:S(2)}, u32[]{:S(2)}) collective-permute-start(f32[2,2,4,16,128]{4,3,2,1,0:T(8,128)S(1)} %get-tuple-element.34), channel_id=1, source_target_pairs={{0,14},{2,12},{4,10},{6,8},{8,6},{10,4},{12,2},{14,0},{1,15},{3,13... | collective-permute-start | bytes 393224 | tf_op jit(solution)/shard_map/ppermute | solution.py:504

commit v5 on v4

--- a/solution.py
+++ b/solution.py
@@ -480,6 +480,33 @@
     )(*[blocks[step].reshape(size, LANES) for step in steps], near, *weights, steer, range_taps)
 
 
+def scaled(power, totals, samples):
+    own, chunks = power.shape[0], 4
+    each = own // chunks
+
+    def body(power_ref, totals_ref, out_ref, held, sems):
+        noise_level = jnp.sum(totals_ref[...], axis=0, keepdims=True) / samples
+        factor = 1.0 / (noise_level + epsilon)
+        copies = []
+        for chunk in range(chunks):
+            here = pl.ds(chunk * each, each)
+            held[here] = power_ref[here] * factor[None]
+            copies.append(pltpu.make_async_copy(held.at[here], out_ref.at[here], sems.at[chunk]))
+            copies[-1].start()
+        for copy in copies:
+            copy.wait()
+
+    return pl.pallas_call(
+        body,
+        in_specs=[VMEM] * 2,
+        out_specs=HBM,
+        out_shape=jax.ShapeDtypeStruct(power.shape, F32),
+        scratch_shapes=[pltpu.VMEM(power.shape, F32), pltpu.SemaphoreType.DMA((chunks,))],
+        compiler_params=pltpu.CompilerParams(vmem_limit_bytes=LIMIT),
+        name="scaled",
+    )(power, totals)
+
+
 def steering_tables(beam_index, channel_phase):
     channels = channel_phase.shape[0]
     own = channels // 2
@@ -542,8 +569,7 @@
     blocks = {step: later[step] for step in last}
     power, total = beams_kernel(blocks, near, weights, steer, range_taps)
     totals = lax.all_to_all(total, ("section", "sub"), 0, 0, tiled=True)
-    noise_level = jnp.sum(totals, axis=0) / (PULSES * gates * sections)
-    return (power / (noise_level + epsilon))[None]
+    return scaled(power, totals, PULSES * gates * sections)[None]
 
 
 def apply_taps(pad_real, pad_imag, range_taps, gate_count):

time: 74.8 us -> 74.7 us (level)
  other arithmetic: 2.22 us -> 1.3 us
  Pallas kernels: 14.7 us -> 15.6 us
    broadcast_in_dim x1 -> x0, other arithmetic: 0.87 us -> none  [factored_steps(): return (power / (noise_level + epsilon))[None]]
    pallas_call x0 -> x1, Pallas kernels: none -> 0.85 us  [scaled(): pl.pallas_call(body, in_specs=[VMEM] * 2, out_specs=HBM, out_shape=jax.Sh...]
where the time goes in v5:
time: 74.7 us; the launch traced here: 74.5 us
  starting transfers between devices  23.2 us (31%)
  waiting for transfers between devices  22.5 us (30%)
  Pallas kernels  15.6 us (21%)
  blocking collectives  11 us (15%)
  other arithmetic  1.3 us (2%)
  between operations  0.86 us (1%)
    ppermute x14, starting transfers between devices, permuted(): lax.ppermute(block, 'section', [(place, place ^ step) for place in range(...  23.2 us
    ppermute x14, waiting for transfers between devices, permuted(): lax.ppermute(block, 'section', [(place, place ^ step) for place in range(...  22.5 us
    all_to_all x1, blocking collectives, factored_steps(): totals = lax.all_to_all(total, ('section', 'sub'), 0, 0, tiled=True)  11 us
    pallas_call x1, Pallas kernels, weights_kernel(): pl.pallas_call(body, in_specs=[VMEM] * 3 + [SMEM] * 2, out_specs=[VMEM] *...  5.25 us
    pallas_call x2, Pallas kernels, doppler(): pl.pallas_call(body, in_specs=[HBM] * 3, out_specs=[VMEM] * len(outs), ou...  4.26 us
    pallas_call x1, Pallas kernels, near_kernel(): pl.pallas_call(body, in_specs=[VMEM] * (len(steps) + 4) + [SMEM], out_spe...  3 us
    pallas_call x1, Pallas kernels, beams_kernel(): pl.pallas_call(body, in_specs=[VMEM] * (len(steps) + 6) + [SMEM], out_spe...  2.03 us
  transfers between devices with their start and end apart: 16, of which 5 were waited for; matrix products, arithmetic and copies ran while one was open for 2% of the time, Pallas kernels for 14%

profile of v5, /device:TPU:0, one launch (start us, length us, event | category | flops | bytes accessed | tf_op | source)
XLA Modules:
  0.0 74.5 jit_solution(10952167350709954819)
XLA Ops:
  0.0 0.0 copy-start.1
  0.0 2.1 %shard_map.83 = (f32[2,4,32,128]{3,2,1,0:T(8,128)S(1)}, f32[2,4,32,128]{3,2,1,0:T(8,128)S(1)}, f32[2,4,32,128]{3,2,1,0:T(8,128)S(1)}, f32[2,4,32,128]{3,2,1,0:T(...) custom-call(f32[2,3,512,128]{3,2,1,0:T(8,128)} %bitcast.29, ...), custom_call_target="tpu_custom_call" | custom-call | tf_op jit(solution)/shard_map/pallas_call | solution.py:142
  2.2 4.0 %collective-permute-start.10 = (f32[2,4,32,128]{3,2,1,0:T(8,128)S(1)}, f32[2,4,32,128]{3,2,1,0:T(8,128)S(1)}, u32[]{:S(2)}, u32[]{:S(2)}) collective-permute-start(f32[2,4,32,128]{3,2,1,0:T(8,128)S(1)} %get-tuple-element.44), channel_id=1, source_target_pairs={{0,6},{2,4},{4,2},{6,0},{8,14},{10,12},{12,10},{14,8},{1,7},{3,5},... | collective-permute-start | bytes 393224 | tf_op jit(solution)/shard_map/ppermute | solution.py:531
  6.2 2.6 %collective-permute-start.11 = (f32[2,4,32,128]{3,2,1,0:T(8,128)S(1)}, f32[2,4,32,128]{3,2,1,0:T(8,128)S(1)}, u32[]{:S(2)}, u32[]{:S(2)}) collective-permute-start(f32[2,4,32,128]{3,2,1,0:T(8,128)S(1)} %get-tuple-element.45), channel_id=1, source_target_pairs={{0,8},{2,10},{4,12},{6,14},{8,0},{10,2},{12,4},{14,6},{1,9},{3,11}... | collective-permute-start | bytes 393224 | tf_op jit(solution)/shard_map/ppermute | solution.py:531
  8.8 0.3 collective-permute-start.12
  9.1 2.5 %collective-permute-start.13 = (f32[2,4,32,128]{3,2,1,0:T(8,128)S(1)}, f32[2,4,32,128]{3,2,1,0:T(8,128)S(1)}, u32[]{:S(2)}, u32[]{:S(2)}) collective-permute-start(f32[2,4,32,128]{3,2,1,0:T(8,128)S(1)} %get-tuple-element.47), channel_id=1, source_target_pairs={{0,12},{2,14},{4,8},{6,10},{8,4},{10,6},{12,0},{14,2},{1,13},{3,15... | collective-permute-start | bytes 393224 | tf_op jit(solution)/shard_map/ppermute | solution.py:531
  11.6 2.3 %collective-permute-start.14 = (f32[2,4,32,128]{3,2,1,0:T(8,128)S(1)}, f32[2,4,32,128]{3,2,1,0:T(8,128)S(1)}, u32[]{:S(2)}, u32[]{:S(2)}) collective-permute-start(f32[2,4,32,128]{3,2,1,0:T(8,128)S(1)} %get-tuple-element.48), channel_id=1, source_target_pairs={{0,14},{2,12},{4,10},{6,8},{8,6},{10,4},{12,2},{14,0},{1,15},{3,13... | collective-permute-start | bytes 393224 | tf_op jit(solution)/shard_map/ppermute | solution.py:531
  13.9 2.1 %shard_map.82 = (f32[8,2,4,16,128]{4,3,2,1,0:T(8,128)S(1)}, f32[8,2,4,16,128]{4,3,2,1,0:T(8,128)S(1)}) custom-call(f32[2,3,512,128]{3,2,1,0:T(8,128)} %bitcast.30, f32[2,128]{1,0:T(2,128)} %bitcast.32, bf16[4,128,256]{2,1,0:T(8,128)(2,1)} %constant.25.clone.table_ref), custom_call_target="tpu_custom_call" | custom-call | tf_op jit(solution)/shard_map/pallas_call | solution.py:142
  16.0 0.0 copy-done.1
  16.0 0.0 collective-permute-done.10.refs_3_
  16.0 0.6 collective-permute-start.8
  16.6 7.8 %collective-permute-done.11.refs_4_ = f32[2,4,32,128]{3,2,1,0:T(8,128)S(1)} collective-permute-done((f32[2,4,32,128]{3,2,1,0:T(8,128)S(1)}, f32[2,4,32,128]{3,2,1,0:T(8,128)S(1)}, u32[]{:S(2)}, u32[]{:S(2)}) %collective-permute-start.11) | collective-permute-done | bytes 131104 | tf_op jit(solution)/shard_map/ppermute | solution.py:531
  24.4 0.0 collective-permute-start.9
  24.4 2.3 %collective-permute-done.12.refs_5_ = f32[2,4,32,128]{3,2,1,0:T(8,128)S(1)} collective-permute-done((f32[2,4,32,128]{3,2,1,0:T(8,128)S(1)}, f32[2,4,32,128]{3,2,1,0:T(8,128)S(1)}, u32[]{:S(2)}, u32[]{:S(2)}) %collective-permute-start.12) | collective-permute-done | bytes 131104 | tf_op jit(solution)/shard_map/ppermute | solution.py:531
  26.7 0.0 collective-permute-start
  26.7 0.0 collective-permute-done.13.refs_6_
  26.7 0.0 collective-permute-done.14.refs_7_
  26.7 0.0 collective-permute-done.8.refs_1_
  26.7 2.6 %collective-permute-done.9.refs_2_ = f32[2,4,32,128]{3,2,1,0:T(8,128)S(1)} collective-permute-done((f32[2,4,32,128]{3,2,1,0:T(8,128)S(1)}, f32[2,4,32,128]{3,2,1,0:T(8,128)S(1)}, u32[]{:S(2)}, u32[]{:S(2)}) %collective-permute-start.9) | collective-permute-done | bytes 131104 | tf_op jit(solution)/shard_map/ppermute | solution.py:531
  29.4 0.1 gather_sub.1
  29.5 0.1 collective-permute-start.15
  29.6 0.0 copy-done.2
  29.6 1.0 %fusion.4 = (f32[256,256]{1,0:T(8,128)S(1)}, f32[256,256]{1,0:T(8,128)S(1)}, f32[256,256]{1,0:T(8,128)S(1)}) fusion(f32[256]{0:T(256)S(1)} %get-tuple-element.65, f32[256]{0:T(256)S(1)} %multiply_add_fusion.1, f32[256]{0:T(256)S(1)} %get-tuple-element.64), kind=kLoop, calls=%fused_computation.9 | loop fusion | flops 196608 | bytes 789504 | tf_op jit(solution)/shard_map/neg | solution.py:522
  30.6 0.0 collective-permute-done.other_ref
  30.6 0.1 pair_up.1
  30.7 0.2 collective-permute-start.3
  30.9 4.4 %collective-permute-start.4 = (f32[2,2,4,16,128]{4,3,2,1,0:T(8,128)S(1)}, f32[2,2,4,16,128]{4,3,2,1,0:T(8,128)S(1)}, u32[]{:S(2)}, u32[]{:S(2)}) collective-permute-start(f32[2,2,4,16,128]{4,3,2,1,0:T(8,128)S(1)} %get-tuple-element.37), channel_id=1, source_target_pairs={{0,4},{2,6},{4,0},{6,2},{8,12},{10,14},{12,8},{14,10},{1,5},{3,7},... | collective-permute-start | bytes 393224 | tf_op jit(solution)/shard_map/ppermute | solution.py:531
  35.2 0.1 reduce-precision_convert_fusion
  35.4 0.1 collective-permute-start.5
  35.5 2.9 %collective-permute-start.6 = (f32[2,2,4,16,128]{4,3,2,1,0:T(8,128)S(1)}, f32[2,2,4,16,128]{4,3,2,1,0:T(8,128)S(1)}, u32[]{:S(2)}, u32[]{:S(2)}) collective-permute-start(f32[2,2,4,16,128]{4,3,2,1,0:T(8,128)S(1)} %get-tuple-element.39), channel_id=1, source_target_pairs={{0,8},{2,10},{4,12},{6,14},{8,0},{10,2},{12,4},{14,6},{1,9},{3,11}... | collective-permute-start | bytes 393224 | tf_op jit(solution)/shard_map/ppermute | solution.py:531
  38.4 0.0 collective-permute-done.15
  38.4 0.9 %collective-permute-start.7 = (f32[2,2,4,16,128]{4,3,2,1,0:T(8,128)S(1)}, f32[2,2,4,16,128]{4,3,2,1,0:T(8,128)S(1)}, u32[]{:S(2)}, u32[]{:S(2)}) collective-permute-start(f32[2,2,4,16,128]{4,3,2,1,0:T(8,128)S(1)} %get-tuple-element.40), channel_id=1, source_target_pairs={{0,10},{2,8},{4,14},{6,12},{8,2},{10,0},{12,6},{14,4},{1,11},{3,9}... | collective-permute-start | bytes 393224 | tf_op jit(solution)/shard_map/ppermute | solution.py:531
  39.4 0.0 collective-permute-done.3
  39.4 2.4 %collective-permute-start.1 = (f32[2,2,4,16,128]{4,3,2,1,0:T(8,128)S(1)}, f32[2,2,4,16,128]{4,3,2,1,0:T(8,128)S(1)}, u32[]{:S(2)}, u32[]{:S(2)}) collective-permute-start(f32[2,2,4,16,128]{4,3,2,1,0:T(8,128)S(1)} %get-tuple-element.33), channel_id=1, source_target_pairs={{0,12},{2,14},{4,8},{6,10},{8,4},{10,6},{12,0},{14,2},{1,13},{3,15... | collective-permute-start | bytes 393224 | tf_op jit(solution)/shard_map/ppermute | solution.py:531
  41.7 1.9 %collective-permute-done.4 = f32[2,2,4,16,128]{4,3,2,1,0:T(8,128)S(1)} collective-permute-done((f32[2,2,4,16,128]{4,3,2,1,0:T(8,128)S(1)}, f32[2,2,4,16,128]{4,3,2,1,0:T(8,128)S(1)}, u32[]{:S(2)}, u32[]{:S(2)}) %collective-permute-start.4) | collective-permute-done | bytes 131104 | tf_op jit(solution)/shard_map/ppermute | solution.py:531
  43.7 0.0 collective-permute-start.2
  43.7 0.1 pad_maximum_fusion.steer_ref.refs_9_.refs_7_
  44.4 0.0 copy-done
  44.5 5.2 %weights.1 = (bf16[16,128,512]{2,1,0:T(8,128)(2,1)S(1)}, bf16[16,64,512]{2,1,0:T(8,128)(2,1)S(1)}, bf16[16,64,512]{2,1,0:T(8,128)(2,1)S(1)}, f32[16,256]{1,0:T(8,128)S(1)}) custom-call(f32[1024,128]{1,0:T(8,128)S(1)} %bitcast.17, f32[1024,128]{1,0:T(8,128)S(1)} %bitcast.18, bf16[1536,512]{1,0:T(8,128)(2,1)S(1)} %pad_maximum_fusion.steer_ref.refs_9_.refs_7_, ...), custom_call_target="tpu_custom_call" | custom-call | tf_op jit(solution)/shard_map/weights/pallas_call | solution.py:336
  49.7 0.0 collective-permute-done.5
  49.7 0.0 collective-permute-done.6
  49.7 7.8 %collective-permute-done.7 = f32[2,2,4,16,128]{4,3,2,1,0:T(8,128)S(1)} collective-permute-done((f32[2,2,4,16,128]{4,3,2,1,0:T(8,128)S(1)}, f32[2,2,4,16,128]{4,3,2,1,0:T(8,128)S(1)}, u32[]{:S(2)}, u32[]{:S(2)}) %collective-permute-start.7) | collective-permute-done | bytes 131104 | tf_op jit(solution)/shard_map/ppermute | solution.py:531
  57.6 3.0 %near.1.refs_2_ = f32[16,64,256]{2,1,0:T(8,128)S(1)} custom-call(f32[256,128]{1,0:T(8,128)S(1)} %bitcast.19, f32[256,128]{1,0:T(8,128)S(1)} %bitcast.20, f32[256,128]{1,0:T(8,128)S(1)} %bitcast.21, f32[256,128]{1,0:T(8,128)S(1)} %bitcast.22, f32[256,128]{1,0:T(8,128)S(1)} %bitcast.23, f32[256,128]{1,0:T(8,128)S(1)} %bitcast.24, ...), custom_call_target="tpu_custom_call" | custom-call | tf_op jit(solution)/shard_map/near/pallas_call | solution.py:401
  60.6 0.0 collective-permute-done.1
  60.6 0.0 collective-permute-done.2
  60.6 2.0 %beams.1 = (f32[16,32,256]{2,1,0:T(8,128)S(1)}, f32[16,256]{1,0:T(8,128)S(1)}) custom-call(f32[256,128]{1,0:T(8,128)S(1)} %bitcast.25, f32[256,128]{1,0:T(8,128)S(1)} %bitcast.26, f32[16,64,256]{2,1,0:T(8,128)S(1)} %near.1.refs_2_, bf16[16,128,512]{2,1,0:T(8,128)(2,1)S(1)} %get-tuple-element.51.refs_6_.refs_3_, ...), custom_call_target="tpu_custom_call" | custom-call | tf_op jit(solution)/shard_map/beams/pallas_call | solution.py:469
  62.7 11.0 %all_to_all.11 = f32[16,1,256]{2,1,0:T(1,128)S(1)} all-to-all(f32[16,1,256]{2,1,0:T(1,128)S(1)} %copy.9), channel_id=1, replica_groups=mesh['groups'=2,'section'=8,'sub'=2] {'section','sub'}, dimensions={0} | all-to-all | bytes 32768 | tf_op jit(solution)/shard_map/all_to_all | solution.py:571
  73.6 0.8 %scaled.1 = f32[16,32,256]{2,1,0:T(8,128)} custom-call(f32[16,32,256]{2,1,0:T(8,128)S(1)} %get-tuple-element.55.power_ref, f32[16,256]{1,0:T(8,128)S(1)} %bitcast.27), custom_call_target="tpu_custom_call" | custom-call | tf_op jit(solution)/shard_map/scaled/pallas_call | solution.py:499
  (7 shorter events, 0.0 us)
Async XLA Ops:
  0.0 16.0 %copy-start.1 = (f32[256]{0:T(256)S(1)}, f32[256]{0:T(256)}, u32[]{:S(2)}) copy-start(f32[256]{0:T(256)} %param.11) | copy-start | bytes 3076
  0.0 29.6 %copy-start.2 = (s32[256]{0:T(256)S(1)}, s32[256]{0:T(256)}, u32[]{:S(2)}) copy-start(s32[256]{0:T(256)} %param.13) | copy-start | bytes 3076
  2.2 13.9 %collective-permute-start.10 = (f32[2,4,32,128]{3,2,1,0:T(8,128)S(1)}, f32[2,4,32,128]{3,2,1,0:T(8,128)S(1)}, u32[]{:S(2)}, u32[]{:S(2)}) collective-permute-start(f32[2,4,32,128]{3,2,1,0:T(8,128)S(1)} %get-tuple-element.44), channel_id=1, source_target_pairs={{0,6},{2,4},{4,2},{6,0},{8,14},{10,12},{12,10},{14,8},{1,7},{3,5},... | collective-permute-start | bytes 393224 | tf_op jit(solution)/shard_map/ppermute | solution.py:531
  6.2 18.2 %collective-permute-start.11 = (f32[2,4,32,128]{3,2,1,0:T(8,128)S(1)}, f32[2,4,32,128]{3,2,1,0:T(8,128)S(1)}, u32[]{:S(2)}, u32[]{:S(2)}) collective-permute-start(f32[2,4,32,128]{3,2,1,0:T(8,128)S(1)} %get-tuple-element.45), channel_id=1, source_target_pairs={{0,8},{2,10},{4,12},{6,14},{8,0},{10,2},{12,4},{14,6},{1,9},{3,11}... | collective-permute-start | bytes 393224 | tf_op jit(solution)/shard_map/ppermute | solution.py:531
  8.8 17.9 %collective-permute-start.12 = (f32[2,4,32,128]{3,2,1,0:T(8,128)S(1)}, f32[2,4,32,128]{3,2,1,0:T(8,128)S(1)}, u32[]{:S(2)}, u32[]{:S(2)}) collective-permute-start(f32[2,4,32,128]{3,2,1,0:T(8,128)S(1)} %get-tuple-element.46), channel_id=1, source_target_pairs={{0,10},{2,8},{4,14},{6,12},{8,2},{10,0},{12,6},{14,4},{1,11},{3,9}... | collective-permute-start | bytes 393224 | tf_op jit(solution)/shard_map/ppermute | solution.py:531
  9.1 17.6 %collective-permute-start.13 = (f32[2,4,32,128]{3,2,1,0:T(8,128)S(1)}, f32[2,4,32,128]{3,2,1,0:T(8,128)S(1)}, u32[]{:S(2)}, u32[]{:S(2)}) collective-permute-start(f32[2,4,32,128]{3,2,1,0:T(8,128)S(1)} %get-tuple-element.47), channel_id=1, source_target_pairs={{0,12},{2,14},{4,8},{6,10},{8,4},{10,6},{12,0},{14,2},{1,13},{3,15... | collective-permute-start | bytes 393224 | tf_op jit(solution)/shard_map/ppermute | solution.py:531
  11.6 15.1 %collective-permute-start.14 = (f32[2,4,32,128]{3,2,1,0:T(8,128)S(1)}, f32[2,4,32,128]{3,2,1,0:T(8,128)S(1)}, u32[]{:S(2)}, u32[]{:S(2)}) collective-permute-start(f32[2,4,32,128]{3,2,1,0:T(8,128)S(1)} %get-tuple-element.48), channel_id=1, source_target_pairs={{0,14},{2,12},{4,10},{6,8},{8,6},{10,4},{12,2},{14,0},{1,15},{3,13... | collective-permute-start | bytes 393224 | tf_op jit(solution)/shard_map/ppermute | solution.py:531
  16.0 10.7 %collective-permute-start.8 = (f32[2,4,32,128]{3,2,1,0:T(8,128)S(1)}, f32[2,4,32,128]{3,2,1,0:T(8,128)S(1)}, u32[]{:S(2)}, u32[]{:S(2)}) collective-permute-start(f32[2,4,32,128]{3,2,1,0:T(8,128)S(1)} %get-tuple-element.42), channel_id=1, source_target_pairs={{0,2},{2,0},{4,6},{6,4},{8,10},{10,8},{12,14},{14,12},{1,3},{3,1},... | collective-permute-start | bytes 393224 | tf_op jit(solution)/shard_map/ppermute | solution.py:531
  24.4 5.0 %collective-permute-start.9 = (f32[2,4,32,128]{3,2,1,0:T(8,128)S(1)}, f32[2,4,32,128]{3,2,1,0:T(8,128)S(1)}, u32[]{:S(2)}, u32[]{:S(2)}) collective-permute-start(f32[2,4,32,128]{3,2,1,0:T(8,128)S(1)} %get-tuple-element.43), channel_id=1, source_target_pairs={{0,4},{2,6},{4,0},{6,2},{8,12},{10,14},{12,8},{14,10},{1,5},{3,7},... | collective-permute-start | bytes 393224 | tf_op jit(solution)/shard_map/ppermute | solution.py:531
  26.7 3.9 %collective-permute-start = (f32[8,2,4,16,128]{4,3,2,1,0:T(8,128)S(1)}, f32[8,2,4,16,128]{4,3,2,1,0:T(8,128)S(1)}, u32[]{:S(2)}, u32[]{:S(2)}) collective-permute-start(f32[8,2,4,16,128]{4,3,2,1,0:T(8,128)S(1)} %get-tuple-element.32), channel_id=1, source_target_pairs={{0,1},{1,0},{2,3},{3,2},{4,5},{5,4},{6,7},{7,6},{8,9},{9,8},{10,11... | collective-permute-start | bytes 1572872 | tf_op jit(solution)/shard_map/ppermute | solution.py:535
  29.5 8.9 %collective-permute-start.15 = (f32[8,2,4,16,128]{4,3,2,1,0:T(8,128)S(1)}, f32[8,2,4,16,128]{4,3,2,1,0:T(8,128)S(1)}, u32[]{:S(2)}, u32[]{:S(2)}) collective-permute-start(f32[8,2,4,16,128]{4,3,2,1,0:T(8,128)S(1)} %get-tuple-element.50), channel_id=1, source_target_pairs={{0,1},{1,0},{2,3},{3,2},{4,5},{5,4},{6,7},{7,6},{8,9},{9,8},{10,11... | collective-permute-start | bytes 1572872 | tf_op jit(solution)/shard_map/ppermute | solution.py:535
  30.7 8.7 %collective-permute-start.3 = (f32[2,2,4,16,128]{4,3,2,1,0:T(8,128)S(1)}, f32[2,2,4,16,128]{4,3,2,1,0:T(8,128)S(1)}, u32[]{:S(2)}, u32[]{:S(2)}) collective-permute-start(f32[2,2,4,16,128]{4,3,2,1,0:T(8,128)S(1)} %get-tuple-element.36), channel_id=1, source_target_pairs={{0,2},{2,0},{4,6},{6,4},{8,10},{10,8},{12,14},{14,12},{1,3},{3,1},... | collective-permute-start | bytes 393224 | tf_op jit(solution)/shard_map/ppermute | solution.py:531
  30.9 12.8 %collective-permute-start.4 = (f32[2,2,4,16,128]{4,3,2,1,0:T(8,128)S(1)}, f32[2,2,4,16,128]{4,3,2,1,0:T(8,128)S(1)}, u32[]{:S(2)}, u32[]{:S(2)}) collective-permute-start(f32[2,2,4,16,128]{4,3,2,1,0:T(8,128)S(1)} %get-tuple-element.37), channel_id=1, source_target_pairs={{0,4},{2,6},{4,0},{6,2},{8,12},{10,14},{12,8},{14,10},{1,5},{3,7},... | collective-permute-start | bytes 393224 | tf_op jit(solution)/shard_map/ppermute | solution.py:531
  35.2 9.2 %copy-start = (f32[2,5]{1,0:T(2,128)S(1)}, f32[2,5]{1,0:T(2,128)}, u32[]{:S(2)}) copy-start(f32[2,5]{1,0:T(2,128)} %refs_8_.1) | copy-start | bytes 124
  35.4 14.3 %collective-permute-start.5 = (f32[2,2,4,16,128]{4,3,2,1,0:T(8,128)S(1)}, f32[2,2,4,16,128]{4,3,2,1,0:T(8,128)S(1)}, u32[]{:S(2)}, u32[]{:S(2)}) collective-permute-start(f32[2,2,4,16,128]{4,3,2,1,0:T(8,128)S(1)} %get-tuple-element.38), channel_id=1, source_target_pairs={{0,6},{2,4},{4,2},{6,0},{8,14},{10,12},{12,10},{14,8},{1,7},{3,5},... | collective-permute-start | bytes 393224 | tf_op jit(solution)/shard_map/ppermute | solution.py:531
  35.5 14.2 %collective-permute-start.6 = (f32[2,2,4,16,128]{4,3,2,1,0:T(8,128)S(1)}, f32[2,2,4,16,128]{4,3,2,1,0:T(8,128)S(1)}, u32[]{:S(2)}, u32[]{:S(2)}) collective-permute-start(f32[2,2,4,16,128]{4,3,2,1,0:T(8,128)S(1)} %get-tuple-element.39), channel_id=1, source_target_pairs={{0,8},{2,10},{4,12},{6,14},{8,0},{10,2},{12,4},{14,6},{1,9},{3,11}... | collective-permute-start | bytes 393224 | tf_op jit(solution)/shard_map/ppermute | solution.py:531
  38.4 19.1 %collective-permute-start.7 = (f32[2,2,4,16,128]{4,3,2,1,0:T(8,128)S(1)}, f32[2,2,4,16,128]{4,3,2,1,0:T(8,128)S(1)}, u32[]{:S(2)}, u32[]{:S(2)}) collective-permute-start(f32[2,2,4,16,128]{4,3,2,1,0:T(8,128)S(1)} %get-tuple-element.40), channel_id=1, source_target_pairs={{0,10},{2,8},{4,14},{6,12},{8,2},{10,0},{12,6},{14,4},{1,11},{3,9}... | collective-permute-start | bytes 393224 | tf_op jit(solution)/shard_map/ppermute | solution.py:531
  39.4 21.2 %collective-permute-start.1 = (f32[2,2,4,16,128]{4,3,2,1,0:T(8,128)S(1)}, f32[2,2,4,16,128]{4,3,2,1,0:T(8,128)S(1)}, u32[]{:S(2)}, u32[]{:S(2)}) collective-permute-start(f32[2,2,4,16,128]{4,3,2,1,0:T(8,128)S(1)} %get-tuple-element.33), channel_id=1, source_target_pairs={{0,12},{2,14},{4,8},{6,10},{8,4},{10,6},{12,0},{14,2},{1,13},{3,15... | collective-permute-start | bytes 393224 | tf_op jit(solution)/shard_map/ppermute | solution.py:531
  43.7 16.9 %collective-permute-start.2 = (f32[2,2,4,16,128]{4,3,2,1,0:T(8,128)S(1)}, f32[2,2,4,16,128]{4,3,2,1,0:T(8,128)S(1)}, u32[]{:S(2)}, u32[]{:S(2)}) collective-permute-start(f32[2,2,4,16,128]{4,3,2,1,0:T(8,128)S(1)} %get-tuple-element.34), channel_id=1, source_target_pairs={{0,14},{2,12},{4,10},{6,8},{8,6},{10,4},{12,2},{14,0},{1,15},{3,13... | collective-permute-start | bytes 393224 | tf_op jit(solution)/shard_map/ppermute | solution.py:531
